TPU v7x, 256 devices: a whole 4x4x8 slice. The times are simulated.
256 devices in a mesh: dp: 4 (over x), seq: 64 (over y, z, core).
Axes of the slice: x: 4, y: 4, z: 8, core: 2. Of those that a mesh axis runs over, the one named last changes fastest.
Arguments:
- tokens: bfloat16 [4, 8192, 2048], P('dp', 'seq'), may hold values from -6 to 6
- values: bfloat16 [4, 8192, 1024], P('dp', 'seq'), may hold values from -6 to 6
- cotangent: bfloat16 [4, 8192, 1024], P('dp', 'seq'), may hold values from -6 to 6
- sel_weight: bfloat16 [2048, 128], P(('dp', 'seq')), may hold values from -0.03125 to 0.03125
- step_weight: bfloat16 [2048, 32], P(('dp', 'seq')), may hold values from -0.125 to 0.125
- sel_dir: bfloat16 [2048, 128], P(('dp', 'seq')), may hold values from -0.03125 to 0.03125
- step_dir: bfloat16 [2048, 32], P(('dp', 'seq')), may hold values from -0.125 to 0.125
- conv_weight: float32 [4, 128], replicated, may hold values from -3 to 3
- step_bias: float32 [32], replicated, may hold values from -1 to 0.5
- decay_rate: float32 [32], replicated, may hold values from 0 to 1
Outputs:
- sel_grad: float32 [2048, 128], P(('dp', 'seq'))
- step_grad: float32 [2048, 32], P(('dp', 'seq'))
- sel_hvp: float32 [2048, 128], P(('dp', 'seq'))
- step_hvp: float32 [2048, 32], P(('dp', 'seq'))
All inputs are finite; a program needn't handle non-finite values.
Results may differ from a plain program's by a relative error of at most 0.0003.
Values may be sent and summed in bfloat16 or wider, within the bound.
A program may use at most 192 MiB of HBM per device.

v0:
```python
import math

import jax
import jax.numpy as jnp
from jax import lax
from jax.sharding import PartitionSpec as P

N = 64
P_SIZE = 32
H = 32
KCONV = 4


HIGHEST = lax.Precision.HIGHEST


def shifted(value, axis, steps):
    count = lax.axis_size(axis)
    initial, last = (max(0, -steps), min(count, count - steps))
    return lax.ppermute(value, axis, [(source, source + steps) for source in range(initial, last)])


def prefix(part, axis, combine, identity, reverse):
    count = lax.axis_size(axis)
    place = lax.axis_index(axis)
    ahead = count - 1 - place if reverse else place
    gathered = jax.tree.map(lambda a: lax.all_gather(a, axis), part)
    state = jax.tree.map(lambda a, e: jnp.zeros_like(a) + jnp.asarray(e, a.dtype), part, identity)

    def one(turn, state):
        source = count - 1 - turn if reverse else turn
        return combine(
            state, jax.tree.map(lambda a: lax.dynamic_index_in_dim(a, source, 0, False), gathered)
        )

    return lax.fori_loop(0, ahead, one, state)


def state_space(in_map, out_map, step_size, head_values, decay_rate, state_in):
    cumulated = jnp.cumsum(-step_size * decay_rate[None, :], axis=0)
    cumulated_heads = cumulated.T
    spans = cumulated_heads[:, :, None] - cumulated_heads[:, None, :]
    length = in_map.shape[0]
    causal = jnp.arange(length)[:, None] >= jnp.arange(length)[None, :]
    decays = jnp.exp(jnp.where(causal[None], spans, -1e30))
    intersection = jnp.dot(out_map, in_map.T, precision=HIGHEST)
    mixing = decays * intersection[None] * step_size.T[:, None, :]
    within = jnp.einsum("hts,shp->thp", mixing, head_values, precision=HIGHEST)
    carried = jnp.exp(cumulated)[:, :, None] * jnp.einsum(
        "tn,hpn->thp", out_map, state_in, precision=HIGHEST
    )
    whole_decay = cumulated[-1]
    tail_weight = jnp.exp(whole_decay[None, :] - cumulated) * step_size
    local_state = jnp.einsum(
        "thp,tn->hpn", head_values * tail_weight[:, :, None], in_map, precision=HIGHEST
    )
    state_out = jnp.exp(whole_decay)[:, None, None] * state_in + local_state
    return (within + carried, state_out)


def features(sel_float, step_float, extended, conv_weight, step_bias, length):
    projected = jnp.dot(extended, sel_float, precision=HIGHEST)
    convolved = conv_weight[0][None, :] * projected[0:length]
    for offset in range(1, KCONV):
        convolved = convolved + conv_weight[offset][None, :] * projected[offset : offset + length]
    activated = jax.nn.silu(convolved)
    step_size = jax.nn.softplus(
        jnp.dot(extended[KCONV - 1 :], step_float, precision=HIGHEST) + step_bias[None, :]
    )
    return (activated[:, :N], activated[:, N:], step_size)


def combine(earlier_segment, later_segment):
    decay_first, state_first, tangent_decay_first, tangent_state_first = earlier_segment
    decay_second, state_second, tangent_decay_second, tangent_state_second = later_segment
    combined_decay = decay_first * decay_second
    combined_state = decay_second[:, None, None] * state_first + state_second
    tangent_decay_combined = tangent_decay_first * decay_second + decay_first * tangent_decay_second
    tangent_state_combined = (
        tangent_decay_second[:, None, None] * state_first
        + decay_second[:, None, None] * tangent_state_first
        + tangent_state_second
    )
    return (combined_decay, combined_state, tangent_decay_combined, tangent_state_combined)


def body(
    tokens,
    values,
    cotangent,
    sel_weight,
    step_weight,
    sel_dir,
    step_dir,
    conv_weight,
    step_bias,
    decay_rate,
):
    own_tokens = tokens[0]
    length = own_tokens.shape[0]
    head_values = values[0].reshape(length, H, P_SIZE).astype(jnp.float32)
    head_cotangent = cotangent[0].reshape(length, H, P_SIZE).astype(jnp.float32)
    gathered = (
        lax.all_gather(sel_weight, ("dp", "seq"), axis=0, tiled=True),
        lax.all_gather(step_weight, ("dp", "seq"), axis=0, tiled=True),
        lax.all_gather(sel_dir, ("dp", "seq"), axis=0, tiled=True),
        lax.all_gather(step_dir, ("dp", "seq"), axis=0, tiled=True),
    )
    parameters = (gathered[0].astype(jnp.float32), gathered[1].astype(jnp.float32))
    directions = (gathered[2].astype(jnp.float32), gathered[3].astype(jnp.float32))
    previous = shifted(own_tokens[length - (KCONV - 1) :], "seq", 1)
    extended = jnp.concatenate([previous, own_tokens], axis=0).astype(jnp.float32)
    token_count = lax.axis_size("dp") * lax.axis_size("seq") * length
    scale_factor = 1.0 / math.sqrt(token_count)

    def summaries(weights):
        in_map, out_map, step_size = features(
            weights[0], weights[1], extended, conv_weight, step_bias, length
        )
        cumulated = jnp.cumsum(-step_size * decay_rate[None, :], axis=0)
        whole_decay = cumulated[-1]
        tail_weight = jnp.exp(whole_decay[None, :] - cumulated) * step_size
        local_state = jnp.einsum(
            "thp,tn->hpn", head_values * tail_weight[:, :, None], in_map, precision=HIGHEST
        )
        local_adjoint = scale_factor * jnp.einsum(
            "thp,tn->hpn",
            head_cotangent * jnp.exp(cumulated)[:, :, None],
            out_map,
            precision=HIGHEST,
        )
        return (jnp.exp(whole_decay), local_state, local_adjoint)

    primal, tangent = jax.jvp(summaries, (parameters,), (directions,))
    identity = (
        jnp.ones((H,), jnp.float32),
        jnp.zeros((H, P_SIZE, N), jnp.float32),
        jnp.zeros((H,), jnp.float32),
        jnp.zeros((H, P_SIZE, N), jnp.float32),
    )
    forward = prefix(
        (primal[0], primal[1], tangent[0], tangent[1]), "seq", combine, identity, False
    )
    backward = prefix(
        (primal[0], primal[2], tangent[0], tangent[2]), "seq", combine, identity, True
    )

    def objective(weights, state_start, end_adjoint):
        in_map, out_map, step_size = features(
            weights[0], weights[1], extended, conv_weight, step_bias, length
        )
        outputs, state_end = state_space(
            in_map, out_map, step_size, head_values, decay_rate, state_start
        )
        return scale_factor * jnp.sum(head_cotangent * outputs) + jnp.sum(end_adjoint * state_end)

    local_gradient = jax.grad(objective)
    gradients, curvature = jax.jvp(
        local_gradient, (parameters, forward[1], backward[1]), (directions, forward[3], backward[3])
    )
    reduced = (
        lax.psum_scatter(gradients[0], ("dp", "seq"), scatter_dimension=0, tiled=True),
        lax.psum_scatter(gradients[1], ("dp", "seq"), scatter_dimension=0, tiled=True),
        lax.psum_scatter(curvature[0], ("dp", "seq"), scatter_dimension=0, tiled=True),
        lax.psum_scatter(curvature[1], ("dp", "seq"), scatter_dimension=0, tiled=True),
    )
    return (reduced[0], reduced[1], reduced[2], reduced[3])


def solution(mesh):
    return jax.shard_map(
        body,
        mesh=mesh,
        in_specs=(
            P("dp", "seq", None),
            P("dp", "seq", None),
            P("dp", "seq", None),
            P(("dp", "seq"), None),
            P(("dp", "seq"), None),
            P(("dp", "seq"), None),
            P(("dp", "seq"), None),
            P(),
            P(),
            P(),
        ),
        out_specs=(
            P(("dp", "seq"), None),
            P(("dp", "seq"), None),
            P(("dp", "seq"), None),
            P(("dp", "seq"), None),
        ),
        check_vma=False,
    )
```

profile of v0, /device:TPU:1, one launch (start us, length us, event | category | flops | bytes accessed | tf_op | source)
XLA Modules:
  0.0 1397.6 jit_solution(11636096432629976415)
XLA Ops:
  8.1 4.9 collective-permute-start
  13.0 70.1 %all_gather.55 = bf16[2048,128]{1,0:T(8,128)(2,1)S(1)} all-gather(bf16[8,128]{1,0:T(8,128)(2,1)} %param.19), channel_id=1, replica_groups=mesh['dp'=4,'seq'=64] {'dp','seq'}, dimensions={0}, use_global_device_ids=true | all-gather | bytes 526336 | tf_op jit(solution)/shard_map/all_gather | solution.py:106
  83.1 65.5 %all_gather.50 = bf16[2048,128]{1,0:T(8,128)(2,1)S(1)} all-gather(bf16[8,128]{1,0:T(8,128)(2,1)} %param.17), channel_id=1, replica_groups=mesh['dp'=4,'seq'=64] {'dp','seq'}, dimensions={0}, use_global_device_ids=true | all-gather | bytes 526336 | tf_op jit(solution)/shard_map/all_gather | solution.py:104
  148.6 65.6 %all_gather.48 = bf16[2048,32]{1,0:T(8,128)(2,1)S(1)} all-gather(bf16[8,32]{1,0:T(8,128)(2,1)} %param.18), channel_id=1, replica_groups=mesh['dp'=4,'seq'=64] {'dp','seq'}, dimensions={0}, use_global_device_ids=true | all-gather | bytes 131584 | tf_op jit(solution)/shard_map/all_gather | solution.py:105
  214.2 65.5 %all_gather.53 = bf16[2048,32]{1,0:T(8,128)(2,1)S(1)} all-gather(bf16[8,32]{1,0:T(8,128)(2,1)} %param.20), channel_id=1, replica_groups=mesh['dp'=4,'seq'=64] {'dp','seq'}, dimensions={0}, use_global_device_ids=true | all-gather | bytes 131584 | tf_op jit(solution)/shard_map/all_gather | solution.py:107
  287.0 37.6 %all-gather.4 = f32[64,1,32]{2,1,0:T(1,128)S(1)} all-gather(f32[1,1,32]{2,1,0:T(1,128)S(1)} %get-tuple-element.315), channel_id=1, replica_groups=mesh['dp'=4,'seq'=64] {'seq'}, dimensions={0}, use_global_device_ids=true | all-gather | bytes 8320 | tf_op jit(solution)/shard_map/all_gather | solution.py:27
  324.7 37.8 %all-gather.5 = f32[64,1,32]{2,1,0:T(1,128)S(1)} all-gather(f32[1,1,32]{2,1,0:T(1,128)S(1)} %get-tuple-element.313), channel_id=1, replica_groups=mesh['dp'=4,'seq'=64] {'seq'}, dimensions={0}, use_global_device_ids=true | all-gather | bytes 8320 | tf_op jit(solution)/shard_map/all_gather | solution.py:27
  362.5 62.2 %all-gather.17.cloned.1.call-done = f32[2048,32,64]{2,1,0:T(8,128)} async-done(((f32[32,32,64]{2,1,0:T(8,128)}), f32[2048,32,64]{2,1,0:T(8,128)}) %all-gather.17.cloned.1.call-update) | async-done | bytes 16777232 | tf_op jit(solution)/shard_map/all_gather | solution.py:27
  424.7 142.3 %all-gather.15.cloned.1.call-done = f32[2048,32,64]{2,1,0:T(8,128)} async-done(((f32[32,32,64]{2,1,0:T(8,128)}), f32[2048,32,64]{2,1,0:T(8,128)}) %all-gather.15.cloned.1.call-update) | async-done | bytes 16777232 | tf_op jit(solution)/shard_map/all_gather | solution.py:27
  567.1 107.2 %while.33 = (s32[]{:T(128)}, f32[32,32,64]{2,1,0:T(8,128)S(1)}, f32[32,32,64]{2,1,0:T(8,128)S(1)}, s32[]{:T(128)}, f32[64,32]{1,0:T(8,128)S(1)}, /*index=5*/f32[...) while((s32[]{:T(128)}, f32[32,32,64]{2,1,0:T(8,128)S(1)}, ...), condition=%wide.region_6.7_spmd, body=%wide.region_5.6_spmd.sunk | while | flops 393222 | bytes 1573803 | solution.py:36
  568.9 1.7 bitcast_add_fusion.13
  577.5 1.7 bitcast_add_fusion.13
  580.9 1.7 bitcast_add_fusion.13
  584.4 1.7 bitcast_add_fusion.13
  587.8 1.7 bitcast_add_fusion.13
  591.3 1.7 bitcast_add_fusion.13
  684.0 5.9 fusion.150
  699.9 118.7 %all-gather.13.cloned.1.call-done = f32[2048,32,64]{2,1,0:T(8,128)} async-done(((f32[32,32,64]{2,1,0:T(8,128)}), f32[2048,32,64]{2,1,0:T(8,128)}) %all-gather.13.cloned.1.call-update) | async-done | bytes 16777232 | tf_op jit(solution)/shard_map/all_gather | solution.py:27
  818.6 142.2 %all-gather.11.cloned.1.call-done = f32[2048,32,64]{2,1,0:T(8,128)} async-done(((f32[32,32,64]{2,1,0:T(8,128)}), f32[2048,32,64]{2,1,0:T(8,128)}) %all-gather.11.cloned.1.call-update) | async-done | bytes 16777232 | tf_op jit(solution)/shard_map/all_gather | solution.py:27
  960.9 2.6 while.32
  967.8 1.8 convolution_bitcast_fusion.5
  977.5 2.3 fusion.42
  979.8 2.3 fusion.50
  982.2 405.5 %all-reduce.21.cloned.1.call-done = (f32[2048,128]{1,0:T(8,128)}, f32[2048,32]{0,1:T(8,128)}, f32[2048,128]{1,0:T(8,128)}, f32[2048,32]{0,1:T(8,128)}) async-done(((f32[2048,128]{1,0:T(8,128)}, f32[2048,32]{0,1:T(8,128)}, f32[2048,128]{1,0:T(8,128)}, f32[2048,32]{0,1:T(8,128)}), (f32[2048,128]{1,0:T(8,128)}, f32[2048,32]{0,1:T(8,128)}, f32[2048,128]{1,0:T(8,128)}, ...) | async-done | bytes 2621456
  (305 shorter events, 140.0 us)
Async XLA Ops:
  7.2 272.5 %copy-start = (bf16[1,128,2048]{2,1,0:T(8,128)(2,1)S(1)}, bf16[1,128,2048]{2,1,0:T(8,128)(2,1)}, u32[]{:S(2)}) copy-start(bf16[1,128,2048]{2,1,0:T(8,128)(2,1)} %param.14) | copy-start | bytes 1572868
  7.2 272.5 %copy-start.46 = (f32[32]{0:T(128)S(1)}, f32[32]{0:T(128)}, u32[]{:S(2)}) copy-start(f32[32]{0:T(128)} %param.22) | copy-start | bytes 388
  7.2 272.8 %copy-start.29 = (f32[32]{0:T(128)S(1)}, f32[32]{0:T(128)}, u32[]{:S(2)}) copy-start(f32[32]{0:T(128)} %param.23) | copy-start | bytes 388
  7.2 417.5 %all-gather.17.cloned.1.call-start = ((), (), s32[]{:S(2)}) async-start(), calls=%async_computation.3 | async-start | bytes 34078720 | tf_op jit(solution)/shard_map/all_gather | solution.py:27
  8.1 273.6 %collective-permute-start = (bf16[3,2048]{1,0:T(4,128)(2,1)S(1)}, bf16[3,2048]{1,0:T(4,128)(2,1)S(1)}, u32[]{:S(2)}, u32[]{:S(2)}) collective-permute-start(bf16[3,2048]{1,0:T(4,128)(2,1)S(1)} %slice_bitcast_fusion), channel_id=1, source_target_pairs={{0,1},{1,2},{2,3},{3,4},{4,5},{5,6},{6,7},{7,8},{8,9},{9,10},{10,1... | collective-permute-start | bytes 36872 | tf_op jit(solution)/shard_map/ppermute | solution.py:20
  148.6 132.7 %copy-start.43 = (f32[4,128]{1,0:T(4,128)S(1)}, f32[4,128]{1,0:T(4,128)}, u32[]{:S(2)}) copy-start(f32[4,128]{1,0:T(4,128)} %param.21) | copy-start | bytes 6148
  148.6 132.8 %copy-start.12 = (bf16[1,128,1024]{2,1,0:T(8,128)(2,1)S(1)}, bf16[1,128,1024]{2,1,0:T(8,128)(2,1)}, u32[]{:S(2)}) copy-start(bf16[1,128,1024]{2,1,0:T(8,128)(2,1)} %param.16) | copy-start | bytes 786436
  280.3 401.7 %copy-start.1 = (f32[128,32]{1,0:T(8,128)}, f32[128,32]{1,0:T(8,128)S(1)}, u32[]{:S(2)}) copy-start(f32[128,32]{1,0:T(8,128)S(1)} %get-tuple-element.326) | copy-start | bytes 49156
  285.3 281.7 %all-gather.15.cloned.1.call-start = ((), (), s32[]{:S(2)}) async-start(), calls=%async_computation.2 | async-start | bytes 34078720 | tf_op jit(solution)/shard_map/all_gather | solution.py:27
  286.7 531.9 %all-gather.13.cloned.1.call-start = ((), (), s32[]{:S(2)}) async-start(), calls=%async_computation.1 | async-start | bytes 34078720 | tf_op jit(solution)/shard_map/all_gather | solution.py:27
  287.0 389.3 %copy-start.27 = (f32[32]{0:T(128)}, f32[32]{0:T(128)S(1)}, u32[]{:S(2)}) copy-start(f32[32]{0:T(128)S(1)} %get-tuple-element.314) | copy-start | bytes 388
  287.0 389.3 %copy-start.31 = (f32[32]{0:T(128)}, f32[32]{0:T(128)S(1)}, u32[]{:S(2)}) copy-start(f32[32]{0:T(128)S(1)} %get-tuple-element.312) | copy-start | bytes 388
  680.6 280.2 %all-gather.11.cloned.1.call-start = ((), (), s32[]{:S(2)}) async-start(), calls=%async_computation | async-start | bytes 34078720 | tf_op jit(solution)/shard_map/all_gather | solution.py:27
  682.0 705.7 %all-reduce.21.cloned.1.call-start = ((), (), s32[]{:S(2)}) async-start(), calls=%async_computation.4 | async-start | bytes 5242880
  689.9 270.9 %copy-start.3 = (f32[128,128]{1,0:T(8,128)}, f32[128,128]{1,0:T(8,128)S(1)}, u32[]{:S(2)}) copy-start(f32[128,128]{1,0:T(8,128)S(1)} %get-tuple-element.236) | copy-start | bytes 196612
  969.8 5.9 copy-start.2
  969.8 5.9 copy-start.6
  969.8 5.9 copy-start.14
  971.0 6.0 copy-start.24
  971.0 6.3 copy-start.11
  971.0 6.3 copy-start.16
  971.0 6.3 copy-start.22
  971.0 6.3 copy-start.23
  971.0 6.3 copy-start.40
  (29 other events, 101.8 us)
Sparse Core Ops, SparseCore 0:
  285.4 139.1 all-gather.16
  427.4 139.4 all-gather.14
  680.7 137.9 all-gather.12
  821.3 139.4 all-gather.10
  982.3 405.3 all-reduce.20
where the time goes:
time: 1400 us
  waiting for transfers between devices  871 us (62%)
  blocking collectives  342 us (24%)
  other arithmetic  112 us (8%)
  matrix products  35.7 us (3%)
  between operations  14.7 us (1%)
    all_gather x4, waiting for transfers between devices, prefix(): gathered = jax.tree.map(lambda a: lax.all_gather(a, axis), part)  465 us
    unnamed x6, waiting for transfers between devices  406 us
    add x63, other arithmetic, combine(): tangent_decay_second[:, None, None] * state_first  106 us
    all_gather x2, blocking collectives, prefix(): gathered = jax.tree.map(lambda a: lax.all_gather(a, axis), part)  75.5 us
    all_gather x1, blocking collectives, body(): lax.all_gather(sel_dir, ('dp', 'seq'), axis=0, tiled=True)  70.1 us
    all_gather x1, blocking collectives, body(): lax.all_gather(step_weight, ('dp', 'seq'), axis=0, tiled=True)  65.6 us
    all_gather x1, blocking collectives, body(): lax.all_gather(step_dir, ('dp', 'seq'), axis=0, tiled=True)  65.5 us
    all_gather x1, blocking collectives, body(): lax.all_gather(sel_weight, ('dp', 'seq'), axis=0, tiled=True)  65.5 us
  transfers between devices with their start and end apart: 6, of which 5 were waited for; matrix products, arithmetic and copies ran while one was open for 2% of the time, Pallas kernels for 0%

commit v1 on v0

v1 whole, which is shorter than its diff:
```python
import functools
import math

import jax
import jax.numpy as jnp
from jax import lax
from jax.experimental import pallas as pl
from jax.experimental.pallas import tpu as pltpu
from jax.sharding import PartitionSpec as P

N = 64
P_SIZE = 32
H = 32
KCONV = 4
L = 128
HALO = 16
HP = H * P_SIZE
HALF = HP // 2
WIDE = 384
NX, NY, NZ = 4, 4, 8
CHIPS = NY * NZ
MESH = pl.DeviceIdType.MESH
F32 = jnp.float32
BF16 = jnp.bfloat16
VMEM_LIMIT = 56 * 1024 * 1024


def roll64(x):
    return pltpu.roll(x, 64, 1)


def split(x):
    high = x.astype(BF16)
    low = (x - high.astype(F32)).astype(BF16)
    return high, low


def split3(x):
    high = x.astype(BF16)
    rest = x - high.astype(F32)
    mid = rest.astype(BF16)
    low = (rest - mid.astype(F32)).astype(BF16)
    return high, mid, low


def dg(a, b, ca, cb):
    return lax.dot_general(a, b, (((ca,), (cb,)), ((), ())), preferred_element_type=F32)


def dot_split(a, b, ca, cb):
    ah, al = split(a)
    bh, bl = split(b)
    return dg(ah, bh, ca, cb) + (dg(ah, bl, ca, cb) + dg(al, bh, ca, cb))


def dot_left(a, b, ca, cb):
    ah, al = split(a)
    return dg(ah, b, ca, cb) + dg(al, b, ca, cb)


def iota(shape, dim):
    return lax.broadcasted_iota(jnp.int32, shape, dim)


def low_lanes():
    return iota((L, 128), 1) < 64


def head_spread():
    return (iota((H, HP), 0) == iota((H, HP), 1) // P_SIZE).astype(F32).astype(BF16)


def triangle(reverse):
    row, column = iota((L, L), 0), iota((L, L), 1)
    keep = (column >= row) if reverse else (row >= column)
    return keep.astype(F32).astype(BF16)


def cumulate(x, reverse):
    tri = triangle(reverse)
    a, b, c = split3(x)
    return dg(tri, a, 1, 0) + (dg(tri, b, 1, 0) + dg(tri, c, 1, 0))


def features(proj, conv2, bias, rate):
    z = jnp.zeros((L, 128), F32)
    zd = jnp.zeros((L, 128), F32)
    for k in range(KCONV):
        rows = HALO - (KCONV - 1) + k
        z = z + conv2[k : k + 1, :128] * proj(rows, 0, 128)
        zd = zd + conv2[k : k + 1, :128] * proj(rows, 128, 128)
    sg = jax.nn.sigmoid(z)
    act = z * sg
    first = sg * (1.0 + z * (1.0 - sg))
    second = sg * (1.0 - sg) * (2.0 + z * (1.0 - 2.0 * sg))
    actd = first * zd
    steps = proj(HALO, 256, 128)
    q = steps[:, :H] + bias
    qd = steps[:, H : 2 * H]
    delta = jnp.maximum(q, 0.0) + jnp.log1p(jnp.exp(-jnp.abs(q)))
    sq = jax.nn.sigmoid(q)
    deltad = sq * qd
    cum = cumulate(-(delta * rate), False)
    cumd = cumulate(-(deltad * rate), False)
    return dict(
        zd=zd, act=act, actd=actd, first=first, second=second,
        qd=qd, sq=sq, delta=delta, deltad=deltad, cum=cum, cumd=cumd,
    )


def weights_of(ft):
    cum, cumd = ft["cum"], ft["cumd"]
    last, lastd = cum[L - 1 :, :], cumd[L - 1 :, :]
    e = jnp.exp(cum)
    ed = e * cumd
    f = jnp.exp(last - cum)
    fd = f * (lastd - cumd)
    w = f * ft["delta"]
    wd = fd * ft["delta"] + f * ft["deltad"]
    return e, ed, f, fd, w, wd


def pair_parts(ft):
    act, actd = ft["act"], ft["actd"]
    actr, actdr = roll64(act), roll64(actd)
    m = low_lanes()
    return dict(
        b_bd=jnp.where(m, act, actdr),
        o_b=jnp.where(m, 0.0, actr),
        c_cd=jnp.where(m, actr, actd),
        o_c=jnp.where(m, 0.0, act),
        b_o=jnp.where(m, act, 0.0),
        bd_b=jnp.where(m, actd, actr),
        c_o=jnp.where(m, actr, 0.0),
        cd_c=jnp.where(m, actdr, act),
        b_c=act,
        c_b=actr,
    )


def spread_rows(rows):
    return dot_left(rows, head_spread(), 1, 0)


def streams(wts, values, cotangent):
    e, ed, _, _, w, wd = wts
    v = values.astype(F32)
    u = cotangent.astype(F32)
    we = spread_rows(w) * v
    wde = spread_rows(wd) * v
    es = spread_rows(e)
    eds = spread_rows(ed)
    return we, wde, es, eds, es * u, eds * u


def local_states(pp, we, wde, eu, edu):
    left = jnp.concatenate([pp["b_bd"], pp["o_b"]], 0)
    right = jnp.concatenate([we, wde], 0)
    forward = dot_split(left, right, 0, 0)
    left = jnp.concatenate([pp["c_cd"], pp["o_c"]], 0)
    right = jnp.concatenate([eu, edu], 0)
    backward = dot_split(left, right, 0, 0)
    return forward, backward


def intra(ft, pp, v_of, u_of, cols_ref, rows_ref, row1_ref, row2_ref, colq_ref, colqd_ref):
    g = dot_split(pp["c_o"], pp["b_c"], 1, 1)
    gd = dot_split(pp["cd_c"], pp["b_bd"], 1, 1)
    eta = ft["deltad"] - ft["delta"] * ft["cumd"]
    rows_ref[0:H, :] = ft["cum"].T
    rows_ref[H : 2 * H, :] = ft["delta"].T
    rows_ref[2 * H : 3 * H, :] = eta.T
    parts = split3(ft["cum"])
    partsd = split(ft["cumd"])
    row, lane = iota((L, L), 0), iota((L, L), 1)
    causal = row >= lane
    row1_ref[...] = jnp.zeros((L, L), F32)
    row2_ref[...] = jnp.zeros((L, L), F32)

    def one(i, carry):
        dgm, dgd = carry
        pick = (iota((H, 512), 0) == (4 * i + iota((H, 512), 1) // 128)).astype(F32).astype(BF16)
        ct4 = dg(parts[0], pick, 1, 0) + (dg(parts[1], pick, 1, 0) + dg(parts[2], pick, 1, 0))
        cd4 = dg(partsd[0], pick, 1, 0) + dg(partsd[1], pick, 1, 0)
        v_tile, u_tile = v_of(i), u_of(i)
        row1, row2 = row1_ref[...], row2_ref[...]
        for j in range(4):
            h = 4 * i + j
            mask = (iota((L, 128), 1) // P_SIZE == j).astype(F32)
            w = dg((u_tile.astype(F32) * mask).astype(BF16), v_tile, 1, 1)
            ct = ct4[:, 128 * j : 128 * j + 128]
            cd = cd4[:, 128 * j : 128 * j + 128]
            cs = rows_ref[pl.ds(h, 1), :]
            ds = rows_ref[pl.ds(H + h, 1), :]
            et = rows_ref[pl.ds(2 * H + h, 1), :]
            x = jnp.exp(jnp.where(causal, ct - cs, -1e30)) * w
            xd = x * ds
            dgm = dgm + xd
            dgd = dgd + (x * et + cd * xd)
            q = x * g
            xgd = x * gd
            colq_ref[pl.ds(h, 1), :] = jnp.sum(q, axis=0, keepdims=True)
            colqd_ref[pl.ds(h, 1), :] = jnp.sum(xgd + q * cd, axis=0, keepdims=True)
            r1 = jnp.sum(q * ds, axis=1, keepdims=True)
            r2 = jnp.sum(xgd * ds + q * et, axis=1, keepdims=True)
            here = lane == h
            row1 = jnp.where(here, r1, row1)
            row2 = jnp.where(here, r2, row2)
        row1_ref[...] = row1
        row2_ref[...] = row2
        return dgm, dgd

    zero = jnp.zeros((L, L), F32)
    return lax.fori_loop(0, H // 4, one, (zero, zero))


def head_sums(x):
    return dot_left(x, head_spread(), 1, 1)


def finish(ft, wts, pp, dgm, dgd, row1, row2, colq, colqd, we, wde, eu, edu, values, cotangent, xf, xb, rate, scale):
    e, ed, f, fd, w, wd = wts
    v = values.astype(F32)
    u = cotangent.astype(F32)
    zz = dot_split(jnp.concatenate([pp["c_o"], pp["cd_c"]], 0), xf, 1, 0)
    yy = dot_split(jnp.concatenate([pp["b_o"], pp["bd_b"]], 0), xb, 1, 0)
    g = head_sums(zz[:L] * u)
    gdot = head_sums(zz[L:] * u)
    kk = head_sums(yy[:L] * v)
    kdot = head_sums(yy[L:] * v)
    kap = jnp.sum(xb[:64] * xf[:64], axis=0, keepdims=True)
    kapd = jnp.sum(xb[64:] * xf[:64] + xb[:64] * xf[64:], axis=0, keepdims=True)
    both = head_sums(jnp.concatenate([jnp.broadcast_to(kap, (8, HP)), jnp.broadcast_to(kapd, (8, HP))], 0))
    kap, kapd = both[0:1], both[8:9]

    pc = dot_split(jnp.concatenate([eu, edu], 0), xf, 1, 1)
    pb = dot_split(jnp.concatenate([we, wde], 0), xb, 1, 1)
    m = low_lanes()
    t1 = dot_split(dgm, pp["b_bd"], 1, 0)
    t2 = dot_split(dgd, pp["b_c"], 1, 0)
    t3 = dot_split(dgm, pp["c_cd"], 0, 0)
    t4 = dot_split(dgd, pp["c_b"], 0, 0)
    pair_c = t1 + pc[:L] + jnp.where(m, 0.0, roll64(t2 + pc[L:]))
    pair_b = t3 + pb[:L] + jnp.where(m, 0.0, roll64(t4 + pb[L:]))
    dact = jnp.where(m, pair_b, roll64(pair_c))
    dactd = jnp.where(m, roll64(pair_b), pair_c)
    dz = scale * (ft["first"] * dact)
    dzd = scale * (ft["second"] * ft["zd"] * dact + ft["first"] * dactd)

    delta, deltad, cum, cumd = ft["delta"], ft["deltad"], ft["cum"], ft["cumd"]
    colq, colqd = colq.T, colqd.T
    colqd = colqd - cumd * colq
    row1, row2 = row1[:, :H], row2[:, :H]
    row2 = row2 + cumd * row1
    wk = w * kk
    wkd = wd * kk + w * kdot
    dc = row1 - delta * colq + e * g - wk
    dcd = row2 - (deltad * colq + delta * colqd) + ed * g + e * gdot - wkd
    el, edl = e[L - 1 :, :], ed[L - 1 :, :]
    extra = el * kap + jnp.sum(wk, axis=0, keepdims=True)
    extrad = edl * kap + el * kapd + jnp.sum(wkd, axis=0, keepdims=True)
    ddelta = colq + f * kk - rate * (cumulate(dc, True) + extra)
    ddeltad = colqd + fd * kk + f * kdot - rate * (cumulate(dcd, True) + extrad)
    sq = ft["sq"]
    dq = scale * (sq * ddelta)
    dqd = scale * (sq * (1.0 - sq) * ft["qd"] * ddelta + sq * ddeltad)
    return dz, dzd, dq, dqd


def place():
    x = lax.axis_index("dp")
    s = lax.axis_index("seq")
    chip = s // 2
    return x, chip // NZ, lax.rem(chip, NZ), lax.rem(s, 2), chip


def device(x, y, z, k):
    return (x, (y * NZ + z) * 2 + k)


def remote(src, dst, send_sem, recv_sem, dev):
    return pltpu.make_async_remote_copy(
        src_ref=src, dst_ref=dst, send_sem=send_sem, recv_sem=recv_sem,
        device_id=dev, device_id_type=MESH,
    )


def hello(partners):
    barrier = pltpu.get_barrier_semaphore()
    for dev in partners:
        pl.semaphore_signal(barrier, inc=1, device_id=dev, device_id_type=MESH)
    pl.semaphore_wait(barrier, len(partners))


def line_partners():
    x, y, z, k, _ = place()
    out = [device(x, y, z, 1 - k)]
    out += [device(lax.rem(x + d, NX), y, z, k) for d in range(1, NX)]
    out += [device(x, lax.rem(y + d, NY), z, k) for d in range(1, NY)]
    out += [device(x, y, lax.rem(z + d, NZ), k) for d in range(1, NZ)]
    return out


def gather_kernel(shard_ref, tok_ref, proj_ref, ext, pair, wbuf, s_send, s_pair, s_halo, s_tok, s_z, s_slab, s_swap):
    x, y, z, k, chip = place()
    s = 2 * chip + k
    seq = CHIPS * 2
    own = pltpu.make_async_copy(tok_ref, ext.at[pl.ds(HALO, L)], s_tok)
    own.start()
    partners = line_partners()
    barrier = pltpu.get_barrier_semaphore()
    for dev in partners + [(x, lax.rem(s + 1, seq)), (x, lax.rem(s + seq - 1, seq))]:
        pl.semaphore_signal(barrier, inc=1, device_id=dev, device_id_type=MESH)
    pl.semaphore_wait(barrier, len(partners) + 2)

    mate = device(x, y, z, 1 - k)
    to_mate = remote(shard_ref, pair, s_send.at[0], s_pair, mate)
    to_mate.start()
    halo = remote(
        tok_ref.at[pl.ds(L - HALO, HALO)], ext.at[pl.ds(0, HALO)], s_send.at[1], s_halo,
        (x, lax.rem(s + 1, seq)),
    )
    halo.start()
    to_mate.wait()
    first = k == 0
    mine, other = shard_ref[...], pair[...]
    block = jnp.concatenate([jnp.where(first, mine, other), jnp.where(first, other, mine)], 0)
    half = z // 2
    source = lax.rem(z, 2) == k

    @pl.when(source)
    def _():
        wbuf[x, y, half, k] = block.astype(BF16)

    def z_copy(d):
        return remote(
            wbuf.at[x, y, half, k], wbuf.at[x, y, half, k], s_send.at[1 + d], s_z.at[half],
            device(x, y, lax.rem(z + d, NZ), k),
        )

    @pl.when(source)
    def _():
        for d in range(1, NZ):
            z_copy(d).start()

    for i in range(NZ // 2):

        @pl.when(2 * i + k != z)
        def _(i=i):
            remote(
                wbuf.at[x, y, i, k], wbuf.at[x, y, i, k], s_send.at[0], s_z.at[i], mate
            ).wait_recv()

    def slab(sx, sy):
        return wbuf.at[sx, sy, :, k]

    def slab_copy(sx, sy, tx, ty, sem):
        return remote(slab(sx, sy), slab(sx, sy), s_send.at[sem], s_slab.at[sx * NY + sy], device(tx, ty, z, k))

    def swap(sx, sy, kk):
        return remote(
            wbuf.at[sx, sy, :, kk], wbuf.at[sx, sy, :, kk], s_send.at[24 + 0], s_swap.at[sx * NY + sy], mate
        )

    def swap_out(sx, sy, n):
        return remote(
            wbuf.at[sx, sy, :, k], wbuf.at[sx, sy, :, k], s_send.at[24 + n], s_swap.at[sx * NY + sy], mate
        )

    sent = []

    def start(copy):
        copy.start()
        sent.append(copy)

    def near(d):
        return lax.rem(x + d * k, NX), lax.rem(y + d * (1 - k), NY)

    def far(d):
        return lax.rem(x + d * (1 - k), NX), lax.rem(y + d * k, NY)

    for d in range(1, 4):
        tx, ty = near(d)
        start(slab_copy(x, y, tx, ty, 8 + d))
    for d in range(1, 4):
        tx, ty = far(d)
        start(slab_copy(x, y, tx, ty, 11 + d))
    start(swap_out(x, y, 0))
    n = 0
    for d in range(1, 4):
        sx, sy = near(4 - d)
        slab_copy(sx, sy, x, y, 0).wait_recv()
        for t in range(1, 4):
            tx = lax.rem(x + t * (1 - k), NX)
            ty = lax.rem(y + t * k, NY)
            start(slab_copy(sx, sy, tx, ty, 15 + n))
            n += 1
        start(swap_out(sx, sy, d))
    n = 4
    for e in range(4):
        for d in range(1, 4):
            dx, dy = far(4 - d)
            sx = lax.rem(dx + e * k, NX)
            sy = lax.rem(dy + e * (1 - k), NY)
            slab_copy(sx, sy, x, y, 0).wait_recv()
            start(swap_out(sx, sy, n))
            n += 1
    halo.wait()
    own.wait()

    @pl.when(s == 0)
    def _():
        ext[0:HALO, :] = jnp.zeros((HALO, ext.shape[1]), BF16)

    for sx in range(NX):
        for sy in range(NY):
            swap(sx, sy, 1 - k).wait_recv()
    depth = ext.shape[1]
    proj_ref[...] = dg(ext[...], wbuf[...].reshape(depth, WIDE), 1, 0)
    for copy in sent:
        copy.wait_send()

    @pl.when(source)
    def _():
        for d in range(1, NZ):
            z_copy(d).wait_send()


def proj_reader(ref):
    def read(row, lane, lanes):
        return ref[row : row + L, lane : lane + lanes]

    return read


def states_kernel(proj_ref, v_ref, u_ref, conv_ref, bias_ref, rate_ref, out_ref):
    ft = features(proj_reader(proj_ref), conv_ref[...], bias_ref[...], rate_ref[...])
    wts = weights_of(ft)
    pp = pair_parts(ft)
    we, wde, es, eds, eu, edu = streams(wts, v_ref[...], u_ref[...])
    forward, backward = local_states(pp, we, wde, eu, edu)
    row = iota((8, HP), 0)
    dec = jnp.where(row == 0, es[L - 1 :, :], jnp.where(row == 1, eds[L - 1 :, :], 0.0))
    for half in range(2):
        lanes = slice(HALF * half, HALF * half + HALF)
        out_ref[half, 0:128, :] = forward[:, lanes]
        out_ref[half, 128:256, :] = backward[:, lanes]
        out_ref[half, 256:264, :] = dec[:, lanes]


def scan_kernel(loc_ref, out_ref, part, snd, rcv, snd2, rcv2, mine_in, other_in, s_send, s_part, s_one, s_two, s_fin):
    x, y, z, k, chip = place()
    mate = device(x, y, z, 1 - k)

    def peer(d):
        c = lax.rem(chip + d, CHIPS)
        return c, (x, 2 * c + k)

    barrier = pltpu.get_barrier_semaphore()
    pl.semaphore_signal(barrier, inc=1, device_id=mate, device_id_type=MESH)

    def greet(d, carry):
        pl.semaphore_signal(barrier, inc=1, device_id=peer(d)[1], device_id_type=MESH)
        return carry

    lax.fori_loop(1, CHIPS, greet, 0)
    pl.semaphore_wait(barrier, CHIPS)

    to_mate = remote(loc_ref.at[1 - k], part, s_send.at[0], s_part, mate)
    to_mate.start()
    to_mate.wait()
    first = k == 0
    own, other = loc_ref[k], part[...]
    one0 = jnp.where(first, own, other)
    one1 = jnp.where(first, other, own)
    a0, ad0 = one0[256:257], one0[257:258]
    a1, ad1 = one1[256:257], one1[257:258]
    fs = a1 * one0[0:64] + one1[0:64]
    ft = a1 * one0[64:128] + ad1 * one0[0:64] + one1[64:128]
    bs = a0 * one1[128:192] + one0[128:192]
    bt = a0 * one1[192:256] + ad0 * one1[128:192] + one0[192:256]
    a, ad = a0 * a1, ad0 * a1 + a0 * ad1
    row = iota((8, HALF), 0)
    dec = jnp.where(row == 0, a, jnp.where(row == 1, ad, 0.0))
    for g in range(8):
        for i in range(4):
            j = 4 * g + i
            lanes = slice(128 * i, 128 * i + 128)
            rows = slice(8 * g, 8 * g + 8)
            snd[j, 0] = fs[rows, lanes]
            snd[j, 1] = ft[rows, lanes]
            snd[j, 2] = bs[rows, lanes]
            snd[j, 3] = bt[rows, lanes]
            snd[j, 4] = dec[:, lanes]

    def first_copy(d):
        c, dev = peer(d)
        return remote(snd.at[c], rcv.at[chip], s_send.at[d], s_one.at[chip], dev)

    def second_copy(d):
        c, dev = peer(d)
        return remote(snd2.at[c], rcv2.at[chip], s_send.at[CHIPS + d], s_two.at[chip], dev)

    def loop(fn):
        def body(d, carry):
            fn(d)
            return carry

        lax.fori_loop(1, CHIPS, body, 0)

    loop(lambda d: first_copy(d).start())
    rcv[chip] = snd[chip]

    def first_arrived(d):
        c, dev = peer(d)
        remote(snd.at[c], rcv.at[c], s_send.at[d], s_one.at[c], dev).wait_recv()

    loop(first_arrived)
    zero = jnp.zeros((8, 128), F32)

    s, t = zero, zero
    for c in range(CHIPS):
        snd2[c, 0] = s
        snd2[c, 1] = t
        ca, cad = rcv[c, 4, 0:1, :], rcv[c, 4, 1:2, :]
        s, t = ca * s + rcv[c, 0], ca * t + (cad * s + rcv[c, 1])
    s, t = zero, zero
    for c in range(CHIPS - 1, -1, -1):
        snd2[c, 2] = s
        snd2[c, 3] = t
        ca, cad = rcv[c, 4, 0:1, :], rcv[c, 4, 1:2, :]
        s, t = ca * s + rcv[c, 2], ca * t + (cad * s + rcv[c, 3])

    loop(lambda d: second_copy(d).start())
    rcv2[chip] = snd2[chip]

    def second_arrived(d):
        c, dev = peer(d)
        remote(snd2.at[c], rcv2.at[c], s_send.at[CHIPS + d], s_two.at[c], dev).wait_recv()

    loop(second_arrived)
    for g in range(8):
        for i in range(4):
            j = 4 * g + i
            lanes = slice(128 * i, 128 * i + 128)
            for part_index in range(4):
                base = 64 * part_index + 8 * g
                mine_in[base : base + 8, lanes] = rcv2[j, part_index]
    fs, ft, bs, bt = (mine_in[64 * i : 64 * i + 64, :] for i in range(4))
    later_s = a0 * fs + one0[0:64]
    later_t = a0 * ft + ad0 * fs + one0[64:128]
    early_s = a1 * bs + one1[128:192]
    early_t = a1 * bt + ad1 * bs + one1[192:256]
    out_ref[k, 0:64, :] = jnp.where(first, fs, later_s)
    out_ref[k, 64:128, :] = jnp.where(first, ft, later_t)
    out_ref[k, 128:192, :] = jnp.where(first, early_s, bs)
    out_ref[k, 192:256, :] = jnp.where(first, early_t, bt)
    other_in[0:64, :] = jnp.where(first, later_s, fs)
    other_in[64:128, :] = jnp.where(first, later_t, ft)
    other_in[128:192, :] = jnp.where(first, bs, early_s)
    other_in[192:256, :] = jnp.where(first, bt, early_t)
    back = remote(other_in, out_ref.at[k], s_send.at[2 * CHIPS], s_fin, mate)
    back.start()
    loop(lambda d: first_copy(d).wait_send())
    loop(lambda d: second_copy(d).wait_send())
    back.wait_send()
    remote(other_in, out_ref.at[1 - k], s_send.at[2 * CHIPS], s_fin, mate).wait_recv()


def grads_kernel(scale, proj_ref, v_ref, u_ref, st_ref, conv_ref, bias_ref, rate_ref, dp_ref,
                 rows_ref, row1_ref, row2_ref, colq_ref, colqd_ref, zp_ref):
    rate = rate_ref[...]
    ft = features(proj_reader(proj_ref), conv_ref[...], bias_ref[...], rate)
    wts = weights_of(ft)
    pp = pair_parts(ft)

    def tile(ref):
        return lambda i: ref[:, pl.ds(pl.multiple_of(i * 128, 128), 128)]

    dgm, dgd = intra(ft, pp, tile(v_ref), tile(u_ref), None, rows_ref, row1_ref, row2_ref, colq_ref, colqd_ref)
    we, wde, es, eds, eu, edu = streams(wts, v_ref[...], u_ref[...])
    xf = jnp.concatenate([st_ref[0, 0:128, :], st_ref[1, 0:128, :]], 1)
    xb = jnp.concatenate([st_ref[0, 128:256, :], st_ref[1, 128:256, :]], 1)
    dz, dzd, dq, dqd = finish(
        ft, wts, pp, dgm, dgd, row1_ref[...], row2_ref[...], colq_ref[...], colqd_ref[...],
        we, wde, eu, edu, v_ref[...], u_ref[...], xf, xb, rate, scale,
    )
    zp_ref[...] = jnp.zeros(zp_ref.shape, F32)
    zp_ref[HALO : HALO + L, 0:128] = dz
    zp_ref[HALO : HALO + L, 128:256] = dzd
    conv = conv_ref[...]
    for half in range(2):
        lanes = slice(128 * half, 128 * half + 128)
        total = conv[0:1, :128] * zp_ref[3 : 3 + HALO + L, lanes]
        for k in range(1, KCONV):
            total = total + conv[k : k + 1, :128] * zp_ref[3 - k : 3 - k + HALO + L, lanes]
        dp_ref[:, lanes] = total
    dp_ref[:, 256:384] = jnp.zeros((HALO + L, 128), F32)
    dp_ref[HALO:, 256 : 256 + H] = dq
    dp_ref[HALO:, 256 + H : 256 + 2 * H] = dqd


def reduce_kernel(ext_ref, dp_ref, out_ref, full, mate_in, a0, a1, a2, r0, r1, r2, b0, b1, b2,
                  q0, q1, q2, c0, c1, c2, p0, p1, p2, s_send, s_mate, s_a, s_b, s_c):
    x, y, z, k, chip = place()
    mate = device(x, y, z, 1 - k)
    hello(line_partners())

    def x_to(d):
        return device(lax.rem(x + d, NX), y, z, k)

    def y_to(d):
        return device(x, lax.rem(y + d, NY), z, k)

    def z_to(d):
        return device(x, y, lax.rem(z + d, NZ), k)

    high, low = split(dp_ref[...])
    ext = ext_ref[...]
    rows = NX * NY * NZ
    for tile in range(3):
        lanes = slice(128 * tile, 128 * tile + 128)
        part = dg(ext, high[:, lanes], 0, 0) + dg(ext, low[:, lanes], 0, 0)
        full[tile] = part.reshape(NX, NY, NZ, 2, 8, 128)
    to_mate = remote(full.at[:, :, :, :, 1 - k], mate_in, s_send.at[0], s_mate, mate)
    to_mate.start()
    to_mate.wait()
    for tile, acc in enumerate((a0, a1, a2)):
        acc[...] = full[tile, :, :, :, k] + mate_in[tile]

    first = []
    for d in range(1, NX):
        first.append(remote(a0.at[lax.rem(x + d, NX)], r0.at[d - 1], s_send.at[d], s_a.at[d], x_to(d)))
    for d in range(1, NY):
        first.append(remote(a1.at[:, lax.rem(y + d, NY)], r1.at[d - 1], s_send.at[3 + d], s_a.at[3 + d], y_to(d)))
    for d in range(1, NZ):
        first.append(remote(a2.at[:, :, lax.rem(z + d, NZ)], r2.at[d - 1], s_send.at[6 + d], s_a.at[6 + d], z_to(d)))
    for copy in first:
        copy.start()

    second = []
    for copy in first[0:3]:
        copy.wait_recv()
    b0[...] = (a0[x] + r0[0]) + (r0[1] + r0[2])
    for d in range(1, NY):
        second.append(remote(b0.at[lax.rem(y + d, NY)], q0.at[d - 1], s_send.at[13 + d], s_b.at[d], y_to(d)))
        second[-1].start()
    for copy in first[3:6]:
        copy.wait_recv()
    b1[...] = (a1[:, y] + r1[0]) + (r1[1] + r1[2])
    for d in range(1, NZ):
        second.append(remote(b1.at[:, lax.rem(z + d, NZ)], q1.at[d - 1], s_send.at[16 + d], s_b.at[3 + d], z_to(d)))
        second[-1].start()
    for copy in first[6:13]:
        copy.wait_recv()
    b2[...] = a2[:, :, z] + ((r2[0] + r2[1]) + (r2[2] + r2[3])) + ((r2[4] + r2[5]) + r2[6])
    for d in range(1, NX):
        second.append(remote(b2.at[lax.rem(x + d, NX)], q2.at[d - 1], s_send.at[23 + d], s_b.at[10 + d], x_to(d)))
        second[-1].start()

    third = []
    for copy in second[0:3]:
        copy.wait_recv()
    c0[...] = (b0[y] + q0[0]) + (q0[1] + q0[2])
    for d in range(1, NZ):
        third.append(remote(c0.at[lax.rem(z + d, NZ)], p0.at[d - 1], s_send.at[26 + d], s_c.at[d], z_to(d)))
        third[-1].start()
    for copy in second[3:10]:
        copy.wait_recv()
    c1[...] = b1[:, z] + ((q1[0] + q1[1]) + (q1[2] + q1[3])) + ((q1[4] + q1[5]) + q1[6])
    for d in range(1, NX):
        third.append(remote(c1.at[lax.rem(x + d, NX)], p1.at[d - 1], s_send.at[33 + d], s_c.at[7 + d], x_to(d)))
        third[-1].start()
    for copy in second[10:13]:
        copy.wait_recv()
    c2[...] = (b2[x] + q2[0]) + (q2[1] + q2[2])
    for d in range(1, NY):
        third.append(remote(c2.at[lax.rem(y + d, NY)], p2.at[d - 1], s_send.at[36 + d], s_c.at[10 + d], y_to(d)))
        third[-1].start()
    for copy in third[0:7]:
        copy.wait_recv()
    out_ref[:, 0:128] = c0[z] + ((p0[0] + p0[1]) + (p0[2] + p0[3])) + ((p0[4] + p0[5]) + p0[6])
    for copy in third[7:10]:
        copy.wait_recv()
    out_ref[:, 128:256] = (c1[x] + p1[0]) + (p1[1] + p1[2])
    for copy in third[10:13]:
        copy.wait_recv()
    out_ref[:, 256:384] = (c2[y] + p2[0]) + (p2[1] + p2[2])
    for copy in first + second + third:
        copy.wait_send()


def vmem(shape, dtype=F32):
    return pltpu.VMEM(shape, dtype)


def dma(*shape):
    return pltpu.SemaphoreType.DMA(shape)


def call(kernel, out_shape, in_specs, scratch, out_specs=None, cid=None):
    spec = pl.BlockSpec(memory_space=pltpu.VMEM)
    n_out = len(out_shape) if isinstance(out_shape, (list, tuple)) else 1
    if out_specs is None:
        out_specs = [spec] * n_out if isinstance(out_shape, (list, tuple)) else spec
    params = dict(vmem_limit_bytes=VMEM_LIMIT)
    if cid is not None:
        params.update(collective_id=cid, has_side_effects=True)
    return pl.pallas_call(
        kernel, out_shape=out_shape, in_specs=in_specs, out_specs=out_specs,
        scratch_shapes=scratch, compiler_params=pltpu.CompilerParams(**params),
    )


def body(tokens, values, cotangent, sel_weight, step_weight, sel_dir, step_dir, conv_weight, step_bias, decay_rate):
    own_tokens, v, u = tokens[0], values[0], cotangent[0]
    depth = own_tokens.shape[1]
    scale = 1.0 / math.sqrt(NX * CHIPS * 2 * L)
    spec = pl.BlockSpec(memory_space=pltpu.VMEM)
    hbm = pl.BlockSpec(memory_space=pl.ANY)
    shard = jnp.concatenate(
        [sel_weight, sel_dir, step_weight, step_dir, jnp.zeros((sel_weight.shape[0], 64), BF16)], 1
    ).astype(F32)
    bias, rate = step_bias[None, :], decay_rate[None, :]
    rows = shard.shape[0]
    ext_shape = (HALO + L, depth)
    proj, ext = call(
        lambda sh, tok, pr, ex, *rest: gather_kernel(sh, tok, pr, ex, *rest),
        [jax.ShapeDtypeStruct((HALO + L, WIDE), F32), jax.ShapeDtypeStruct(ext_shape, BF16)],
        [spec, hbm],
        [vmem((rows, WIDE)), vmem((NX, NY, NZ // 2, 2, 2 * rows, WIDE), BF16),
         dma(40), dma(), dma(), dma(), dma(NZ // 2), dma(NX * NY), dma(NX * NY)],
        cid=0,
    )(shard, own_tokens)
    loc = call(
        states_kernel, jax.ShapeDtypeStruct((2, 264, HALF), F32), [spec] * 6, [],
    )(proj, v, u, conv_weight, bias, rate)
    st = call(
        scan_kernel, jax.ShapeDtypeStruct((2, 256, HALF), F32), [spec],
        [vmem((264, HALF)), vmem((CHIPS, 5, 8, 128)), vmem((CHIPS, 5, 8, 128)),
         vmem((CHIPS, 4, 8, 128)), vmem((CHIPS, 4, 8, 128)), vmem((256, HALF)), vmem((256, HALF)),
         dma(2 * CHIPS + 1), dma(), dma(CHIPS), dma(CHIPS), dma()],
        cid=1,
    )(loc)
    dp = call(
        functools.partial(grads_kernel, scale), jax.ShapeDtypeStruct((HALO + L, WIDE), F32), [spec] * 7,
        [vmem((3 * H, L)), vmem((L, L)), vmem((L, L)), vmem((H, L)), vmem((H, L)), vmem((HALO + L + 8, 256))],
    )(proj, v, u, st, conv_weight, bias, rate)
    out = call(
        reduce_kernel, jax.ShapeDtypeStruct((rows, WIDE), F32), [spec] * 2,
        [vmem((3, NX, NY, NZ, 2, 8, 128)), vmem((3, NX, NY, NZ, 8, 128))]
        + [vmem((NX, NY, NZ, 8, 128))] * 3
        + [vmem((3, NY, NZ, 8, 128)), vmem((3, NX, NZ, 8, 128)), vmem((7, NX, NY, 8, 128))]
        + [vmem((NY, NZ, 8, 128)), vmem((NX, NZ, 8, 128)), vmem((NX, NY, 8, 128))]
        + [vmem((3, NZ, 8, 128)), vmem((7, NX, 8, 128)), vmem((3, NY, 8, 128))]
        + [vmem((NZ, 8, 128)), vmem((NX, 8, 128)), vmem((NY, 8, 128))]
        + [vmem((7, 8, 128)), vmem((3, 8, 128)), vmem((3, 8, 128))]
        + [dma(40), dma(), dma(14), dma(14), dma(14)],
        cid=2,
    )(ext, dp)
    return (
        out[:, 0:128],
        out[:, 256 : 256 + H],
        out[:, 128:256],
        out[:, 256 + H : 256 + 2 * H],
    )


def solution(mesh):
    shards = P(("dp", "seq"), None)
    stream = P("dp", "seq", None)
    return jax.shard_map(
        body,
        mesh=mesh,
        in_specs=(stream, stream, stream, shards, shards, shards, shards, P(), P(), P()),
        out_specs=(shards, shards, shards, shards),
        check_vma=False,
    )
```

time: 1400 us -> 127 us (0.09)
  waiting for transfers between devices: 871 us -> 0 us
  blocking collectives: 342 us -> 0 us
  Pallas kernels: 0 us -> 121 us
  other arithmetic: 112 us -> 0.6 us
  matrix products: 35.7 us -> 0 us
  between operations: 14.7 us -> 0.66 us
    all_gather x4 -> x0, waiting for transfers between devices: 465 us -> none  [prefix(): gathered = jax.tree.map(lambda a: lax.all_gather(a, axis), part)]
    unnamed x6 -> x0, waiting for transfers between devices: 406 us -> none
    all_gather x6 -> x0, blocking collectives: 342 us -> none  [the longest x2 75.5 us: prefix(): gathered = jax.tree.map(lambda a: lax.all_gather(a, axis), part)]
    pallas_call x0 -> x5, Pallas kernels: none -> 121 us  [the longest x1 43.6 us: body(): call(scan_kernel, jax.ShapeDtypeStruct((2, 256, HALF), F32), [spec], [vme...]
    add x64 -> x0, other arithmetic: 106 us -> none  [the longest x63 106 us: combine(): tangent_decay_second[:, None, None] * state_first]
    dot_general x36 -> x0, matrix products: 35.7 us -> none  [the longest x6 6.15 us: state_space(): jnp.einsum('tn,hpn->thp', out_map, state_in, precision=HIGHEST)]
  transfers between devices with their start and end apart: 6 -> 0, of which waited for: 5 -> 0; matrix products, arithmetic and copies ran while one was open for 2% -> 0% of each run, Pallas kernels for 0% -> 0%
where the time goes in v1:
time: 127 us; the launch traced here: 125 us
  Pallas kernels  121 us (95%)
  local copies, waits for them, and re-layouts  3.52 us (3%)
    pallas_call x1, Pallas kernels, body(): call(scan_kernel, jax.ShapeDtypeStruct((2, 256, HALF), F32), [spec], [vme...  43.6 us
    pallas_call x1, Pallas kernels, body(): call(reduce_kernel, jax.ShapeDtypeStruct((rows, WIDE), F32), [spec] * 2,...  31.7 us
    pallas_call x1, Pallas kernels, body(): call(lambda sh, tok, pr, ex, *rest: gather_kernel(sh, tok, pr, ex, *rest)...  31.3 us
    pallas_call x1, Pallas kernels, body(): call(functools.partial(grads_kernel, scale), jax.ShapeDtypeStruct((HALO +...  10.6 us
    pallas_call x1, Pallas kernels, body(): call(states_kernel, jax.ShapeDtypeStruct((2, 264, HALF), F32), [spec] * 6...  3.53 us

profile of v1, /device:TPU:1, one launch (start us, length us, event | category | flops | bytes accessed | tf_op | source)
XLA Modules:
  0.0 125.5 jit_solution(3720824996336210798)
XLA Ops:
  0.6 0.8 concatenate.3
  1.5 0.6 convert_element_type.3.sh
  2.1 31.3 %shard_map.129 = (f32[144,384]{1,0:T(8,128)}, bf16[144,2048]{1,0:T(8,128)(2,1)}) custom-call(f32[8,384]{1,0:T(8,128)} %convert_element_type.3.sh, bf16[128,2048]{1,0:T(8,128)(2,1)} %bitcast.9), custom_call_target="tpu_custom_call" | custom-call | tf_op jit(solution)/shard_map/pallas_call | solution.py:727
  33.4 3.5 %shard_map.130.loc_ref = f32[2,264,512]{2,1,0:T(8,128)} custom-call(f32[144,384]{1,0:T(8,128)} %get-tuple-element.7.proj_ref, bf16[128,1024]{1,0:T(8,128)(2,1)} %bitcast.5, bf16[128,1024]{1,0:T(8,128)(2,1)} %bitcast.7, f32[4,128]{1,0:T(4,128)} %conv_ref.3, f32[1,32]{1,0:T(1,128)} %bitcast.10, f32[1,32]{1,0:T(1,128)} %bitcast.12), custom_call_target="tpu_custom_call" | custom-call | tf_op jit(solution)/shard_map/pallas_call | solution.py:735
  36.9 43.6 %shard_map.131.st_ref = f32[2,256,512]{2,1,0:T(8,128)} custom-call(f32[2,264,512]{2,1,0:T(8,128)} %shard_map.130.loc_ref), custom_call_target="tpu_custom_call" | custom-call | tf_op jit(solution)/shard_map/pallas_call | solution.py:738
  80.4 10.6 %shard_map.132.dp_ref = f32[144,384]{1,0:T(8,128)} custom-call(f32[144,384]{1,0:T(8,128)} %get-tuple-element.7.proj_ref, bf16[128,1024]{1,0:T(8,128)(2,1)} %bitcast.6, bf16[128,1024]{1,0:T(8,128)(2,1)} %bitcast.8, f32[2,256,512]{2,1,0:T(8,128)} %shard_map.131.st_ref, f32[4,128]{1,0:T(4,128)} %conv_ref.3, f32[1,32]{1,0:T(1,128)} %bitcast.11, f32[1,32]{1,0:T(1,128)} %bitcast.13), custom_call_target="tpu_custom_call" | custom-call | tf_op jit(solution)/shard_map/pallas_call | solution.py:745
  91.0 31.7 %shard_map.133 = f32[8,384]{1,0:T(8,128)} custom-call(bf16[144,2048]{1,0:T(8,128)(2,1)} %get-tuple-element.6.ext_ref, f32[144,384]{1,0:T(8,128)} %shard_map.132.dp_ref), custom_call_target="tpu_custom_call" | custom-call | tf_op jit(solution)/shard_map/pallas_call | solution.py:749
  122.8 1.4 %fusion = (f32[8,32]{1,0:T(8,128)}, f32[8,32]{1,0:T(8,128)}) fusion(f32[8,384]{1,0:T(8,128)} %shard_map.133), kind=kLoop, calls=%fused_computation | loop fusion | bytes 4096 | tf_op jit(solution)/shard_map/slice | solution.py:765
  124.2 1.3 %fusion.1 = (f32[8,128]{1,0:T(8,128)}, f32[8,128]{1,0:T(8,128)}) fusion(f32[8,384]{1,0:T(8,128)} %shard_map.133), kind=kLoop, calls=%fused_computation.1 | loop fusion | bytes 16384 | tf_op jit(solution)/shard_map/slice | solution.py:764
  (1 shorter events, 0.0 us)

commit v2 on v1

v2 whole, which is shorter than its diff:
```python
import functools
import math

import jax
import jax.numpy as jnp
from jax import lax
from jax.experimental import pallas as pl
from jax.experimental.pallas import tpu as pltpu
from jax.sharding import PartitionSpec as P

N = 64
P_SIZE = 32
H = 32
KCONV = 4
L = 128
HALO = 16
HP = H * P_SIZE
HALF = HP // 2
WIDE = 384
NX, NY, NZ = 4, 4, 8
CHIPS = NY * NZ
MESH = pl.DeviceIdType.MESH
F32 = jnp.float32
BF16 = jnp.bfloat16
VMEM_LIMIT = 56 * 1024 * 1024


def roll64(x):
    return pltpu.roll(x, 64, 1)


def split(x):
    high = x.astype(BF16)
    low = (x - high.astype(F32)).astype(BF16)
    return high, low


def split3(x):
    high = x.astype(BF16)
    rest = x - high.astype(F32)
    mid = rest.astype(BF16)
    low = (rest - mid.astype(F32)).astype(BF16)
    return high, mid, low


def dg(a, b, ca, cb):
    return lax.dot_general(a, b, (((ca,), (cb,)), ((), ())), preferred_element_type=F32)


def dot_split(a, b, ca, cb):
    ah, al = split(a)
    bh, bl = split(b)
    return dg(ah, bh, ca, cb) + (dg(ah, bl, ca, cb) + dg(al, bh, ca, cb))


def dot_left(a, b, ca, cb):
    ah, al = split(a)
    return dg(ah, b, ca, cb) + dg(al, b, ca, cb)


def iota(shape, dim):
    return lax.broadcasted_iota(jnp.int32, shape, dim)


def low_lanes():
    return iota((L, 128), 1) < 64


def head_spread():
    return (iota((H, HP), 0) == iota((H, HP), 1) // P_SIZE).astype(F32).astype(BF16)


def triangle(reverse):
    row, column = iota((L, L), 0), iota((L, L), 1)
    keep = (column >= row) if reverse else (row >= column)
    return keep.astype(F32).astype(BF16)


def cumulate(x, reverse):
    tri = triangle(reverse)
    a, b, c = split3(x)
    return dg(tri, a, 1, 0) + (dg(tri, b, 1, 0) + dg(tri, c, 1, 0))


def features(proj, conv2, bias, rate):
    z = jnp.zeros((L, 128), F32)
    zd = jnp.zeros((L, 128), F32)
    for k in range(KCONV):
        rows = HALO - (KCONV - 1) + k
        z = z + conv2[k : k + 1, :128] * proj(rows, 0, 128)
        zd = zd + conv2[k : k + 1, :128] * proj(rows, 128, 128)
    sg = jax.nn.sigmoid(z)
    act = z * sg
    first = sg * (1.0 + z * (1.0 - sg))
    second = sg * (1.0 - sg) * (2.0 + z * (1.0 - 2.0 * sg))
    actd = first * zd
    steps = proj(HALO, 256, 128)
    q = steps[:, :H] + bias
    qd = steps[:, H : 2 * H]
    delta = jnp.maximum(q, 0.0) + jnp.log1p(jnp.exp(-jnp.abs(q)))
    sq = jax.nn.sigmoid(q)
    deltad = sq * qd
    cum = cumulate(-(delta * rate), False)
    cumd = cumulate(-(deltad * rate), False)
    return dict(
        zd=zd, act=act, actd=actd, first=first, second=second,
        qd=qd, sq=sq, delta=delta, deltad=deltad, cum=cum, cumd=cumd,
    )


def weights_of(ft):
    cum, cumd = ft["cum"], ft["cumd"]
    last, lastd = cum[L - 1 :, :], cumd[L - 1 :, :]
    e = jnp.exp(cum)
    ed = e * cumd
    f = jnp.exp(last - cum)
    fd = f * (lastd - cumd)
    w = f * ft["delta"]
    wd = fd * ft["delta"] + f * ft["deltad"]
    return e, ed, f, fd, w, wd


def pair_parts(ft):
    act, actd = ft["act"], ft["actd"]
    actr, actdr = roll64(act), roll64(actd)
    m = low_lanes()
    return dict(
        b_bd=jnp.where(m, act, actdr),
        o_b=jnp.where(m, 0.0, actr),
        c_cd=jnp.where(m, actr, actd),
        o_c=jnp.where(m, 0.0, act),
        b_o=jnp.where(m, act, 0.0),
        bd_b=jnp.where(m, actd, actr),
        c_o=jnp.where(m, actr, 0.0),
        cd_c=jnp.where(m, actdr, act),
        b_c=act,
        c_b=actr,
    )


def spread_rows(rows):
    return dot_left(rows, head_spread(), 1, 0)


def streams(wts, values, cotangent):
    e, ed, _, _, w, wd = wts
    v = values.astype(F32)
    u = cotangent.astype(F32)
    we = spread_rows(w) * v
    wde = spread_rows(wd) * v
    es = spread_rows(e)
    eds = spread_rows(ed)
    return we, wde, es, eds, es * u, eds * u


def local_states(pp, we, wde, eu, edu):
    left = jnp.concatenate([pp["b_bd"], pp["o_b"]], 0)
    right = jnp.concatenate([we, wde], 0)
    forward = dot_split(left, right, 0, 0)
    left = jnp.concatenate([pp["c_cd"], pp["o_c"]], 0)
    right = jnp.concatenate([eu, edu], 0)
    backward = dot_split(left, right, 0, 0)
    return forward, backward


def intra_setup(ft, pp, rows_ref, row1_ref, row2_ref):
    g = dot_split(pp["c_o"], pp["b_c"], 1, 1)
    gd = dot_split(pp["cd_c"], pp["b_bd"], 1, 1)
    eta = ft["deltad"] - ft["delta"] * ft["cumd"]
    rows_ref[0:H, :] = ft["cum"].T
    rows_ref[H : 2 * H, :] = ft["delta"].T
    rows_ref[2 * H : 3 * H, :] = eta.T
    row1_ref[...] = jnp.zeros((L, L), F32)
    row2_ref[...] = jnp.zeros((L, L), F32)
    return g, gd


def intra(ft, g, gd, v_of, u_of, rows_ref, row1_ref, row2_ref, colq_ref, colqd_ref):
    parts = split3(ft["cum"])
    partsd = split(ft["cumd"])
    row, lane = iota((L, L), 0), iota((L, L), 1)
    causal = row >= lane

    def one(i, carry):
        dgm, dgd = carry
        pick = (iota((H, 512), 0) == (4 * i + iota((H, 512), 1) // 128)).astype(F32).astype(BF16)
        ct4 = dg(parts[0], pick, 1, 0) + (dg(parts[1], pick, 1, 0) + dg(parts[2], pick, 1, 0))
        cd4 = dg(partsd[0], pick, 1, 0) + dg(partsd[1], pick, 1, 0)
        v_tile, u_tile = v_of(i), u_of(i)
        row1, row2 = row1_ref[...], row2_ref[...]
        for j in range(4):
            h = 4 * i + j
            mask = (iota((L, 128), 1) // P_SIZE == j).astype(F32)
            w = dg((u_tile.astype(F32) * mask).astype(BF16), v_tile, 1, 1)
            ct = ct4[:, 128 * j : 128 * j + 128]
            cd = cd4[:, 128 * j : 128 * j + 128]
            cs = rows_ref[pl.ds(h, 1), :]
            ds = rows_ref[pl.ds(H + h, 1), :]
            et = rows_ref[pl.ds(2 * H + h, 1), :]
            x = jnp.exp(jnp.where(causal, ct - cs, -1e30)) * w
            xd = x * ds
            dgm = dgm + xd
            dgd = dgd + (x * et + cd * xd)
            q = x * g
            xgd = x * gd
            colq_ref[pl.ds(h, 1), :] = jnp.sum(q, axis=0, keepdims=True)
            colqd_ref[pl.ds(h, 1), :] = jnp.sum(xgd + q * cd, axis=0, keepdims=True)
            r1 = jnp.sum(q * ds, axis=1, keepdims=True)
            r2 = jnp.sum(xgd * ds + q * et, axis=1, keepdims=True)
            here = lane == h
            row1 = jnp.where(here, r1, row1)
            row2 = jnp.where(here, r2, row2)
        row1_ref[...] = row1
        row2_ref[...] = row2
        return dgm, dgd

    zero = jnp.zeros((L, L), F32)
    return lax.fori_loop(0, H // 4, one, (zero, zero))


def intra_pairs(pp, dgm, dgd):
    return (
        dot_split(dgm, pp["b_bd"], 1, 0),
        dot_split(dgd, pp["b_c"], 1, 0),
        dot_split(dgm, pp["c_cd"], 0, 0),
        dot_split(dgd, pp["c_b"], 0, 0),
    )


def head_sums(x):
    return dot_left(x, head_spread(), 1, 1)


def finish(ft, wts, pp, pairs, row1, row2, colq, colqd, we, wde, eu, edu, values, cotangent, xf, xb, rate, scale):
    e, ed, f, fd, w, wd = wts
    v = values.astype(F32)
    u = cotangent.astype(F32)
    zz = dot_split(jnp.concatenate([pp["c_o"], pp["cd_c"]], 0), xf, 1, 0)
    yy = dot_split(jnp.concatenate([pp["b_o"], pp["bd_b"]], 0), xb, 1, 0)
    g = head_sums(zz[:L] * u)
    gdot = head_sums(zz[L:] * u)
    kk = head_sums(yy[:L] * v)
    kdot = head_sums(yy[L:] * v)
    kap = jnp.sum(xb[:64] * xf[:64], axis=0, keepdims=True)
    kapd = jnp.sum(xb[64:] * xf[:64] + xb[:64] * xf[64:], axis=0, keepdims=True)
    both = head_sums(jnp.concatenate([jnp.broadcast_to(kap, (8, HP)), jnp.broadcast_to(kapd, (8, HP))], 0))
    kap, kapd = both[0:1], both[8:9]

    pc = dot_split(jnp.concatenate([eu, edu], 0), xf, 1, 1)
    pb = dot_split(jnp.concatenate([we, wde], 0), xb, 1, 1)
    m = low_lanes()
    t1, t2, t3, t4 = pairs
    pair_c = t1 + pc[:L] + jnp.where(m, 0.0, roll64(t2 + pc[L:]))
    pair_b = t3 + pb[:L] + jnp.where(m, 0.0, roll64(t4 + pb[L:]))
    dact = jnp.where(m, pair_b, roll64(pair_c))
    dactd = jnp.where(m, roll64(pair_b), pair_c)
    dz = scale * (ft["first"] * dact)
    dzd = scale * (ft["second"] * ft["zd"] * dact + ft["first"] * dactd)

    delta, deltad, cum, cumd = ft["delta"], ft["deltad"], ft["cum"], ft["cumd"]
    colq, colqd = colq.T, colqd.T
    colqd = colqd - cumd * colq
    row1, row2 = row1[:, :H], row2[:, :H]
    row2 = row2 + cumd * row1
    wk = w * kk
    wkd = wd * kk + w * kdot
    dc = row1 - delta * colq + e * g - wk
    dcd = row2 - (deltad * colq + delta * colqd) + ed * g + e * gdot - wkd
    el, edl = e[L - 1 :, :], ed[L - 1 :, :]
    extra = el * kap + jnp.sum(wk, axis=0, keepdims=True)
    extrad = edl * kap + el * kapd + jnp.sum(wkd, axis=0, keepdims=True)
    ddelta = colq + f * kk - rate * (cumulate(dc, True) + extra)
    ddeltad = colqd + fd * kk + f * kdot - rate * (cumulate(dcd, True) + extrad)
    sq = ft["sq"]
    dq = scale * (sq * ddelta)
    dqd = scale * (sq * (1.0 - sq) * ft["qd"] * ddelta + sq * ddeltad)
    return dz, dzd, dq, dqd


def place():
    x = lax.axis_index("dp")
    s = lax.axis_index("seq")
    chip = s // 2
    return x, chip // NZ, lax.rem(chip, NZ), lax.rem(s, 2), chip


def device(x, y, z, k):
    return (x, (y * NZ + z) * 2 + k)


def remote(src, dst, send_sem, recv_sem, dev):
    return pltpu.make_async_remote_copy(
        src_ref=src, dst_ref=dst, send_sem=send_sem, recv_sem=recv_sem,
        device_id=dev, device_id_type=MESH,
    )


def over(first, last, fn):
    def step(d, carry):
        fn(d)
        return carry

    lax.fori_loop(first, last, step, 0)


def enter():
    x, y, z, k, chip = place()
    s = 2 * chip + k
    seq = CHIPS * 2
    partners = [device(x, y, z, 1 - k)]
    partners += [device(lax.rem(x + d, NX), y, z, k) for d in range(1, NX)]
    partners += [device(x, lax.rem(y + d, NY), z, k) for d in range(1, NY)]
    partners += [device(x, y, lax.rem(z + d, NZ), k) for d in range(1, NZ)]
    partners += [(x, lax.rem(s + 1, seq)), (x, lax.rem(s + seq - 1, seq))]
    barrier = pltpu.get_barrier_semaphore()
    for dev in partners:
        pl.semaphore_signal(barrier, inc=1, device_id=dev, device_id_type=MESH)
    pl.semaphore_wait(barrier, len(partners))


def gather(shard, pair, wbuf, ext, ext_t, proj, tok_ref, s_send, s_pair, s_halo, s_z, s_slab, s_swap, landed):
    x, y, z, k, chip = place()
    s = 2 * chip + k
    mate = device(x, y, z, 1 - k)
    to_mate = remote(shard, pair, s_send.at[0], s_pair, mate)
    to_mate.start()
    halo = remote(
        tok_ref.at[pl.ds(L - HALO, HALO)], ext.at[pl.ds(L, HALO)], s_send.at[1], s_halo,
        (x, lax.rem(s + 1, 2 * CHIPS)),
    )
    halo.start()
    ext[L + HALO :, :] = jnp.zeros((ext.shape[0] - L - HALO, ext.shape[1]), BF16)
    to_mate.wait_recv()
    first = k == 0
    mine, other = shard[...], pair[...]
    block = jnp.concatenate([jnp.where(first, mine, other), jnp.where(first, other, mine)], 0)
    half = z // 2
    source = lax.rem(z, 2) == k

    @pl.when(source)
    def _():
        wbuf[x, y, half, k] = block.astype(BF16)

    def z_copy(d):
        return remote(
            wbuf.at[x, y, half, k], wbuf.at[x, y, half, k], s_send.at[1 + d], s_z.at[half],
            device(x, y, lax.rem(z + d, NZ), k),
        )

    @pl.when(source)
    def _():
        for d in range(1, NZ):
            z_copy(d).start()

    for i in range(NZ // 2):

        @pl.when(2 * i + k != z)
        def _(i=i):
            remote(
                wbuf.at[x, y, i, k], wbuf.at[x, y, i, k], s_send.at[0], s_z.at[i], mate
            ).wait_recv()

    sent = []

    def slab_copy(sx, sy, tx, ty, sem):
        ref = wbuf.at[sx, sy, :, k]
        return remote(ref, ref, s_send.at[sem], s_slab.at[sx * NY + sy], device(tx, ty, z, k))

    def swap(sx, sy, kk, sem):
        ref = wbuf.at[sx, sy, :, kk]
        return remote(ref, ref, s_send.at[24 + sem], s_swap.at[sx * NY + sy], mate)

    def start(copy):
        copy.start()
        sent.append(copy)

    def near(d):
        return lax.rem(x + d * k, NX), lax.rem(y + d * (1 - k), NY)

    def far(d):
        return lax.rem(x + d * (1 - k), NX), lax.rem(y + d * k, NY)

    for d in range(1, 4):
        tx, ty = near(d)
        start(slab_copy(x, y, tx, ty, 8 + d))
    for d in range(1, 4):
        tx, ty = far(d)
        start(slab_copy(x, y, tx, ty, 11 + d))
    start(swap(x, y, k, 0))
    n = 0
    for d in range(1, 4):
        sx, sy = near(d)
        slab_copy(sx, sy, x, y, 0).wait_recv()
        for t in range(1, 4):
            tx, ty = far(t)
            start(slab_copy(sx, sy, tx, ty, 15 + n))
            n += 1
        start(swap(sx, sy, k, d))
    landed()
    halo.wait_recv()

    @pl.when(s == 0)
    def _():
        ext[L : L + HALO, :] = jnp.zeros((HALO, ext.shape[1]), BF16)

    ext_t[...] = ext[...].T
    n = 4
    for e in range(4):
        for d in range(1, 4):
            fx, fy = far(d)
            sx = lax.rem(fx + e * k, NX)
            sy = lax.rem(fy + e * (1 - k), NY)
            slab_copy(sx, sy, x, y, 0).wait_recv()
            start(swap(sx, sy, k, n))
            n += 1
    for sx in range(NX):
        for sy in range(NY):
            swap(sx, sy, 1 - k, 0).wait_recv()
    result = dg(ext[0 : L + HALO, :], wbuf[...].reshape(ext.shape[1], WIDE), 1, 0)
    proj[HALO:, :] = result[0:L]
    proj[0:HALO, :] = result[L:]

    def drain():
        to_mate.wait_send()
        halo.wait_send()
        for copy in sent:
            copy.wait_send()

        @pl.when(source)
        def _():
            for d in range(1, NZ):
                z_copy(d).wait_send()

    return drain


def scan(loc, part, snd, rcv, snd2, rcv2, mine_in, other_in, st, s_send, s_part, s_one, s_two, s_fin, meanwhile, meanwhile2):
    x, y, z, k, chip = place()
    mate = device(x, y, z, 1 - k)

    def peer(d):
        c = lax.rem(chip + d, CHIPS)
        return c, (x, 2 * c + k)

    to_mate = remote(loc.at[1 - k], part, s_send.at[0], s_part, mate)
    to_mate.start()
    to_mate.wait_recv()
    first = k == 0
    own, other = loc[k], part[...]
    one0 = jnp.where(first, own, other)
    one1 = jnp.where(first, other, own)
    a0, ad0 = one0[256:257], one0[257:258]
    a1, ad1 = one1[256:257], one1[257:258]
    fs = a1 * one0[0:64] + one1[0:64]
    ft = a1 * one0[64:128] + ad1 * one0[0:64] + one1[64:128]
    bs = a0 * one1[128:192] + one0[128:192]
    bt = a0 * one1[192:256] + ad0 * one1[128:192] + one0[192:256]
    a, ad = a0 * a1, ad0 * a1 + a0 * ad1
    row = iota((8, HALF), 0)
    dec = jnp.where(row == 0, a, jnp.where(row == 1, ad, 0.0))
    for g in range(8):
        for i in range(4):
            j = 4 * g + i
            lanes = slice(128 * i, 128 * i + 128)
            rows = slice(8 * g, 8 * g + 8)
            snd[j, 0] = fs[rows, lanes]
            snd[j, 1] = ft[rows, lanes]
            snd[j, 2] = bs[rows, lanes]
            snd[j, 3] = bt[rows, lanes]
            snd[j, 4] = dec[:, lanes]

    def first_copy(d):
        c, dev = peer(d)
        return remote(snd.at[c], rcv.at[chip], s_send.at[d], s_one.at[chip], dev)

    def second_copy(d):
        c, dev = peer(d)
        return remote(snd2.at[c], rcv2.at[chip], s_send.at[CHIPS + d], s_two.at[chip], dev)

    over(1, CHIPS, lambda d: first_copy(d).start())
    rcv[chip] = snd[chip]
    ready = meanwhile()

    def first_arrived(d):
        c, dev = peer(d)
        remote(snd.at[c], rcv.at[c], s_send.at[d], s_one.at[c], dev).wait_recv()

    over(1, CHIPS, first_arrived)
    zero = jnp.zeros((8, 128), F32)
    s, t = zero, zero
    for c in range(CHIPS):
        snd2[c, 0] = s
        snd2[c, 1] = t
        ca, cad = rcv[c, 4, 0:1, :], rcv[c, 4, 1:2, :]
        s, t = ca * s + rcv[c, 0], ca * t + (cad * s + rcv[c, 1])
    s, t = zero, zero
    for c in range(CHIPS - 1, -1, -1):
        snd2[c, 2] = s
        snd2[c, 3] = t
        ca, cad = rcv[c, 4, 0:1, :], rcv[c, 4, 1:2, :]
        s, t = ca * s + rcv[c, 2], ca * t + (cad * s + rcv[c, 3])

    over(1, CHIPS, lambda d: second_copy(d).start())
    rcv2[chip] = snd2[chip]
    ready = meanwhile2(ready)

    def second_arrived(d):
        c, dev = peer(d)
        remote(snd2.at[c], rcv2.at[c], s_send.at[CHIPS + d], s_two.at[c], dev).wait_recv()

    over(1, CHIPS, second_arrived)
    for g in range(8):
        for i in range(4):
            j = 4 * g + i
            lanes = slice(128 * i, 128 * i + 128)
            for kind in range(4):
                base = 64 * kind + 8 * g
                mine_in[base : base + 8, lanes] = rcv2[j, kind]
    own, other = loc[k], part[...]
    one0 = jnp.where(first, own, other)
    one1 = jnp.where(first, other, own)
    fs, ft, bs, bt = (mine_in[64 * i : 64 * i + 64, :] for i in range(4))
    later_s = a0 * fs + one0[0:64]
    later_t = a0 * ft + ad0 * fs + one0[64:128]
    early_s = a1 * bs + one1[128:192]
    early_t = a1 * bt + ad1 * bs + one1[192:256]
    other_in[0:64, :] = jnp.where(first, later_s, fs)
    other_in[64:128, :] = jnp.where(first, later_t, ft)
    other_in[128:192, :] = jnp.where(first, bs, early_s)
    other_in[192:256, :] = jnp.where(first, bt, early_t)
    back = remote(other_in, st.at[k], s_send.at[2 * CHIPS], s_fin, mate)
    back.start()
    st[k, 0:64, :] = jnp.where(first, fs, later_s)
    st[k, 64:128, :] = jnp.where(first, ft, later_t)
    st[k, 128:192, :] = jnp.where(first, early_s, bs)
    st[k, 192:256, :] = jnp.where(first, early_t, bt)
    remote(other_in, st.at[1 - k], s_send.at[2 * CHIPS], s_fin, mate).wait_recv()

    def drain():
        to_mate.wait_send()
        over(1, CHIPS, lambda d: first_copy(d).wait_send())
        over(1, CHIPS, lambda d: second_copy(d).wait_send())
        back.wait_send()

    return ready, drain


def reduce(dp, ext_t, full, g2, m01, m2, a0, a1, a2, r0, r1, r2, b0, b1, b2, q0, q1, q2, c0, c1, c2, p0, p1, p2,
           e2, f2, s_send, s_mate, s_a, s_b, s_c, s_e, outs):
    x, y, z, k, chip = place()
    mate = device(x, y, z, 1 - k)
    holder = lax.rem(z, 2) == k

    def x_to(d):
        return device(lax.rem(x + d, NX), y, z, k)

    def y_to(d):
        return device(x, lax.rem(y + d, NY), z, k)

    def z_to(d):
        return device(x, y, lax.rem(z + d, NZ), k)

    high, low = split(dp)
    low_half = iota((8, 128), 1) < 64
    block_rows = NY * NZ * 16
    used = [0]

    def copy(src, dst, recv_sem, dev):
        used[0] += 1
        return remote(src, dst, s_send.at[used[0] - 1], recv_sem, dev)

    everything = []
    mates, first0, first1 = [], [], []

    def settle(i):
        xb = lax.rem(x + 1 + i, NX)
        for c in mates[3 * i : 3 * i + 3]:
            c.wait_recv()
        a0[xb] = full[0, xb, :, :, k] + m01[0, xb]
        if i < NX - 1:
            first0.append(copy(a0.at[xb], r0.at[i], s_a.at[i], x_to(1 + i)))
            first0[-1].start()
        a1[xb] = full[1, xb, :, :, k] + m01[1, xb]
        for d in range(1, NY):
            first1.append(copy(a1.at[xb, lax.rem(y + d, NY)], r1.at[d - 1, xb], s_a.at[3 + 3 * i + d - 1], y_to(d)))
            first1[-1].start()
        a2[xb] = g2[k, xb] + m2[xb]

    for i in range(NX):
        xb = lax.rem(x + 1 + i, NX)
        rows = ext_t[pl.ds(pl.multiple_of(xb * block_rows, block_rows), block_rows), :]
        part = dg(rows, high, 1, 0) + dg(rows, low, 1, 0)
        full[0, xb] = part[:, 0:128].reshape(NY, NZ, 2, 8, 128)
        full[1, xb] = part[:, 128:256].reshape(NY, NZ, 2, 8, 128)
        steps = part[:, 256:384].reshape(NY, NZ // 2, 2, 2, 8, 128)
        for zp in range(2):
            g2[zp, xb] = jnp.where(low_half, steps[:, :, zp, 0], steps[:, :, zp, 1])
        for tile in range(2):
            mates.append(copy(full.at[tile, xb, :, :, 1 - k], m01.at[tile, xb], s_mate.at[3 * i + tile], mate))
            mates[-1].start()
        mates.append(copy(g2.at[1 - k, xb], m2.at[xb], s_mate.at[3 * i + 2], mate))
        mates[-1].start()
        if i > 0:
            settle(i - 1)
    settle(NX - 1)

    def z_block(i, slot):
        used[0] += 1
        return remote(a2.at[:, :, i], r2.at[slot], s_send.at[used[0] - 1], s_a.at[16 + slot], device(x, y, 2 * i + k, k))

    zsend = []
    for i in range(NZ // 2):
        gap = lax.rem(z - (2 * i + k) + NZ, NZ)
        zsend.append((2 * i + k != z, z_block(i, gap)))
        pl.when(zsend[-1][0])(zsend[-1][1].start)

    for c in first0:
        c.wait_recv()
    b0[...] = (a0[x] + r0[0]) + (r0[1] + r0[2])
    second0 = []
    for d in range(1, NY):
        second0.append(copy(b0.at[lax.rem(y + d, NY)], q0.at[d - 1], s_b.at[d], y_to(d)))
        second0[-1].start()
    for i in range(NX):
        xb = lax.rem(x + 1 + i, NX)
        for c in first1[3 * i : 3 * i + 3]:
            c.wait_recv()
    b1[...] = (a1[:, y] + r1[0]) + (r1[1] + r1[2])
    second1 = []
    for d in range(1, NZ):
        second1.append(copy(b1.at[:, lax.rem(z + d, NZ)], q1.at[d - 1], s_b.at[3 + d], z_to(d)))
        second1[-1].start()
    second2 = [copy(b2.at[lax.rem(x + d, NX)], q2.at[d - 1], s_b.at[10 + d], x_to(d)) for d in range(1, NX)]

    @pl.when(holder)
    def _():
        for gap in range(1, NZ):
            remote(a2.at[:, :, 0], r2.at[gap], s_send.at[0], s_a.at[16 + gap], mate).wait_recv()
        total = a2[:, :, z // 2] + ((r2[1] + r2[2]) + (r2[3] + r2[4]))
        b2[...] = total + ((r2[5] + r2[6]) + r2[7])
        for c in second2:
            c.start()

    for c in second0:
        c.wait_recv()
    c0[...] = (b0[y] + q0[0]) + (q0[1] + q0[2])
    third0, third1 = [], []
    for d in range(1, NZ):
        third0.append(copy(c0.at[lax.rem(z + d, NZ)], p0.at[d - 1], s_c.at[d], z_to(d)))
        third0[-1].start()
    third2 = [copy(c2.at[lax.rem(y + d, NY)], p2.at[d - 1], s_c.at[10 + d], y_to(d)) for d in range(1, NY)]

    @pl.when(holder)
    def _():
        for c in second2:
            c.wait_recv()
        c2[...] = (b2[x] + q2[0]) + (q2[1] + q2[2])
        for c in third2:
            c.start()

    for c in second1:
        c.wait_recv()
    c1[...] = b1[:, z] + ((q1[0] + q1[1]) + (q1[2] + q1[3])) + ((q1[4] + q1[5]) + q1[6])
    for d in range(1, NX):
        third1.append(copy(c1.at[lax.rem(x + d, NX)], p1.at[d - 1], s_c.at[7 + d], x_to(d)))
        third1[-1].start()
    last = copy(e2, f2, s_e, mate)

    @pl.when(holder)
    def _():
        for c in third2:
            c.wait_recv()
        e2[...] = (c2[y] + p2[0]) + (p2[1] + p2[2])
        last.start()

    for c in third0:
        c.wait_recv()
    outs[0][...] = c0[z] + ((p0[0] + p0[1]) + (p0[2] + p0[3])) + ((p0[4] + p0[5]) + p0[6])
    for c in third1:
        c.wait_recv()
    outs[2][...] = (c1[x] + p1[0]) + (p1[1] + p1[2])

    @pl.when(jnp.logical_not(holder))
    def _():
        last.wait_recv()
        e2[...] = f2[...]

    steps = e2[...]
    mine = jnp.where(k == 0, steps[:, 0:64], steps[:, 64:128])
    outs[1][...] = mine[:, 0:H]
    outs[3][...] = mine[:, H : 2 * H]

    for c in mates + first0 + first1 + second0 + second1 + third0 + third1:
        c.wait_send()
    for used_here, c in zsend:
        pl.when(used_here)(c.wait_send)

    @pl.when(holder)
    def _():
        for c in second2 + third2:
            c.wait_send()
        last.wait_send()


def everything(scale, sw_ref, sd_ref, tw_ref, td_ref, tok_ref, v_hbm, u_hbm, conv_ref, bias_ref, rate_ref,
               o_sel, o_step, o_selh, o_steph, v_ref, u_ref, shard, pair, wbuf, ext, ext_t, proj,
               loc, part, snd, rcv, snd2, rcv2, mine_in, other_in, st,
               rows_ref, row1_ref, row2_ref, colq_ref, colqd_ref, zp_ref, reduce_scratch,
               s_in, gather_sems, scan_sems, reduce_sems):
    local = [
        pltpu.make_async_copy(tok_ref, ext.at[pl.ds(0, L)], s_in.at[0]),
        pltpu.make_async_copy(v_hbm, v_ref, s_in.at[1]),
        pltpu.make_async_copy(u_hbm, u_ref, s_in.at[2]),
    ]
    for c in local:
        c.start()
    shard[:, 0:128] = sw_ref[...].astype(F32)
    shard[:, 128:256] = sd_ref[...].astype(F32)
    shard[:, 256 : 256 + H] = tw_ref[...].astype(F32)
    shard[:, 256 + H : 256 + 2 * H] = td_ref[...].astype(F32)
    shard[:, 256 + 2 * H :] = jnp.zeros((shard.shape[0], 128 - 2 * H), F32)
    enter()

    def landed():
        for c in local:
            c.wait()

    drain_gather = gather(shard, pair, wbuf, ext, ext_t, proj, tok_ref, *gather_sems, landed)

    rate = rate_ref[...]
    ft = features(lambda row, lane, lanes: proj[row : row + L, lane : lane + lanes], conv_ref[...], bias_ref[...], rate)
    wts = weights_of(ft)
    pp = pair_parts(ft)
    we, wde, es, eds, eu, edu = streams(wts, v_ref[...], u_ref[...])
    forward, backward = local_states(pp, we, wde, eu, edu)
    row = iota((8, HP), 0)
    dec = jnp.where(row == 0, es[L - 1 :, :], jnp.where(row == 1, eds[L - 1 :, :], 0.0))
    for half in range(2):
        lanes = slice(HALF * half, HALF * half + HALF)
        loc[half, 0:128, :] = forward[:, lanes]
        loc[half, 128:256, :] = backward[:, lanes]
        loc[half, 256:264, :] = dec[:, lanes]

    def tile(ref):
        return lambda i: ref[:, pl.ds(pl.multiple_of(i * 128, 128), 128)]

    def meanwhile():
        g, gd = intra_setup(ft, pp, rows_ref, row1_ref, row2_ref)
        return intra(ft, g, gd, tile(v_ref), tile(u_ref), rows_ref, row1_ref, row2_ref, colq_ref, colqd_ref)

    def meanwhile2(ready):
        return intra_pairs(pp, *ready)

    pairs, drain_scan = scan(
        loc, part, snd, rcv, snd2, rcv2, mine_in, other_in, st, *scan_sems, meanwhile, meanwhile2
    )
    xf = jnp.concatenate([st[0, 0:128, :], st[1, 0:128, :]], 1)
    xb = jnp.concatenate([st[0, 128:256, :], st[1, 128:256, :]], 1)
    dz, dzd, dq, dqd = finish(
        ft, wts, pp, pairs, row1_ref[...], row2_ref[...], colq_ref[...], colqd_ref[...],
        we, wde, eu, edu, v_ref[...], u_ref[...], xf, xb, rate, scale,
    )
    zp_ref[...] = jnp.zeros(zp_ref.shape, F32)
    zp_ref[HALO : HALO + L, 0:128] = dz
    zp_ref[HALO : HALO + L, 128:256] = dzd
    conv = conv_ref[...]

    def spread(first_row, count, lanes):
        total = conv[0:1, :] * zp_ref[first_row + 3 : first_row + 3 + count, lanes]
        for tap in range(1, KCONV):
            total = total + conv[tap : tap + 1, :] * zp_ref[first_row + 3 - tap : first_row + 3 - tap + count, lanes]
        return total

    pad = jnp.zeros((128 - HALO, 128), F32)
    columns = []
    for half in range(2):
        lanes = slice(128 * half, 128 * half + 128)
        columns.append(jnp.concatenate([spread(HALO, L, lanes), spread(0, HALO, lanes), pad], 0))
    both = jnp.concatenate([dq, dqd, dq, dqd], 1)
    columns.append(jnp.concatenate([both, jnp.zeros((128, 128), F32)], 0))
    dp = jnp.concatenate(columns, 1)
    reduce(dp, ext_t, *reduce_scratch, *reduce_sems, (o_sel, o_step, o_selh, o_steph))
    drain_gather()
    drain_scan()


def vmem(shape, dtype=F32):
    return pltpu.VMEM(shape, dtype)


def dma(*shape):
    return pltpu.SemaphoreType.DMA(shape)


def body(tokens, values, cotangent, sel_weight, step_weight, sel_dir, step_dir, conv_weight, step_bias, decay_rate):
    own_tokens, v, u = tokens[0], values[0], cotangent[0]
    depth = own_tokens.shape[1]
    rows = sel_weight.shape[0]
    scale = 1.0 / math.sqrt(NX * CHIPS * 2 * L)
    spec = pl.BlockSpec(memory_space=pltpu.VMEM)
    hbm = pl.BlockSpec(memory_space=pl.ANY)
    tiles = NX * NY * NZ
    reduce_scratch = (
        [vmem((2, NX, NY, NZ, 2, 8, 128)), vmem((2, NX, NY, NZ // 2, 8, 128)),
         vmem((2, NX, NY, NZ, 8, 128)), vmem((NX, NY, NZ // 2, 8, 128))]
        + [vmem((NX, NY, NZ, 8, 128))] * 2 + [vmem((NX, NY, NZ // 2, 8, 128))]
        + [vmem((3, NY, NZ, 8, 128)), vmem((3, NX, NZ, 8, 128)), vmem((NZ, NX, NY, 8, 128))]
        + [vmem((NY, NZ, 8, 128)), vmem((NX, NZ, 8, 128)), vmem((NX, NY, 8, 128))]
        + [vmem((3, NZ, 8, 128)), vmem((7, NX, 8, 128)), vmem((3, NY, 8, 128))]
        + [vmem((NZ, 8, 128)), vmem((NX, 8, 128)), vmem((NY, 8, 128))]
        + [vmem((7, 8, 128)), vmem((3, 8, 128)), vmem((3, 8, 128))]
        + [vmem((8, 128)), vmem((8, 128))]
    )
    scratch = [
        vmem((L, HP), BF16), vmem((L, HP), BF16),
        vmem((rows, WIDE)), vmem((rows, WIDE)), vmem((NX, NY, NZ // 2, 2, 2 * rows, WIDE), BF16),
        vmem((2 * L, depth), BF16), vmem((depth, 2 * L), BF16), vmem((HALO + L, WIDE)),
        vmem((2, 264, HALF)), vmem((264, HALF)), vmem((CHIPS, 5, 8, 128)), vmem((CHIPS, 5, 8, 128)),
        vmem((CHIPS, 4, 8, 128)), vmem((CHIPS, 4, 8, 128)), vmem((256, HALF)), vmem((256, HALF)),
        vmem((2, 256, HALF)),
        vmem((3 * H, L)), vmem((L, L)), vmem((L, L)), vmem((H, L)), vmem((H, L)), vmem((HALO + L + 8, 256)),
        reduce_scratch,
        dma(3),
        [dma(40), dma(), dma(), dma(NZ // 2), dma(NX * NY), dma(NX * NY)],
        [dma(2 * CHIPS + 1), dma(), dma(CHIPS), dma(CHIPS), dma()],
        [dma(64), dma(12), dma(24), dma(14), dma(14), dma()],
    ]
    return tuple(
        pl.pallas_call(
            functools.partial(everything, scale),
            out_shape=[
                jax.ShapeDtypeStruct((rows, 128), F32), jax.ShapeDtypeStruct((rows, H), F32),
                jax.ShapeDtypeStruct((rows, 128), F32), jax.ShapeDtypeStruct((rows, H), F32),
            ],
            in_specs=[spec] * 4 + [hbm] * 3 + [spec] * 3,
            out_specs=[spec] * 4,
            scratch_shapes=scratch,
            compiler_params=pltpu.CompilerParams(
                vmem_limit_bytes=VMEM_LIMIT, collective_id=0, has_side_effects=True
            ),
        )(sel_weight, sel_dir, step_weight, step_dir, own_tokens, v, u, conv_weight, step_bias[None, :], decay_rate[None, :])
    )


def solution(mesh):
    shards = P(("dp", "seq"), None)
    stream = P("dp", "seq", None)
    return jax.shard_map(
        body,
        mesh=mesh,
        in_specs=(stream, stream, stream, shards, shards, shards, shards, P(), P(), P()),
        out_specs=(shards, shards, shards, shards),
        check_vma=False,
    )
```

time: 127 us -> 96.8 us (0.76)
  Pallas kernels: 121 us -> 92.2 us
    pallas_call x5 -> x1, Pallas kernels: 121 us -> 92.2 us  [body(): pl.pallas_call(functools.partial(everything, scale), out_shape=[jax.Shape...]
    unnamed x0 -> x12, local copies, waits for them, and re-layouts: none -> 3.3 us
    slice x2 -> x0, local copies, waits for them, and re-layouts: 2.7 us -> none  [the longest x1 1.41 us: body(): out[:, 256 + H:256 + 2 * H]]
where the time goes in v2:
time: 96.8 us; the launch traced here: 96.1 us
  Pallas kernels  92.2 us (95%)
  local copies, waits for them, and re-layouts  3.3 us (3%)
    pallas_call x1, Pallas kernels, body(): pl.pallas_call(functools.partial(everything, scale), out_shape=[jax.Shape...  92.2 us
    unnamed x12, local copies, waits for them, and re-layouts  3.3 us

profile of v2, /device:TPU:1, one launch (start us, length us, event | category | flops | bytes accessed | tf_op | source)
XLA Modules:
  0.0 96.1 jit_solution(7002782546807956018)
XLA Ops:
  0.6 92.2 %shard_map.129 = (f32[8,128]{1,0:T(8,128)}, f32[8,32]{1,0:T(8,128)}, f32[8,128]{1,0:T(8,128)}, f32[8,32]{1,0:T(8,128)}) custom-call(bf16[8,128]{1,0:T(8,128)(2,1)} %sw_ref.1, bf16[8,128]{1,0:T(8,128)(2,1)} %sd_ref.1, bf16[8,32]{1,0:T(8,128)(2,1)} %tw_ref.1, bf16[8,32]{1,0:T(8,128)(2,1)} %td_ref.1, bf16[128,2048]{1,0:T(8,128)(2,1)} %bitcast.5, ...), custom_call_target="tpu_custom_call" | custom-call | tf_op jit(solution)/shard_map/pallas_call | solution.py:829
  92.8 0.0 copy-start.3
  92.8 0.7 copy-done.3
  93.5 0.0 copy-start.2
  93.5 0.6 copy.18
  94.1 0.1 copy-done.2
  94.2 0.0 copy-start.1
  94.2 0.6 copy.19
  94.8 0.1 copy-done.1
  94.9 0.0 copy-start
  94.9 0.6 copy.20
  95.4 0.1 copy-done
  95.5 0.6 copy.21
Async XLA Ops:
  92.8 0.7 copy-start.3
  93.5 0.7 copy-start.2
  94.2 0.7 copy-start.1
  94.9 0.7 copy-start

commit v3 on v2

--- a/solution.py
+++ b/solution.py
@@ -153,14 +153,14 @@
     return we, wde, es, eds, es * u, eds * u
 
 
-def local_states(pp, we, wde, eu, edu):
+def forward_states(pp, we, wde):
     left = jnp.concatenate([pp["b_bd"], pp["o_b"]], 0)
-    right = jnp.concatenate([we, wde], 0)
-    forward = dot_split(left, right, 0, 0)
+    return dot_split(left, jnp.concatenate([we, wde], 0), 0, 0)
+
+
+def backward_states(pp, eu, edu):
     left = jnp.concatenate([pp["c_cd"], pp["o_c"]], 0)
-    right = jnp.concatenate([eu, edu], 0)
-    backward = dot_split(left, right, 0, 0)
-    return forward, backward
+    return dot_split(left, jnp.concatenate([eu, edu], 0), 0, 0)
 
 
 def intra_setup(ft, pp, rows_ref, row1_ref, row2_ref):
@@ -175,7 +175,7 @@
     return g, gd
 
 
-def intra(ft, g, gd, v_of, u_of, rows_ref, row1_ref, row2_ref, colq_ref, colqd_ref):
+def intra(ft, g, gd, v_of, u_of, rows_ref, row1_ref, row2_ref, colq_ref, colqd_ref, first, last, carry):
     parts = split3(ft["cum"])
     partsd = split(ft["cumd"])
     row, lane = iota((L, L), 0), iota((L, L), 1)
@@ -214,8 +214,7 @@
         row2_ref[...] = row2
         return dgm, dgd
 
-    zero = jnp.zeros((L, L), F32)
-    return lax.fori_loop(0, H // 4, one, (zero, zero))
+    return lax.fori_loop(first, last, one, carry)
 
 
 def intra_pairs(pp, dgm, dgd):
@@ -231,23 +230,27 @@
     return dot_left(x, head_spread(), 1, 1)
 
 
-def finish(ft, wts, pp, pairs, row1, row2, colq, colqd, we, wde, eu, edu, values, cotangent, xf, xb, rate, scale):
-    e, ed, f, fd, w, wd = wts
-    v = values.astype(F32)
+def finish_forward(pp, eu, edu, cotangent, xf):
     u = cotangent.astype(F32)
     zz = dot_split(jnp.concatenate([pp["c_o"], pp["cd_c"]], 0), xf, 1, 0)
+    return head_sums(zz[:L] * u), head_sums(zz[L:] * u), dot_split(jnp.concatenate([eu, edu], 0), xf, 1, 1)
+
+
+def finish_backward(pp, we, wde, values, xb):
+    v = values.astype(F32)
     yy = dot_split(jnp.concatenate([pp["b_o"], pp["bd_b"]], 0), xb, 1, 0)
-    g = head_sums(zz[:L] * u)
-    gdot = head_sums(zz[L:] * u)
-    kk = head_sums(yy[:L] * v)
-    kdot = head_sums(yy[L:] * v)
+    return head_sums(yy[:L] * v), head_sums(yy[L:] * v), dot_split(jnp.concatenate([we, wde], 0), xb, 1, 1)
+
+
+def finish(ft, wts, pairs, row1, row2, colq, colqd, from_forward, from_backward, xf, xb, rate, scale):
+    e, ed, f, fd, w, wd = wts
+    g, gdot, pc = from_forward
+    kk, kdot, pb = from_backward
     kap = jnp.sum(xb[:64] * xf[:64], axis=0, keepdims=True)
     kapd = jnp.sum(xb[64:] * xf[:64] + xb[:64] * xf[64:], axis=0, keepdims=True)
     both = head_sums(jnp.concatenate([jnp.broadcast_to(kap, (8, HP)), jnp.broadcast_to(kapd, (8, HP))], 0))
     kap, kapd = both[0:1], both[8:9]
 
-    pc = dot_split(jnp.concatenate([eu, edu], 0), xf, 1, 1)
-    pb = dot_split(jnp.concatenate([we, wde], 0), xb, 1, 1)
     m = low_lanes()
     t1, t2, t3, t4 = pairs
     pair_c = t1 + pc[:L] + jnp.where(m, 0.0, roll64(t2 + pc[L:]))
@@ -404,6 +407,16 @@
         ext[L : L + HALO, :] = jnp.zeros((HALO, ext.shape[1]), BF16)
 
     ext_t[...] = ext[...].T
+    proj[...] = jnp.zeros(proj.shape, F32)
+
+    def project(sx, sy):
+        swap(sx, sy, 1 - k, 0).wait_recv()
+        depth = NZ * 2 * shard.shape[0]
+        at = pl.multiple_of((sx * NY + sy) * depth, depth)
+        piece = dg(ext[0 : L + HALO, pl.ds(at, depth)], wbuf[sx, sy].reshape(depth, WIDE), 1, 0)
+        proj[HALO:, :] += piece[0:L]
+        proj[0:HALO, :] += piece[L:]
+
     n = 4
     for e in range(4):
         for d in range(1, 4):
@@ -413,12 +426,14 @@
             slab_copy(sx, sy, x, y, 0).wait_recv()
             start(swap(sx, sy, k, n))
             n += 1
-    for sx in range(NX):
-        for sy in range(NY):
-            swap(sx, sy, 1 - k, 0).wait_recv()
-    result = dg(ext[0 : L + HALO, :], wbuf[...].reshape(ext.shape[1], WIDE), 1, 0)
-    proj[HALO:, :] = result[0:L]
-    proj[0:HALO, :] = result[L:]
+        if e == 0:
+            project(x, y)
+            for d in range(1, 4):
+                project(lax.rem(x + d, NX), y)
+                project(x, lax.rem(y + d, NY))
+    for e in range(1, 4):
+        for d in range(1, 4):
+            project(lax.rem(x + d, NX), lax.rem(y + e, NY))
 
     def drain():
         to_mate.wait_send()
@@ -434,119 +449,109 @@
     return drain
 
 
-def scan(loc, part, snd, rcv, snd2, rcv2, mine_in, other_in, st, s_send, s_part, s_one, s_two, s_fin, meanwhile, meanwhile2):
-    x, y, z, k, chip = place()
-    mate = device(x, y, z, 1 - k)
-
-    def peer(d):
-        c = lax.rem(chip + d, CHIPS)
-        return c, (x, 2 * c + k)
-
-    to_mate = remote(loc.at[1 - k], part, s_send.at[0], s_part, mate)
-    to_mate.start()
-    to_mate.wait_recv()
-    first = k == 0
-    own, other = loc[k], part[...]
-    one0 = jnp.where(first, own, other)
-    one1 = jnp.where(first, other, own)
-    a0, ad0 = one0[256:257], one0[257:258]
-    a1, ad1 = one1[256:257], one1[257:258]
-    fs = a1 * one0[0:64] + one1[0:64]
-    ft = a1 * one0[64:128] + ad1 * one0[0:64] + one1[64:128]
-    bs = a0 * one1[128:192] + one0[128:192]
-    bt = a0 * one1[192:256] + ad0 * one1[128:192] + one0[192:256]
-    a, ad = a0 * a1, ad0 * a1 + a0 * ad1
-    row = iota((8, HALF), 0)
-    dec = jnp.where(row == 0, a, jnp.where(row == 1, ad, 0.0))
-    for g in range(8):
-        for i in range(4):
-            j = 4 * g + i
-            lanes = slice(128 * i, 128 * i + 128)
-            rows = slice(8 * g, 8 * g + 8)
-            snd[j, 0] = fs[rows, lanes]
-            snd[j, 1] = ft[rows, lanes]
-            snd[j, 2] = bs[rows, lanes]
-            snd[j, 3] = bt[rows, lanes]
-            snd[j, 4] = dec[:, lanes]
-
-    def first_copy(d):
-        c, dev = peer(d)
-        return remote(snd.at[c], rcv.at[chip], s_send.at[d], s_one.at[chip], dev)
-
-    def second_copy(d):
-        c, dev = peer(d)
-        return remote(snd2.at[c], rcv2.at[chip], s_send.at[CHIPS + d], s_two.at[chip], dev)
-
-    over(1, CHIPS, lambda d: first_copy(d).start())
-    rcv[chip] = snd[chip]
-    ready = meanwhile()
-
-    def first_arrived(d):
-        c, dev = peer(d)
-        remote(snd.at[c], rcv.at[c], s_send.at[d], s_one.at[c], dev).wait_recv()
-
-    over(1, CHIPS, first_arrived)
-    zero = jnp.zeros((8, 128), F32)
-    s, t = zero, zero
-    for c in range(CHIPS):
-        snd2[c, 0] = s
-        snd2[c, 1] = t
-        ca, cad = rcv[c, 4, 0:1, :], rcv[c, 4, 1:2, :]
-        s, t = ca * s + rcv[c, 0], ca * t + (cad * s + rcv[c, 1])
-    s, t = zero, zero
-    for c in range(CHIPS - 1, -1, -1):
-        snd2[c, 2] = s
-        snd2[c, 3] = t
-        ca, cad = rcv[c, 4, 0:1, :], rcv[c, 4, 1:2, :]
-        s, t = ca * s + rcv[c, 2], ca * t + (cad * s + rcv[c, 3])
-
-    over(1, CHIPS, lambda d: second_copy(d).start())
-    rcv2[chip] = snd2[chip]
-    ready = meanwhile2(ready)
-
-    def second_arrived(d):
-        c, dev = peer(d)
-        remote(snd2.at[c], rcv2.at[c], s_send.at[CHIPS + d], s_two.at[c], dev).wait_recv()
-
-    over(1, CHIPS, second_arrived)
-    for g in range(8):
-        for i in range(4):
-            j = 4 * g + i
-            lanes = slice(128 * i, 128 * i + 128)
-            for kind in range(4):
-                base = 64 * kind + 8 * g
-                mine_in[base : base + 8, lanes] = rcv2[j, kind]
-    own, other = loc[k], part[...]
-    one0 = jnp.where(first, own, other)
-    one1 = jnp.where(first, other, own)
-    fs, ft, bs, bt = (mine_in[64 * i : 64 * i + 64, :] for i in range(4))
-    later_s = a0 * fs + one0[0:64]
-    later_t = a0 * ft + ad0 * fs + one0[64:128]
-    early_s = a1 * bs + one1[128:192]
-    early_t = a1 * bt + ad1 * bs + one1[192:256]
-    other_in[0:64, :] = jnp.where(first, later_s, fs)
-    other_in[64:128, :] = jnp.where(first, later_t, ft)
-    other_in[128:192, :] = jnp.where(first, bs, early_s)
-    other_in[192:256, :] = jnp.where(first, bt, early_t)
-    back = remote(other_in, st.at[k], s_send.at[2 * CHIPS], s_fin, mate)
-    back.start()
-    st[k, 0:64, :] = jnp.where(first, fs, later_s)
-    st[k, 64:128, :] = jnp.where(first, ft, later_t)
-    st[k, 128:192, :] = jnp.where(first, early_s, bs)
-    st[k, 192:256, :] = jnp.where(first, early_t, bt)
-    remote(other_in, st.at[1 - k], s_send.at[2 * CHIPS], s_fin, mate).wait_recv()
-
-    def drain():
-        to_mate.wait_send()
-        over(1, CHIPS, lambda d: first_copy(d).wait_send())
-        over(1, CHIPS, lambda d: second_copy(d).wait_send())
-        back.wait_send()
-
-    return ready, drain
+class Half:
+    def __init__(self, loc, part, snd, rcv, snd2, rcv2, other, st, rows, s_send, s_mate, s_one, s_two):
+        self.loc, self.part, self.snd, self.rcv, self.snd2, self.rcv2 = loc, part, snd, rcv, snd2, rcv2
+        self.other, self.st, self.rows = other, st, rows
+        self.s_send, self.s_mate, self.s_one, self.s_two = s_send, s_mate, s_one, s_two
+        self.x, self.y, self.z, self.k, self.chip = place()
+        self.mate = device(self.x, self.y, self.z, 1 - self.k)
+        self.first = self.k == 0
+
+    def peer(self, d):
+        c = lax.rem(self.chip + d, CHIPS)
+        return c, (self.x, 2 * c + self.k)
+
+    def to_mate(self):
+        return remote(self.loc.at[1 - self.k], self.part, self.s_send.at[0], self.s_mate.at[0], self.mate)
+
+    def one(self, d):
+        c, dev = self.peer(d)
+        piece = pl.ds(0, self.rows)
+        return remote(self.snd.at[c, piece], self.rcv.at[self.chip, piece], self.s_send.at[d], self.s_one.at[self.chip], dev)
+
+    def one_in(self, d):
+        c, dev = self.peer(d)
+        piece = pl.ds(0, self.rows)
+        return remote(self.snd.at[c, piece], self.rcv.at[c, piece], self.s_send.at[d], self.s_one.at[c], dev)
+
+    def two(self, d):
+        c, dev = self.peer(d)
+        return remote(self.snd2.at[c], self.rcv2.at[self.chip], self.s_send.at[CHIPS + d], self.s_two.at[self.chip], dev)
+
+    def two_in(self, d):
+        c, dev = self.peer(d)
+        return remote(self.snd2.at[c], self.rcv2.at[c], self.s_send.at[CHIPS + d], self.s_two.at[c], dev)
+
+    def back(self):
+        return remote(self.other, self.st.at[self.k], self.s_send.at[2 * CHIPS], self.s_mate.at[1], self.mate)
+
+    def back_in(self):
+        return remote(self.other, self.st.at[1 - self.k], self.s_send.at[2 * CHIPS], self.s_mate.at[1], self.mate)
+
+    def cores(self):
+        own, other = self.loc[self.k], self.part[...]
+        return jnp.where(self.first, own, other), jnp.where(self.first, other, own)
+
+    def start_one(self):
+        over(1, CHIPS, lambda d: self.one(d).start())
+        self.rcv[self.chip] = self.snd[self.chip]
+
+    def start_two(self):
+        over(1, CHIPS, lambda d: self.two(d).start())
+        self.rcv2[self.chip] = self.snd2[self.chip]
+
+    def wait_one(self):
+        over(1, CHIPS, lambda d: self.one_in(d).wait_recv())
+
+    def wait_two(self):
+        over(1, CHIPS, lambda d: self.two_in(d).wait_recv())
+
+    def slices(self, s, t, rest):
+        for j in range(CHIPS):
+            rows = slice(8 * (j // 4), 8 * (j // 4) + 8)
+            lanes = slice(128 * (j % 4), 128 * (j % 4) + 128)
+            self.snd[j, 0:8] = s[rows, lanes]
+            self.snd[j, 8:16] = t[rows, lanes]
+            for i, row in enumerate(rest):
+                self.snd[j, 16 + i : 17 + i] = row[:, lanes]
+
+    def prefix(self, order, decays):
+        s = t = jnp.zeros((8, 128), F32)
+        for c in order:
+            self.snd2[c, 0:8] = s
+            self.snd2[c, 8:16] = t
+            a, ad = decays[c, 16:17, :], decays[c, 17:18, :]
+            s, t = a * s + self.rcv[c, 0:8], a * t + (ad * s + self.rcv[c, 8:16])
+
+    def assemble(self, a, ad, base, base_first):
+        for j in range(CHIPS):
+            row = 8 * (j // 4)
+            lanes = slice(128 * (j % 4), 128 * (j % 4) + 128)
+            self.place_slice(row, lanes, j)
+        s, t = self.other[0:64, :], self.other[64:128, :]
+        next_s = a * s + base[0:64]
+        next_t = a * t + ad * s + base[64:128]
+        mine_is_base = self.first if base_first else jnp.logical_not(self.first)
+        self.st[self.k, 0:64, :] = jnp.where(mine_is_base, s, next_s)
+        self.st[self.k, 64:128, :] = jnp.where(mine_is_base, t, next_t)
+        self.other[0:64, :] = jnp.where(mine_is_base, next_s, s)
+        self.other[64:128, :] = jnp.where(mine_is_base, next_t, t)
+        self.back().start()
+
+    def place_slice(self, row, lanes, j):
+        self.other[row : row + 8, lanes] = self.rcv2[j, 0:8]
+        self.other[64 + row : 72 + row, lanes] = self.rcv2[j, 8:16]
+
+    def drain(self):
+        self.to_mate().wait_send()
+        over(1, CHIPS, lambda d: self.one(d).wait_send())
+        over(1, CHIPS, lambda d: self.two(d).wait_send())
+        self.back().wait_send()
 
 
 def reduce(dp, ext_t, full, g2, m01, m2, a0, a1, a2, r0, r1, r2, b0, b1, b2, q0, q1, q2, c0, c1, c2, p0, p1, p2,
-           e2, f2, s_send, s_mate, s_a, s_b, s_c, s_e, outs):
+           e2, f2, s_send, s_mate, s_a, s_b, s_c, s_e, out_ref):
     x, y, z, k, chip = place()
     mate = device(x, y, z, 1 - k)
     holder = lax.rem(z, 2) == k
@@ -675,20 +680,17 @@
 
     for c in third0:
         c.wait_recv()
-    outs[0][...] = c0[z] + ((p0[0] + p0[1]) + (p0[2] + p0[3])) + ((p0[4] + p0[5]) + p0[6])
+    out_ref[:, 0:128] = c0[z] + ((p0[0] + p0[1]) + (p0[2] + p0[3])) + ((p0[4] + p0[5]) + p0[6])
     for c in third1:
         c.wait_recv()
-    outs[2][...] = (c1[x] + p1[0]) + (p1[1] + p1[2])
+    out_ref[:, 128:256] = (c1[x] + p1[0]) + (p1[1] + p1[2])
 
     @pl.when(jnp.logical_not(holder))
     def _():
         last.wait_recv()
         e2[...] = f2[...]
 
-    steps = e2[...]
-    mine = jnp.where(k == 0, steps[:, 0:64], steps[:, 64:128])
-    outs[1][...] = mine[:, 0:H]
-    outs[3][...] = mine[:, H : 2 * H]
+    out_ref[:, 256:384] = jnp.where(k == 0, e2[...], roll64(e2[...]))
 
     for c in mates + first0 + first1 + second0 + second1 + third0 + third1:
         c.wait_send()
@@ -703,10 +705,9 @@
 
 
 def everything(scale, sw_ref, sd_ref, tw_ref, td_ref, tok_ref, v_hbm, u_hbm, conv_ref, bias_ref, rate_ref,
-               o_sel, o_step, o_selh, o_steph, v_ref, u_ref, shard, pair, wbuf, ext, ext_t, proj,
-               loc, part, snd, rcv, snd2, rcv2, mine_in, other_in, st,
-               rows_ref, row1_ref, row2_ref, colq_ref, colqd_ref, zp_ref, reduce_scratch,
-               s_in, gather_sems, scan_sems, reduce_sems):
+               out_ref, v_ref, u_ref, shard, pair, wbuf, ext, ext_t, proj,
+               forward_scratch, backward_scratch, rows_ref, row1_ref, row2_ref, colq_ref, colqd_ref, zp_ref, reduce_scratch,
+               s_in, gather_sems, forward_sems, backward_sems, reduce_sems):
     local = [
         pltpu.make_async_copy(tok_ref, ext.at[pl.ds(0, L)], s_in.at[0]),
         pltpu.make_async_copy(v_hbm, v_ref, s_in.at[1]),
@@ -732,33 +733,69 @@
     wts = weights_of(ft)
     pp = pair_parts(ft)
     we, wde, es, eds, eu, edu = streams(wts, v_ref[...], u_ref[...])
-    forward, backward = local_states(pp, we, wde, eu, edu)
+    fw = Half(*forward_scratch, 18, *forward_sems)
+    bw = Half(*backward_scratch, 16, *backward_sems)
     row = iota((8, HP), 0)
     dec = jnp.where(row == 0, es[L - 1 :, :], jnp.where(row == 1, eds[L - 1 :, :], 0.0))
+    states = forward_states(pp, we, wde)
     for half in range(2):
         lanes = slice(HALF * half, HALF * half + HALF)
-        loc[half, 0:128, :] = forward[:, lanes]
-        loc[half, 128:256, :] = backward[:, lanes]
-        loc[half, 256:264, :] = dec[:, lanes]
+        fw.loc[half, 0:128, :] = states[:, lanes]
+        fw.loc[half, 128:136, :] = dec[:, lanes]
+    fw.to_mate().start()
+    states = backward_states(pp, eu, edu)
+    for half in range(2):
+        bw.loc[half] = states[:, HALF * half : HALF * half + HALF]
+    bw.to_mate().start()
+
+    fw.to_mate().wait_recv()
+    one0, one1 = fw.cores()
+    a0, ad0 = one0[128:129], one0[129:130]
+    a1, ad1 = one1[128:129], one1[129:130]
+    fw.slices(
+        a1 * one0[0:64] + one1[0:64],
+        a1 * one0[64:128] + ad1 * one0[0:64] + one1[64:128],
+        [a0 * a1, ad0 * a1 + a0 * ad1],
+    )
+    fw.start_one()
+    bw.to_mate().wait_recv()
+    one0, one1 = bw.cores()
+    bw.slices(a0 * one1[0:64] + one0[0:64], a0 * one1[64:128] + ad0 * one1[0:64] + one0[64:128], [])
+    bw.start_one()
 
     def tile(ref):
         return lambda i: ref[:, pl.ds(pl.multiple_of(i * 128, 128), 128)]
 
-    def meanwhile():
-        g, gd = intra_setup(ft, pp, rows_ref, row1_ref, row2_ref)
-        return intra(ft, g, gd, tile(v_ref), tile(u_ref), rows_ref, row1_ref, row2_ref, colq_ref, colqd_ref)
-
-    def meanwhile2(ready):
-        return intra_pairs(pp, *ready)
-
-    pairs, drain_scan = scan(
-        loc, part, snd, rcv, snd2, rcv2, mine_in, other_in, st, *scan_sems, meanwhile, meanwhile2
-    )
-    xf = jnp.concatenate([st[0, 0:128, :], st[1, 0:128, :]], 1)
-    xb = jnp.concatenate([st[0, 128:256, :], st[1, 128:256, :]], 1)
+    g, gd = intra_setup(ft, pp, rows_ref, row1_ref, row2_ref)
+    zero = jnp.zeros((L, L), F32)
+
+    def block_terms(first, last, carry):
+        return intra(
+            ft, g, gd, tile(v_ref), tile(u_ref), rows_ref, row1_ref, row2_ref, colq_ref, colqd_ref, first, last, carry
+        )
+
+    carry = block_terms(0, 6, (zero, zero))
+    fw.wait_one()
+    fw.prefix(range(CHIPS), fw.rcv)
+    fw.start_two()
+    carry = block_terms(6, 8, carry)
+    bw.wait_one()
+    bw.prefix(range(CHIPS - 1, -1, -1), fw.rcv)
+    bw.start_two()
+    pairs = intra_pairs(pp, *carry)
+    fw.wait_two()
+    fw.assemble(a0, ad0, fw.cores()[0], True)
+    fw.back_in().wait_recv()
+    xf = jnp.concatenate([fw.st[0], fw.st[1]], 1)
+    from_forward = finish_forward(pp, eu, edu, u_ref[...], xf)
+    bw.wait_two()
+    bw.assemble(a1, ad1, bw.cores()[1], False)
+    bw.back_in().wait_recv()
+    xb = jnp.concatenate([bw.st[0], bw.st[1]], 1)
+    from_backward = finish_backward(pp, we, wde, v_ref[...], xb)
     dz, dzd, dq, dqd = finish(
-        ft, wts, pp, pairs, row1_ref[...], row2_ref[...], colq_ref[...], colqd_ref[...],
-        we, wde, eu, edu, v_ref[...], u_ref[...], xf, xb, rate, scale,
+        ft, wts, pairs, row1_ref[...], row2_ref[...], colq_ref[...], colqd_ref[...],
+        from_forward, from_backward, xf, xb, rate, scale,
     )
     zp_ref[...] = jnp.zeros(zp_ref.shape, F32)
     zp_ref[HALO : HALO + L, 0:128] = dz
@@ -779,9 +816,17 @@
     both = jnp.concatenate([dq, dqd, dq, dqd], 1)
     columns.append(jnp.concatenate([both, jnp.zeros((128, 128), F32)], 0))
     dp = jnp.concatenate(columns, 1)
-    reduce(dp, ext_t, *reduce_scratch, *reduce_sems, (o_sel, o_step, o_selh, o_steph))
+    reduce(dp, ext_t, *reduce_scratch, *reduce_sems, out_ref)
     drain_gather()
-    drain_scan()
+    fw.drain()
+    bw.drain()
+
+
+def split_outputs(sums_ref, o_sel, o_step, o_selh, o_steph):
+    o_sel[...] = sums_ref[:, 0:128]
+    o_selh[...] = sums_ref[:, 128:256]
+    o_step[...] = sums_ref[:, 256 : 256 + H]
+    o_steph[...] = sums_ref[:, 256 + H : 256 + 2 * H]
 
 
 def vmem(shape, dtype=F32):
@@ -811,35 +856,43 @@
         + [vmem((7, 8, 128)), vmem((3, 8, 128)), vmem((3, 8, 128))]
         + [vmem((8, 128)), vmem((8, 128))]
     )
+
+    def scan_scratch(piece):
+        return [vmem((CHIPS, piece, 128))] * 2 + [vmem((CHIPS, 16, 128))] * 2 + [vmem((128, HALF)), vmem((2, 128, HALF))]
+
     scratch = [
         vmem((L, HP), BF16), vmem((L, HP), BF16),
         vmem((rows, WIDE)), vmem((rows, WIDE)), vmem((NX, NY, NZ // 2, 2, 2 * rows, WIDE), BF16),
         vmem((2 * L, depth), BF16), vmem((depth, 2 * L), BF16), vmem((HALO + L, WIDE)),
-        vmem((2, 264, HALF)), vmem((264, HALF)), vmem((CHIPS, 5, 8, 128)), vmem((CHIPS, 5, 8, 128)),
-        vmem((CHIPS, 4, 8, 128)), vmem((CHIPS, 4, 8, 128)), vmem((256, HALF)), vmem((256, HALF)),
-        vmem((2, 256, HALF)),
+        [vmem((2, 136, HALF)), vmem((136, HALF))] + scan_scratch(24),
+        [vmem((2, 128, HALF)), vmem((128, HALF))] + scan_scratch(16),
         vmem((3 * H, L)), vmem((L, L)), vmem((L, L)), vmem((H, L)), vmem((H, L)), vmem((HALO + L + 8, 256)),
         reduce_scratch,
         dma(3),
         [dma(40), dma(), dma(), dma(NZ // 2), dma(NX * NY), dma(NX * NY)],
-        [dma(2 * CHIPS + 1), dma(), dma(CHIPS), dma(CHIPS), dma()],
+        [dma(2 * CHIPS + 1), dma(2), dma(CHIPS), dma(CHIPS)],
+        [dma(2 * CHIPS + 1), dma(2), dma(CHIPS), dma(CHIPS)],
         [dma(64), dma(12), dma(24), dma(14), dma(14), dma()],
     ]
-    return tuple(
-        pl.pallas_call(
-            functools.partial(everything, scale),
-            out_shape=[
-                jax.ShapeDtypeStruct((rows, 128), F32), jax.ShapeDtypeStruct((rows, H), F32),
-                jax.ShapeDtypeStruct((rows, 128), F32), jax.ShapeDtypeStruct((rows, H), F32),
-            ],
-            in_specs=[spec] * 4 + [hbm] * 3 + [spec] * 3,
-            out_specs=[spec] * 4,
-            scratch_shapes=scratch,
-            compiler_params=pltpu.CompilerParams(
-                vmem_limit_bytes=VMEM_LIMIT, collective_id=0, has_side_effects=True
-            ),
-        )(sel_weight, sel_dir, step_weight, step_dir, own_tokens, v, u, conv_weight, step_bias[None, :], decay_rate[None, :])
-    )
+    sums = pl.pallas_call(
+        functools.partial(everything, scale),
+        out_shape=jax.ShapeDtypeStruct((rows, WIDE), F32),
+        in_specs=[spec] * 4 + [hbm] * 3 + [spec] * 3,
+        out_specs=spec,
+        scratch_shapes=scratch,
+        compiler_params=pltpu.CompilerParams(
+            vmem_limit_bytes=VMEM_LIMIT, collective_id=0, has_side_effects=True
+        ),
+    )(sel_weight, sel_dir, step_weight, step_dir, own_tokens, v, u, conv_weight, step_bias[None, :], decay_rate[None, :])
+    return pl.pallas_call(
+        split_outputs,
+        out_shape=[
+            jax.ShapeDtypeStruct((rows, 128), F32), jax.ShapeDtypeStruct((rows, H), F32),
+            jax.ShapeDtypeStruct((rows, 128), F32), jax.ShapeDtypeStruct((rows, H), F32),
+        ],
+        in_specs=[spec],
+        out_specs=[spec] * 4,
+    )(sums)
 
 
 def solution(mesh):

time: 96.8 us -> 88.9 us (0.918)
  Pallas kernels: 92.2 us -> 88.1 us
  local copies, waits for them, and re-layouts: 3.3 us -> 0 us
    pallas_call x1 -> x2, Pallas kernels: 92.2 us -> 88.1 us  [the longest x1 86.7 us: body(): pl.pallas_call(functools.partial(everything, scale), out_shape=jax.ShapeD...]
    unnamed x12 -> x0, local copies, waits for them, and re-layouts: 3.3 us -> none
where the time goes in v3:
time: 88.9 us; the launch traced here: 88.7 us
  Pallas kernels  88.1 us (99%)
    pallas_call x1, Pallas kernels, body(): pl.pallas_call(functools.partial(everything, scale), out_shape=jax.ShapeD...  86.7 us

profile of v3, /device:TPU:1, one launch (start us, length us, event | category | flops | bytes accessed | tf_op | source)
XLA Modules:
  0.0 88.7 jit_solution(10676082187773441228)
XLA Ops:
  0.6 86.7 %shard_map.129.sums_ref = f32[8,384]{1,0:T(8,128)} custom-call(bf16[8,128]{1,0:T(8,128)(2,1)} %sw_ref.1, bf16[8,128]{1,0:T(8,128)(2,1)} %sd_ref.1, bf16[8,32]{1,0:T(8,128)(2,1)} %tw_ref.1, bf16[8,32]{1,0:T(8,128)(2,1)} %td_ref.1, bf16[128,2048]{1,0:T(8,128)(2,1)} %bitcast.5, bf16[128,1024]{1,0:T(8,128)(2,1)} %bitcast.6, bf16[128,1024]{1,0:T(8,128)(2,1)} %bitcast.7, ...), custom_call_target="tpu_custom_call" | custom-call | tf_op jit(solution)/shard_map/pallas_call | solution.py:877
  87.4 1.4 %shard_map.130 = (f32[8,128]{1,0:T(8,128)}, f32[8,32]{1,0:T(8,128)}, f32[8,128]{1,0:T(8,128)}, f32[8,32]{1,0:T(8,128)}) custom-call(f32[8,384]{1,0:T(8,128)} %shard_map.129.sums_ref), custom_call_target="tpu_custom_call" | custom-call | tf_op jit(solution)/shard_map/pallas_call | solution.py:887

commit v4 on v3

--- a/solution.py
+++ b/solution.py
@@ -298,12 +298,12 @@
     )
 
 
-def over(first, last, fn):
-    def step(d, carry):
-        fn(d)
-        return carry
-
-    lax.fori_loop(first, last, step, 0)
+def arrived(dst, sem, dev):
+    remote(dst, dst, sem, sem, dev).wait_recv()
+
+
+def sent(src, sem, dev):
+    remote(src, src, sem, sem, dev).wait_send()
 
 
 def enter():
@@ -318,64 +318,30 @@
     barrier = pltpu.get_barrier_semaphore()
     for dev in partners:
         pl.semaphore_signal(barrier, inc=1, device_id=dev, device_id_type=MESH)
-    pl.semaphore_wait(barrier, len(partners))
-
-
-def gather(shard, pair, wbuf, ext, ext_t, proj, tok_ref, s_send, s_pair, s_halo, s_z, s_slab, s_swap, landed):
+    return lambda: pl.semaphore_wait(barrier, len(partners))
+
+
+def gather(wbuf, ext, ext_t, proj, tok_ref, s_send, s_halo, s_z, s_slab, s_swap):
     x, y, z, k, chip = place()
     s = 2 * chip + k
     mate = device(x, y, z, 1 - k)
-    to_mate = remote(shard, pair, s_send.at[0], s_pair, mate)
-    to_mate.start()
+    own = wbuf.at[x, y, z, k]
+    for d in range(1, NZ):
+        remote(own, own, s_send.at[0], s_z, device(x, y, lax.rem(z + d, NZ), k)).start()
     halo = remote(
-        tok_ref.at[pl.ds(L - HALO, HALO)], ext.at[pl.ds(L, HALO)], s_send.at[1], s_halo,
+        tok_ref.at[pl.ds(L - HALO, HALO)], ext.at[pl.ds(L, HALO)], s_send.at[4], s_halo,
         (x, lax.rem(s + 1, 2 * CHIPS)),
     )
     halo.start()
-    ext[L + HALO :, :] = jnp.zeros((ext.shape[0] - L - HALO, ext.shape[1]), BF16)
-    to_mate.wait_recv()
-    first = k == 0
-    mine, other = shard[...], pair[...]
-    block = jnp.concatenate([jnp.where(first, mine, other), jnp.where(first, other, mine)], 0)
-    half = z // 2
-    source = lax.rem(z, 2) == k
-
-    @pl.when(source)
-    def _():
-        wbuf[x, y, half, k] = block.astype(BF16)
-
-    def z_copy(d):
-        return remote(
-            wbuf.at[x, y, half, k], wbuf.at[x, y, half, k], s_send.at[1 + d], s_z.at[half],
-            device(x, y, lax.rem(z + d, NZ), k),
-        )
-
-    @pl.when(source)
-    def _():
-        for d in range(1, NZ):
-            z_copy(d).start()
-
-    for i in range(NZ // 2):
-
-        @pl.when(2 * i + k != z)
-        def _(i=i):
-            remote(
-                wbuf.at[x, y, i, k], wbuf.at[x, y, i, k], s_send.at[0], s_z.at[i], mate
-            ).wait_recv()
-
-    sent = []
+    arrived(wbuf.at[x, y, pl.ds(0, NZ - 1), k], s_z, mate)
 
     def slab_copy(sx, sy, tx, ty, sem):
         ref = wbuf.at[sx, sy, :, k]
         return remote(ref, ref, s_send.at[sem], s_slab.at[sx * NY + sy], device(tx, ty, z, k))
 
-    def swap(sx, sy, kk, sem):
+    def swap(sx, sy, kk):
         ref = wbuf.at[sx, sy, :, kk]
-        return remote(ref, ref, s_send.at[24 + sem], s_swap.at[sx * NY + sy], mate)
-
-    def start(copy):
-        copy.start()
-        sent.append(copy)
+        return remote(ref, ref, s_send.at[3], s_swap.at[sx * NY + sy], mate)
 
     def near(d):
         return lax.rem(x + d * k, NX), lax.rem(y + d * (1 - k), NY)
@@ -384,67 +350,48 @@
         return lax.rem(x + d * (1 - k), NX), lax.rem(y + d * k, NY)
 
     for d in range(1, 4):
-        tx, ty = near(d)
-        start(slab_copy(x, y, tx, ty, 8 + d))
+        slab_copy(x, y, *near(d), 1).start()
     for d in range(1, 4):
-        tx, ty = far(d)
-        start(slab_copy(x, y, tx, ty, 11 + d))
-    start(swap(x, y, k, 0))
-    n = 0
+        slab_copy(x, y, *far(d), 2).start()
+    swap(x, y, k).start()
     for d in range(1, 4):
         sx, sy = near(d)
-        slab_copy(sx, sy, x, y, 0).wait_recv()
+        slab_copy(sx, sy, x, y, 1).wait_recv()
         for t in range(1, 4):
-            tx, ty = far(t)
-            start(slab_copy(sx, sy, tx, ty, 15 + n))
-            n += 1
-        start(swap(sx, sy, k, d))
-    landed()
+            slab_copy(sx, sy, *far(t), 2).start()
+        swap(sx, sy, k).start()
     halo.wait_recv()
 
     @pl.when(s == 0)
     def _():
         ext[L : L + HALO, :] = jnp.zeros((HALO, ext.shape[1]), BF16)
 
-    ext_t[...] = ext[...].T
-    proj[...] = jnp.zeros(proj.shape, F32)
-
-    def project(sx, sy):
-        swap(sx, sy, 1 - k, 0).wait_recv()
-        depth = NZ * 2 * shard.shape[0]
-        at = pl.multiple_of((sx * NY + sy) * depth, depth)
-        piece = dg(ext[0 : L + HALO, pl.ds(at, depth)], wbuf[sx, sy].reshape(depth, WIDE), 1, 0)
-        proj[HALO:, :] += piece[0:L]
-        proj[0:HALO, :] += piece[L:]
-
-    n = 4
+    ext_t[:, L:] = ext[L:, :].T
     for e in range(4):
         for d in range(1, 4):
             fx, fy = far(d)
             sx = lax.rem(fx + e * k, NX)
             sy = lax.rem(fy + e * (1 - k), NY)
-            slab_copy(sx, sy, x, y, 0).wait_recv()
-            start(swap(sx, sy, k, n))
-            n += 1
-        if e == 0:
-            project(x, y)
-            for d in range(1, 4):
-                project(lax.rem(x + d, NX), y)
-                project(x, lax.rem(y + d, NY))
-    for e in range(1, 4):
-        for d in range(1, 4):
-            project(lax.rem(x + d, NX), lax.rem(y + e, NY))
+            slab_copy(sx, sy, x, y, 2).wait_recv()
+            swap(sx, sy, k).start()
+    depth = ext.shape[1] // NX
+    total = jnp.zeros((L + HALO, WIDE), F32)
+    for d in range(NX):
+        sx = lax.rem(x + d, NX)
+        for sy in range(NY):
+            swap(sx, sy, 1 - k).wait_recv()
+        at = pl.multiple_of(sx * depth, depth)
+        weights = wbuf[sx].astype(F32).reshape(depth, WIDE).astype(BF16)
+        total = total + dg(ext[0 : L + HALO, pl.ds(at, depth)], weights, 1, 0)
+    proj[HALO:, :] = total[0:L]
+    proj[0:HALO, :] = total[L:]
 
     def drain():
-        to_mate.wait_send()
+        sent(wbuf.at[0, 0, pl.ds(0, NZ - 1), 0], s_send.at[0], mate)
+        sent(wbuf.at[0, pl.ds(0, NY - 1), :, 0], s_send.at[1], mate)
+        sent(wbuf.at[pl.ds(0, NX - 1), :, :, 0], s_send.at[2], mate)
+        sent(wbuf.at[:, :, :, 0], s_send.at[3], mate)
         halo.wait_send()
-        for copy in sent:
-            copy.wait_send()
-
-        @pl.when(source)
-        def _():
-            for d in range(1, NZ):
-                z_copy(d).wait_send()
 
     return drain
 
@@ -465,47 +412,34 @@
     def to_mate(self):
         return remote(self.loc.at[1 - self.k], self.part, self.s_send.at[0], self.s_mate.at[0], self.mate)
 
-    def one(self, d):
-        c, dev = self.peer(d)
+    def start_one(self):
         piece = pl.ds(0, self.rows)
-        return remote(self.snd.at[c, piece], self.rcv.at[self.chip, piece], self.s_send.at[d], self.s_one.at[self.chip], dev)
-
-    def one_in(self, d):
-        c, dev = self.peer(d)
-        piece = pl.ds(0, self.rows)
-        return remote(self.snd.at[c, piece], self.rcv.at[c, piece], self.s_send.at[d], self.s_one.at[c], dev)
-
-    def two(self, d):
-        c, dev = self.peer(d)
-        return remote(self.snd2.at[c], self.rcv2.at[self.chip], self.s_send.at[CHIPS + d], self.s_two.at[self.chip], dev)
-
-    def two_in(self, d):
-        c, dev = self.peer(d)
-        return remote(self.snd2.at[c], self.rcv2.at[c], self.s_send.at[CHIPS + d], self.s_two.at[c], dev)
+        for d in range(1, CHIPS):
+            c, dev = self.peer(d)
+            remote(self.snd.at[c, piece], self.rcv.at[self.chip, piece], self.s_send.at[1], self.s_one, dev).start()
+        self.rcv[self.chip] = self.snd[self.chip]
+
+    def start_two(self):
+        for d in range(1, CHIPS):
+            c, dev = self.peer(d)
+            remote(self.snd2.at[c], self.rcv2.at[self.chip], self.s_send.at[2], self.s_two, dev).start()
+        self.rcv2[self.chip] = self.snd2[self.chip]
+
+    def wait_one(self):
+        arrived(self.rcv.at[pl.ds(0, CHIPS - 1), pl.ds(0, self.rows)], self.s_one, self.mate)
+
+    def wait_two(self):
+        arrived(self.rcv2.at[pl.ds(0, CHIPS - 1)], self.s_two, self.mate)
 
     def back(self):
-        return remote(self.other, self.st.at[self.k], self.s_send.at[2 * CHIPS], self.s_mate.at[1], self.mate)
+        return remote(self.other, self.st.at[self.k], self.s_send.at[3], self.s_mate.at[1], self.mate)
 
     def back_in(self):
-        return remote(self.other, self.st.at[1 - self.k], self.s_send.at[2 * CHIPS], self.s_mate.at[1], self.mate)
+        return remote(self.other, self.st.at[1 - self.k], self.s_send.at[3], self.s_mate.at[1], self.mate)
 
     def cores(self):
         own, other = self.loc[self.k], self.part[...]
         return jnp.where(self.first, own, other), jnp.where(self.first, other, own)
-
-    def start_one(self):
-        over(1, CHIPS, lambda d: self.one(d).start())
-        self.rcv[self.chip] = self.snd[self.chip]
-
-    def start_two(self):
-        over(1, CHIPS, lambda d: self.two(d).start())
-        self.rcv2[self.chip] = self.snd2[self.chip]
-
-    def wait_one(self):
-        over(1, CHIPS, lambda d: self.one_in(d).wait_recv())
-
-    def wait_two(self):
-        over(1, CHIPS, lambda d: self.two_in(d).wait_recv())
 
     def slices(self, s, t, rest):
         for j in range(CHIPS):
@@ -545,8 +479,8 @@
 
     def drain(self):
         self.to_mate().wait_send()
-        over(1, CHIPS, lambda d: self.one(d).wait_send())
-        over(1, CHIPS, lambda d: self.two(d).wait_send())
+        sent(self.snd.at[pl.ds(0, CHIPS - 1), pl.ds(0, self.rows)], self.s_send.at[1], self.mate)
+        sent(self.snd2.at[pl.ds(0, CHIPS - 1)], self.s_send.at[2], self.mate)
         self.back().wait_send()
 
 
@@ -568,27 +502,17 @@
     high, low = split(dp)
     low_half = iota((8, 128), 1) < 64
     block_rows = NY * NZ * 16
-    used = [0]
-
-    def copy(src, dst, recv_sem, dev):
-        used[0] += 1
-        return remote(src, dst, s_send.at[used[0] - 1], recv_sem, dev)
-
-    everything = []
-    mates, first0, first1 = [], [], []
 
     def settle(i):
         xb = lax.rem(x + 1 + i, NX)
-        for c in mates[3 * i : 3 * i + 3]:
-            c.wait_recv()
+        arrived(m01.at[:, xb], s_mate.at[i], mate)
         a0[xb] = full[0, xb, :, :, k] + m01[0, xb]
         if i < NX - 1:
-            first0.append(copy(a0.at[xb], r0.at[i], s_a.at[i], x_to(1 + i)))
-            first0[-1].start()
+            remote(a0.at[xb], r0.at[i], s_send.at[2], s_a.at[0], x_to(1 + i)).start()
         a1[xb] = full[1, xb, :, :, k] + m01[1, xb]
         for d in range(1, NY):
-            first1.append(copy(a1.at[xb, lax.rem(y + d, NY)], r1.at[d - 1, xb], s_a.at[3 + 3 * i + d - 1], y_to(d)))
-            first1[-1].start()
+            remote(a1.at[xb, lax.rem(y + d, NY)], r1.at[d - 1, xb], s_send.at[3], s_a.at[1], y_to(d)).start()
+        arrived(m2.at[xb], s_mate.at[NX + i], mate)
         a2[xb] = g2[k, xb] + m2[xb]
 
     for i in range(NX):
@@ -601,88 +525,71 @@
         for zp in range(2):
             g2[zp, xb] = jnp.where(low_half, steps[:, :, zp, 0], steps[:, :, zp, 1])
         for tile in range(2):
-            mates.append(copy(full.at[tile, xb, :, :, 1 - k], m01.at[tile, xb], s_mate.at[3 * i + tile], mate))
-            mates[-1].start()
-        mates.append(copy(g2.at[1 - k, xb], m2.at[xb], s_mate.at[3 * i + 2], mate))
-        mates[-1].start()
+            remote(full.at[tile, xb, :, :, 1 - k], m01.at[tile, xb], s_send.at[0], s_mate.at[i], mate).start()
+        remote(g2.at[1 - k, xb], m2.at[xb], s_send.at[1], s_mate.at[NX + i], mate).start()
         if i > 0:
             settle(i - 1)
     settle(NX - 1)
 
-    def z_block(i, slot):
-        used[0] += 1
-        return remote(a2.at[:, :, i], r2.at[slot], s_send.at[used[0] - 1], s_a.at[16 + slot], device(x, y, 2 * i + k, k))
-
     zsend = []
     for i in range(NZ // 2):
-        gap = lax.rem(z - (2 * i + k) + NZ, NZ)
-        zsend.append((2 * i + k != z, z_block(i, gap)))
+        target = 2 * i + k
+        gap = lax.rem(z - target + NZ, NZ)
+        zsend.append((target != z, remote(a2.at[:, :, i], r2.at[gap], s_send.at[4 + i], s_a.at[2], device(x, y, target, k))))
         pl.when(zsend[-1][0])(zsend[-1][1].start)
 
-    for c in first0:
-        c.wait_recv()
+    arrived(r0, s_a.at[0], mate)
     b0[...] = (a0[x] + r0[0]) + (r0[1] + r0[2])
-    second0 = []
     for d in range(1, NY):
-        second0.append(copy(b0.at[lax.rem(y + d, NY)], q0.at[d - 1], s_b.at[d], y_to(d)))
-        second0[-1].start()
-    for i in range(NX):
-        xb = lax.rem(x + 1 + i, NX)
-        for c in first1[3 * i : 3 * i + 3]:
-            c.wait_recv()
+        remote(b0.at[lax.rem(y + d, NY)], q0.at[d - 1], s_send.at[8], s_b.at[0], y_to(d)).start()
+    arrived(r1, s_a.at[1], mate)
     b1[...] = (a1[:, y] + r1[0]) + (r1[1] + r1[2])
-    second1 = []
     for d in range(1, NZ):
-        second1.append(copy(b1.at[:, lax.rem(z + d, NZ)], q1.at[d - 1], s_b.at[3 + d], z_to(d)))
-        second1[-1].start()
-    second2 = [copy(b2.at[lax.rem(x + d, NX)], q2.at[d - 1], s_b.at[10 + d], x_to(d)) for d in range(1, NX)]
+        remote(b1.at[:, lax.rem(z + d, NZ)], q1.at[d - 1], s_send.at[9], s_b.at[1], z_to(d)).start()
 
     @pl.when(holder)
     def _():
-        for gap in range(1, NZ):
-            remote(a2.at[:, :, 0], r2.at[gap], s_send.at[0], s_a.at[16 + gap], mate).wait_recv()
+        arrived(r2.at[pl.ds(1, NZ - 1)], s_a.at[2], mate)
         total = a2[:, :, z // 2] + ((r2[1] + r2[2]) + (r2[3] + r2[4]))
         b2[...] = total + ((r2[5] + r2[6]) + r2[7])
-        for c in second2:
-            c.start()
-
-    for c in second0:
-        c.wait_recv()
+        for d in range(1, NX):
+            remote(b2.at[lax.rem(x + d, NX)], q2.at[d - 1], s_send.at[10], s_b.at[2], x_to(d)).start()
+
+    arrived(q0, s_b.at[0], mate)
     c0[...] = (b0[y] + q0[0]) + (q0[1] + q0[2])
-    third0, third1 = [], []
     for d in range(1, NZ):
-        third0.append(copy(c0.at[lax.rem(z + d, NZ)], p0.at[d - 1], s_c.at[d], z_to(d)))
-        third0[-1].start()
-    third2 = [copy(c2.at[lax.rem(y + d, NY)], p2.at[d - 1], s_c.at[10 + d], y_to(d)) for d in range(1, NY)]
+        remote(c0.at[lax.rem(z + d, NZ)], p0.at[d - 1], s_send.at[11], s_c.at[0], z_to(d)).start()
 
     @pl.when(holder)
     def _():
-        for c in second2:
-            c.wait_recv()
+        arrived(q2, s_b.at[2], mate)
         c2[...] = (b2[x] + q2[0]) + (q2[1] + q2[2])
-        for c in third2:
-            c.start()
-
-    for c in second1:
-        c.wait_recv()
+        for d in range(1, NY):
+            remote(c2.at[lax.rem(y + d, NY)], p2.at[d - 1], s_send.at[12], s_c.at[2], y_to(d)).start()
+
+    arrived(q1, s_b.at[1], mate)
     c1[...] = b1[:, z] + ((q1[0] + q1[1]) + (q1[2] + q1[3])) + ((q1[4] + q1[5]) + q1[6])
     for d in range(1, NX):
-        third1.append(copy(c1.at[lax.rem(x + d, NX)], p1.at[d - 1], s_c.at[7 + d], x_to(d)))
-        third1[-1].start()
-    last = copy(e2, f2, s_e, mate)
+        remote(c1.at[lax.rem(x + d, NX)], p1.at[d - 1], s_send.at[13], s_c.at[1], x_to(d)).start()
+    last = remote(e2, f2, s_send.at[14], s_e, mate)
 
     @pl.when(holder)
     def _():
-        for c in third2:
-            c.wait_recv()
+        arrived(p2, s_c.at[2], mate)
         e2[...] = (c2[y] + p2[0]) + (p2[1] + p2[2])
         last.start()
 
-    for c in third0:
-        c.wait_recv()
+    sent(m01, s_send.at[0], mate)
+    sent(m2, s_send.at[1], mate)
+    sent(r0, s_send.at[2], mate)
+    sent(r1, s_send.at[3], mate)
+    for used, copy in zsend:
+        pl.when(used)(copy.wait_send)
+    sent(q0, s_send.at[8], mate)
+    sent(q1, s_send.at[9], mate)
+    arrived(p0, s_c.at[0], mate)
     out_ref[:, 0:128] = c0[z] + ((p0[0] + p0[1]) + (p0[2] + p0[3])) + ((p0[4] + p0[5]) + p0[6])
-    for c in third1:
-        c.wait_recv()
+    arrived(p1, s_c.at[1], mate)
     out_ref[:, 128:256] = (c1[x] + p1[0]) + (p1[1] + p1[2])
 
     @pl.when(jnp.logical_not(holder))
@@ -691,42 +598,44 @@
         e2[...] = f2[...]
 
     out_ref[:, 256:384] = jnp.where(k == 0, e2[...], roll64(e2[...]))
-
-    for c in mates + first0 + first1 + second0 + second1 + third0 + third1:
-        c.wait_send()
-    for used_here, c in zsend:
-        pl.when(used_here)(c.wait_send)
+    sent(p0, s_send.at[11], mate)
+    sent(p1, s_send.at[13], mate)
 
     @pl.when(holder)
     def _():
-        for c in second2 + third2:
-            c.wait_send()
+        sent(q2, s_send.at[10], mate)
+        sent(p2, s_send.at[12], mate)
         last.wait_send()
 
 
-def everything(scale, sw_ref, sd_ref, tw_ref, td_ref, tok_ref, v_hbm, u_hbm, conv_ref, bias_ref, rate_ref,
-               out_ref, v_ref, u_ref, shard, pair, wbuf, ext, ext_t, proj,
+def everything(scale, sw_hbm, sd_hbm, tw_hbm, td_hbm, tok_ref, v_hbm, u_hbm, conv_hbm, bias_hbm, rate_hbm,
+               out_ref, v_ref, u_ref, sw_ref, sd_ref, tw_ref, td_ref, conv_ref, bias_ref, rate_ref, wbuf, ext, ext_t, proj,
                forward_scratch, backward_scratch, rows_ref, row1_ref, row2_ref, colq_ref, colqd_ref, zp_ref, reduce_scratch,
                s_in, gather_sems, forward_sems, backward_sems, reduce_sems):
-    local = [
-        pltpu.make_async_copy(tok_ref, ext.at[pl.ds(0, L)], s_in.at[0]),
-        pltpu.make_async_copy(v_hbm, v_ref, s_in.at[1]),
-        pltpu.make_async_copy(u_hbm, u_ref, s_in.at[2]),
+    entered = enter()
+    pairs = [
+        (sw_hbm, sw_ref), (sd_hbm, sd_ref), (tw_hbm, tw_ref), (td_hbm, td_ref), (tok_ref, ext.at[pl.ds(0, L)]),
+        (v_hbm, v_ref), (u_hbm, u_ref), (conv_hbm, conv_ref), (bias_hbm, bias_ref), (rate_hbm, rate_ref),
     ]
+    local = [pltpu.make_async_copy(src, dst, s_in.at[i]) for i, (src, dst) in enumerate(pairs)]
     for c in local:
         c.start()
-    shard[:, 0:128] = sw_ref[...].astype(F32)
-    shard[:, 128:256] = sd_ref[...].astype(F32)
-    shard[:, 256 : 256 + H] = tw_ref[...].astype(F32)
-    shard[:, 256 + H : 256 + 2 * H] = td_ref[...].astype(F32)
-    shard[:, 256 + 2 * H :] = jnp.zeros((shard.shape[0], 128 - 2 * H), F32)
-    enter()
-
-    def landed():
-        for c in local:
-            c.wait()
-
-    drain_gather = gather(shard, pair, wbuf, ext, ext_t, proj, tok_ref, *gather_sems, landed)
+    x, y, z, k, _ = place()
+    ext[L + HALO :, :] = jnp.zeros((ext.shape[0] - L - HALO, ext.shape[1]), BF16)
+    for c in local[0:4]:
+        c.wait()
+    wbuf[x, y, z, k, :, 0:128] = sw_ref[...]
+    wbuf[x, y, z, k, :, 128:256] = sd_ref[...]
+    rows = sw_ref.shape[0]
+    wbuf[x, y, z, k, :, 256:384] = jnp.concatenate(
+        [tw_ref[...].astype(F32), td_ref[...].astype(F32), jnp.zeros((rows, 128 - 2 * H), F32)], 1
+    ).astype(BF16)
+    local[4].wait()
+    ext_t[:, 0:L] = ext[0:L, :].T
+    for c in local[5:]:
+        c.wait()
+    entered()
+    drain_gather = gather(wbuf, ext, ext_t, proj, tok_ref, *gather_sems)
 
     rate = rate_ref[...]
     ft = features(lambda row, lane, lanes: proj[row : row + L, lane : lane + lanes], conv_ref[...], bias_ref[...], rate)
@@ -816,10 +725,10 @@
     both = jnp.concatenate([dq, dqd, dq, dqd], 1)
     columns.append(jnp.concatenate([both, jnp.zeros((128, 128), F32)], 0))
     dp = jnp.concatenate(columns, 1)
-    reduce(dp, ext_t, *reduce_scratch, *reduce_sems, out_ref)
     drain_gather()
     fw.drain()
     bw.drain()
+    reduce(dp, ext_t, *reduce_scratch, *reduce_sems, out_ref)
 
 
 def split_outputs(sums_ref, o_sel, o_step, o_selh, o_steph):
@@ -862,22 +771,24 @@
 
     scratch = [
         vmem((L, HP), BF16), vmem((L, HP), BF16),
-        vmem((rows, WIDE)), vmem((rows, WIDE)), vmem((NX, NY, NZ // 2, 2, 2 * rows, WIDE), BF16),
+        vmem((rows, 128), BF16), vmem((rows, 128), BF16), vmem((rows, H), BF16), vmem((rows, H), BF16),
+        vmem((KCONV, 128)), vmem((1, H)), vmem((1, H)),
+        vmem((NX, NY, NZ, 2, rows, WIDE), BF16),
         vmem((2 * L, depth), BF16), vmem((depth, 2 * L), BF16), vmem((HALO + L, WIDE)),
         [vmem((2, 136, HALF)), vmem((136, HALF))] + scan_scratch(24),
         [vmem((2, 128, HALF)), vmem((128, HALF))] + scan_scratch(16),
         vmem((3 * H, L)), vmem((L, L)), vmem((L, L)), vmem((H, L)), vmem((H, L)), vmem((HALO + L + 8, 256)),
         reduce_scratch,
-        dma(3),
-        [dma(40), dma(), dma(), dma(NZ // 2), dma(NX * NY), dma(NX * NY)],
-        [dma(2 * CHIPS + 1), dma(2), dma(CHIPS), dma(CHIPS)],
-        [dma(2 * CHIPS + 1), dma(2), dma(CHIPS), dma(CHIPS)],
-        [dma(64), dma(12), dma(24), dma(14), dma(14), dma()],
+        dma(10),
+        [dma(5), dma(), dma(), dma(NX * NY), dma(NX * NY)],
+        [dma(4), dma(2), dma(), dma()],
+        [dma(4), dma(2), dma(), dma()],
+        [dma(15), dma(2 * NX), dma(3), dma(3), dma(3), dma()],
     ]
     sums = pl.pallas_call(
         functools.partial(everything, scale),
         out_shape=jax.ShapeDtypeStruct((rows, WIDE), F32),
-        in_specs=[spec] * 4 + [hbm] * 3 + [spec] * 3,
+        in_specs=[hbm] * 10,
         out_specs=spec,
         scratch_shapes=scratch,
         compiler_params=pltpu.CompilerParams(

time: 88.9 us -> 83.5 us (0.939)
  Pallas kernels: 88.1 us -> 82.7 us
    pallas_call x1, Pallas kernels: 86.7 us -> 81.3 us  [body(): pl.pallas_call(functools.partial(everything, scale), out_shape=jax.ShapeD...]
where the time goes in v4:
time: 83.5 us; the launch traced here: 83.3 us
  Pallas kernels  82.7 us (99%)
    pallas_call x1, Pallas kernels, body(): pl.pallas_call(functools.partial(everything, scale), out_shape=jax.ShapeD...  81.3 us

profile of v4, /device:TPU:1, one launch (start us, length us, event | category | flops | bytes accessed | tf_op | source)
XLA Modules:
  0.0 83.3 jit_solution(1725022285336097517)
XLA Ops:
  0.6 81.3 %shard_map.129.sums_ref = f32[8,384]{1,0:T(8,128)} custom-call(bf16[8,128]{1,0:T(8,128)(2,1)} %sw_hbm.1, bf16[8,128]{1,0:T(8,128)(2,1)} %sd_hbm.1, bf16[8,32]{1,0:T(8,128)(2,1)} %tw_hbm.1, bf16[8,32]{1,0:T(8,128)(2,1)} %td_hbm.1, bf16[128,2048]{1,0:T(8,128)(2,1)} %bitcast.5, bf16[128,1024]{1,0:T(8,128)(2,1)} %bitcast.6, bf16[128,1024]{1,0:T(8,128)(2,1)} %bitcast.7, ...), custom_call_target="tpu_custom_call" | custom-call | tf_op jit(solution)/shard_map/pallas_call | solution.py:788
  81.9 1.4 %shard_map.130 = (f32[8,128]{1,0:T(8,128)}, f32[8,32]{1,0:T(8,128)}, f32[8,128]{1,0:T(8,128)}, f32[8,32]{1,0:T(8,128)}) custom-call(f32[8,384]{1,0:T(8,128)} %shard_map.129.sums_ref), custom_call_target="tpu_custom_call" | custom-call | tf_op jit(solution)/shard_map/pallas_call | solution.py:798

commit v5 on v4

--- a/solution.py
+++ b/solution.py
@@ -306,15 +306,23 @@
     remote(src, src, sem, sem, dev).wait_send()
 
 
+FAR4 = (2, 1, 3)
+FAR8 = (4, 3, 5, 2, 6, 1, 7)
+
+
+def far_first():
+    offsets = [(dy, dz) for dy in range(NY) for dz in range(NZ) if dy or dz]
+    return sorted(offsets, key=lambda o: -(min(o[0], NY - o[0]) + min(o[1], NZ - o[1])))
+
+
 def enter():
     x, y, z, k, chip = place()
     s = 2 * chip + k
     seq = CHIPS * 2
-    partners = [device(x, y, z, 1 - k)]
-    partners += [device(lax.rem(x + d, NX), y, z, k) for d in range(1, NX)]
-    partners += [device(x, lax.rem(y + d, NY), z, k) for d in range(1, NY)]
-    partners += [device(x, y, lax.rem(z + d, NZ), k) for d in range(1, NZ)]
-    partners += [(x, lax.rem(s + 1, seq)), (x, lax.rem(s + seq - 1, seq))]
+    partners = [device(x, y, lax.rem(z + d, NZ), k) for d in FAR8]
+    partners += [device(lax.rem(x + d, NX), y, z, k) for d in FAR4]
+    partners += [device(x, lax.rem(y + d, NY), z, k) for d in FAR4]
+    partners += [(x, lax.rem(s + 1, seq)), (x, lax.rem(s + seq - 1, seq)), device(x, y, z, 1 - k)]
     barrier = pltpu.get_barrier_semaphore()
     for dev in partners:
         pl.semaphore_signal(barrier, inc=1, device_id=dev, device_id_type=MESH)
@@ -326,7 +334,7 @@
     s = 2 * chip + k
     mate = device(x, y, z, 1 - k)
     own = wbuf.at[x, y, z, k]
-    for d in range(1, NZ):
+    for d in FAR8:
         remote(own, own, s_send.at[0], s_z, device(x, y, lax.rem(z + d, NZ), k)).start()
     halo = remote(
         tok_ref.at[pl.ds(L - HALO, HALO)], ext.at[pl.ds(L, HALO)], s_send.at[4], s_halo,
@@ -349,15 +357,15 @@
     def far(d):
         return lax.rem(x + d * (1 - k), NX), lax.rem(y + d * k, NY)
 
-    for d in range(1, 4):
+    for d in FAR4:
         slab_copy(x, y, *near(d), 1).start()
-    for d in range(1, 4):
+    for d in FAR4:
         slab_copy(x, y, *far(d), 2).start()
     swap(x, y, k).start()
-    for d in range(1, 4):
+    for d in (1, 3, 2):
         sx, sy = near(d)
         slab_copy(sx, sy, x, y, 1).wait_recv()
-        for t in range(1, 4):
+        for t in FAR4:
             slab_copy(sx, sy, *far(t), 2).start()
         swap(sx, sy, k).start()
     halo.wait_recv()
@@ -367,8 +375,8 @@
         ext[L : L + HALO, :] = jnp.zeros((HALO, ext.shape[1]), BF16)
 
     ext_t[:, L:] = ext[L:, :].T
-    for e in range(4):
-        for d in range(1, 4):
+    for e in (0, 1, 3, 2):
+        for d in (1, 3, 2):
             fx, fy = far(d)
             sx = lax.rem(fx + e * k, NX)
             sy = lax.rem(fy + e * (1 - k), NY)
@@ -405,8 +413,8 @@
         self.mate = device(self.x, self.y, self.z, 1 - self.k)
         self.first = self.k == 0
 
-    def peer(self, d):
-        c = lax.rem(self.chip + d, CHIPS)
+    def peer(self, offset):
+        c = lax.rem(self.y + offset[0], NY) * NZ + lax.rem(self.z + offset[1], NZ)
         return c, (self.x, 2 * c + self.k)
 
     def to_mate(self):
@@ -414,14 +422,14 @@
 
     def start_one(self):
         piece = pl.ds(0, self.rows)
-        for d in range(1, CHIPS):
-            c, dev = self.peer(d)
+        for offset in far_first():
+            c, dev = self.peer(offset)
             remote(self.snd.at[c, piece], self.rcv.at[self.chip, piece], self.s_send.at[1], self.s_one, dev).start()
         self.rcv[self.chip] = self.snd[self.chip]
 
     def start_two(self):
-        for d in range(1, CHIPS):
-            c, dev = self.peer(d)
+        for offset in far_first():
+            c, dev = self.peer(offset)
             remote(self.snd2.at[c], self.rcv2.at[self.chip], self.s_send.at[2], self.s_two, dev).start()
         self.rcv2[self.chip] = self.snd2[self.chip]
 
@@ -503,20 +511,22 @@
     low_half = iota((8, 128), 1) < 64
     block_rows = NY * NZ * 16
 
+    order = FAR4 + (0,)
+
     def settle(i):
-        xb = lax.rem(x + 1 + i, NX)
+        xb = lax.rem(x + order[i], NX)
         arrived(m01.at[:, xb], s_mate.at[i], mate)
         a0[xb] = full[0, xb, :, :, k] + m01[0, xb]
         if i < NX - 1:
-            remote(a0.at[xb], r0.at[i], s_send.at[2], s_a.at[0], x_to(1 + i)).start()
+            remote(a0.at[xb], r0.at[i], s_send.at[2], s_a.at[0], x_to(order[i])).start()
         a1[xb] = full[1, xb, :, :, k] + m01[1, xb]
-        for d in range(1, NY):
+        for d in FAR4:
             remote(a1.at[xb, lax.rem(y + d, NY)], r1.at[d - 1, xb], s_send.at[3], s_a.at[1], y_to(d)).start()
         arrived(m2.at[xb], s_mate.at[NX + i], mate)
         a2[xb] = g2[k, xb] + m2[xb]
 
     for i in range(NX):
-        xb = lax.rem(x + 1 + i, NX)
+        xb = lax.rem(x + order[i], NX)
         rows = ext_t[pl.ds(pl.multiple_of(xb * block_rows, block_rows), block_rows), :]
         part = dg(rows, high, 1, 0) + dg(rows, low, 1, 0)
         full[0, xb] = part[:, 0:128].reshape(NY, NZ, 2, 8, 128)
@@ -540,11 +550,11 @@
 
     arrived(r0, s_a.at[0], mate)
     b0[...] = (a0[x] + r0[0]) + (r0[1] + r0[2])
-    for d in range(1, NY):
+    for d in FAR4:
         remote(b0.at[lax.rem(y + d, NY)], q0.at[d - 1], s_send.at[8], s_b.at[0], y_to(d)).start()
     arrived(r1, s_a.at[1], mate)
     b1[...] = (a1[:, y] + r1[0]) + (r1[1] + r1[2])
-    for d in range(1, NZ):
+    for d in FAR8:
         remote(b1.at[:, lax.rem(z + d, NZ)], q1.at[d - 1], s_send.at[9], s_b.at[1], z_to(d)).start()
 
     @pl.when(holder)
@@ -552,24 +562,24 @@
         arrived(r2.at[pl.ds(1, NZ - 1)], s_a.at[2], mate)
         total = a2[:, :, z // 2] + ((r2[1] + r2[2]) + (r2[3] + r2[4]))
         b2[...] = total + ((r2[5] + r2[6]) + r2[7])
-        for d in range(1, NX):
+        for d in FAR4:
             remote(b2.at[lax.rem(x + d, NX)], q2.at[d - 1], s_send.at[10], s_b.at[2], x_to(d)).start()
 
     arrived(q0, s_b.at[0], mate)
     c0[...] = (b0[y] + q0[0]) + (q0[1] + q0[2])
-    for d in range(1, NZ):
+    for d in FAR8:
         remote(c0.at[lax.rem(z + d, NZ)], p0.at[d - 1], s_send.at[11], s_c.at[0], z_to(d)).start()
 
     @pl.when(holder)
     def _():
         arrived(q2, s_b.at[2], mate)
         c2[...] = (b2[x] + q2[0]) + (q2[1] + q2[2])
-        for d in range(1, NY):
+        for d in FAR4:
             remote(c2.at[lax.rem(y + d, NY)], p2.at[d - 1], s_send.at[12], s_c.at[2], y_to(d)).start()
 
     arrived(q1, s_b.at[1], mate)
     c1[...] = b1[:, z] + ((q1[0] + q1[1]) + (q1[2] + q1[3])) + ((q1[4] + q1[5]) + q1[6])
-    for d in range(1, NX):
+    for d in FAR4:
         remote(c1.at[lax.rem(x + d, NX)], p1.at[d - 1], s_send.at[13], s_c.at[1], x_to(d)).start()
     last = remote(e2, f2, s_send.at[14], s_e, mate)
 

time: 83.5 us -> 82.1 us (0.983)
  Pallas kernels: 82.7 us -> 81.2 us
    pallas_call x1, Pallas kernels: 81.3 us -> 79.9 us  [body(): pl.pallas_call(functools.partial(everything, scale), out_shape=jax.ShapeD...]
where the time goes in v5:
time: 82.1 us; the launch traced here: 81.9 us
  Pallas kernels  81.2 us (99%)
    pallas_call x1, Pallas kernels, body(): pl.pallas_call(functools.partial(everything, scale), out_shape=jax.ShapeD...  79.9 us

profile of v5, /device:TPU:1, one launch (start us, length us, event | category | flops | bytes accessed | tf_op | source)
XLA Modules:
  0.0 81.9 jit_solution(13797706123904827379)
XLA Ops:
  0.6 79.9 %shard_map.129.sums_ref = f32[8,384]{1,0:T(8,128)} custom-call(bf16[8,128]{1,0:T(8,128)(2,1)} %sw_hbm.1, bf16[8,128]{1,0:T(8,128)(2,1)} %sd_hbm.1, bf16[8,32]{1,0:T(8,128)(2,1)} %tw_hbm.1, bf16[8,32]{1,0:T(8,128)(2,1)} %td_hbm.1, bf16[128,2048]{1,0:T(8,128)(2,1)} %bitcast.5, bf16[128,1024]{1,0:T(8,128)(2,1)} %bitcast.6, bf16[128,1024]{1,0:T(8,128)(2,1)} %bitcast.7, ...), custom_call_target="tpu_custom_call" | custom-call | tf_op jit(solution)/shard_map/pallas_call | solution.py:798
  80.5 1.4 %shard_map.130 = (f32[8,128]{1,0:T(8,128)}, f32[8,32]{1,0:T(8,128)}, f32[8,128]{1,0:T(8,128)}, f32[8,32]{1,0:T(8,128)}) custom-call(f32[8,384]{1,0:T(8,128)} %shard_map.129.sums_ref), custom_call_target="tpu_custom_call" | custom-call | tf_op jit(solution)/shard_map/pallas_call | solution.py:808

commit v6 on v5

--- a/solution.py
+++ b/solution.py
@@ -307,12 +307,8 @@
 
 
 FAR4 = (2, 1, 3)
+LANES = HALF // 128
 FAR8 = (4, 3, 5, 2, 6, 1, 7)
-
-
-def far_first():
-    offsets = [(dy, dz) for dy in range(NY) for dz in range(NZ) if dy or dz]
-    return sorted(offsets, key=lambda o: -(min(o[0], NY - o[0]) + min(o[1], NZ - o[1])))
 
 
 def enter():
@@ -405,90 +401,114 @@
 
 
 class Half:
-    def __init__(self, loc, part, snd, rcv, snd2, rcv2, other, st, rows, s_send, s_mate, s_one, s_two):
-        self.loc, self.part, self.snd, self.rcv, self.snd2, self.rcv2 = loc, part, snd, rcv, snd2, rcv2
-        self.other, self.st, self.rows = other, st, rows
-        self.s_send, self.s_mate, self.s_one, self.s_two = s_send, s_mate, s_one, s_two
+    def __init__(self, loc, part, snd, rcv, tot, tots, snd2, rcv2, other, st, decays, s_send, s_mate, s_one, s_row, s_two):
+        self.loc, self.part, self.snd, self.rcv, self.tot, self.tots = loc, part, snd, rcv, tot, tots
+        self.snd2, self.rcv2, self.other, self.st = snd2, rcv2, other, st
+        self.reverse = decays is not None
+        self.decays = decays if self.reverse else self
+        self.rows = pl.ds(0, 16 if self.reverse else 18)
+        self.s_send, self.s_mate, self.s_one, self.s_row, self.s_two = s_send, s_mate, s_one, s_row, s_two
         self.x, self.y, self.z, self.k, self.chip = place()
         self.mate = device(self.x, self.y, self.z, 1 - self.k)
         self.first = self.k == 0
 
-    def peer(self, offset):
-        c = lax.rem(self.y + offset[0], NY) * NZ + lax.rem(self.z + offset[1], NZ)
-        return c, (self.x, 2 * c + self.k)
-
     def to_mate(self):
         return remote(self.loc.at[1 - self.k], self.part, self.s_send.at[0], self.s_mate.at[0], self.mate)
 
-    def start_one(self):
-        piece = pl.ds(0, self.rows)
-        for offset in far_first():
-            c, dev = self.peer(offset)
-            remote(self.snd.at[c, piece], self.rcv.at[self.chip, piece], self.s_send.at[1], self.s_one, dev).start()
-        self.rcv[self.chip] = self.snd[self.chip]
-
-    def start_two(self):
-        for offset in far_first():
-            c, dev = self.peer(offset)
-            remote(self.snd2.at[c], self.rcv2.at[self.chip], self.s_send.at[2], self.s_two, dev).start()
-        self.rcv2[self.chip] = self.snd2[self.chip]
-
-    def wait_one(self):
-        arrived(self.rcv.at[pl.ds(0, CHIPS - 1), pl.ds(0, self.rows)], self.s_one, self.mate)
-
-    def wait_two(self):
-        arrived(self.rcv2.at[pl.ds(0, CHIPS - 1)], self.s_two, self.mate)
-
     def back(self):
-        return remote(self.other, self.st.at[self.k], self.s_send.at[3], self.s_mate.at[1], self.mate)
+        return remote(self.other, self.st.at[self.k], self.s_send.at[4], self.s_mate.at[1], self.mate)
 
     def back_in(self):
-        return remote(self.other, self.st.at[1 - self.k], self.s_send.at[3], self.s_mate.at[1], self.mate)
+        return remote(self.other, self.st.at[1 - self.k], self.s_send.at[4], self.s_mate.at[1], self.mate)
 
     def cores(self):
         own, other = self.loc[self.k], self.part[...]
         return jnp.where(self.first, own, other), jnp.where(self.first, other, own)
 
-    def slices(self, s, t, rest):
-        for j in range(CHIPS):
-            rows = slice(8 * (j // 4), 8 * (j // 4) + 8)
-            lanes = slice(128 * (j % 4), 128 * (j % 4) + 128)
-            self.snd[j, 0:8] = s[rows, lanes]
-            self.snd[j, 8:16] = t[rows, lanes]
-            for i, row in enumerate(rest):
-                self.snd[j, 16 + i : 17 + i] = row[:, lanes]
-
-    def prefix(self, order, decays):
-        s = t = jnp.zeros((8, 128), F32)
-        for c in order:
-            self.snd2[c, 0:8] = s
-            self.snd2[c, 8:16] = t
-            a, ad = decays[c, 16:17, :], decays[c, 17:18, :]
-            s, t = a * s + self.rcv[c, 0:8], a * t + (ad * s + self.rcv[c, 8:16])
+    def start_one(self, s, t, a, ad):
+        for j in range(NZ):
+            rows = slice(8 * j, 8 * j + 8)
+            for i in range(LANES):
+                lanes = slice(128 * i, 128 * i + 128)
+                self.snd[j, i, 0:8] = s[rows, lanes]
+                self.snd[j, i, 8:16] = t[rows, lanes]
+                if not self.reverse:
+                    self.snd[j, i, 16:17] = a[:, lanes]
+                    self.snd[j, i, 17:18] = ad[:, lanes]
+        for d in FAR8:
+            c = lax.rem(self.z + d, NZ)
+            dev = device(self.x, self.y, c, self.k)
+            remote(self.snd.at[c, :, self.rows], self.rcv.at[self.z, :, self.rows], self.s_send.at[1], self.s_one, dev).start()
+        self.rcv[self.z] = self.snd[self.z]
+
+    def wait_one(self):
+        arrived(self.rcv.at[pl.ds(0, NZ - 1), :, self.rows], self.s_one, self.mate)
+
+    @staticmethod
+    def step(carry, ref, decays, c):
+        s, t = carry
+        a, ad = decays[c, :, 16:17, :], decays[c, :, 17:18, :]
+        return a * s + ref[c, :, 0:8, :], a * t + (ad * s + ref[c, :, 8:16, :])
+
+    def order(self, count):
+        return range(count - 1, -1, -1) if self.reverse else range(count)
+
+    def row_total(self):
+        carry = (jnp.zeros((LANES, 8, 128), F32),) * 2
+        for c in self.order(NZ):
+            carry = self.step(carry, self.rcv, self.decays.rcv, c)
+        self.tot[:, 0:8, :], self.tot[:, 8:16, :] = carry
+        if not self.reverse:
+            a, ad = self.rcv[0, :, 16:17, :], self.rcv[0, :, 17:18, :]
+            for c in range(1, NZ):
+                b, bd = self.rcv[c, :, 16:17, :], self.rcv[c, :, 17:18, :]
+                a, ad = a * b, ad * b + a * bd
+            self.tot[:, 16:17, :], self.tot[:, 17:18, :] = a, ad
+        for d in FAR4:
+            dev = device(self.x, lax.rem(self.y + d, NY), self.z, self.k)
+            remote(self.tot.at[:, self.rows], self.tots.at[self.y, :, self.rows], self.s_send.at[2], self.s_row, dev).start()
+        self.tots[self.y] = self.tot[...]
+
+    def start_two(self):
+        arrived(self.tots.at[pl.ds(0, NY - 1), :, self.rows], self.s_row, self.mate)
+        carry = (jnp.zeros((LANES, 8, 128), F32),) * 2
+        for row in self.order(NY):
+            after = self.step(carry, self.tots, self.decays.tots, row)
+            ahead = (row > self.y) if self.reverse else (row < self.y)
+            carry = tuple(jnp.where(ahead, new, old) for new, old in zip(after, carry))
+        for c in self.order(NZ):
+            self.snd2[c, :, 0:8, :], self.snd2[c, :, 8:16, :] = carry
+            carry = self.step(carry, self.rcv, self.decays.rcv, c)
+        for d in FAR8:
+            c = lax.rem(self.z + d, NZ)
+            dev = device(self.x, self.y, c, self.k)
+            remote(self.snd2.at[c], self.rcv2.at[self.z], self.s_send.at[3], self.s_two, dev).start()
+        self.rcv2[self.z] = self.snd2[self.z]
+
+    def wait_two(self):
+        arrived(self.rcv2.at[pl.ds(0, NZ - 1)], self.s_two, self.mate)
 
     def assemble(self, a, ad, base, base_first):
-        for j in range(CHIPS):
-            row = 8 * (j // 4)
-            lanes = slice(128 * (j % 4), 128 * (j % 4) + 128)
-            self.place_slice(row, lanes, j)
-        s, t = self.other[0:64, :], self.other[64:128, :]
+        s, t = (
+            jnp.concatenate(
+                [jnp.concatenate([self.rcv2[j, i, rows] for j in range(NZ)], 0) for i in range(LANES)], 1
+            )
+            for rows in (slice(0, 8), slice(8, 16))
+        )
         next_s = a * s + base[0:64]
         next_t = a * t + ad * s + base[64:128]
         mine_is_base = self.first if base_first else jnp.logical_not(self.first)
-        self.st[self.k, 0:64, :] = jnp.where(mine_is_base, s, next_s)
-        self.st[self.k, 64:128, :] = jnp.where(mine_is_base, t, next_t)
         self.other[0:64, :] = jnp.where(mine_is_base, next_s, s)
         self.other[64:128, :] = jnp.where(mine_is_base, next_t, t)
         self.back().start()
-
-    def place_slice(self, row, lanes, j):
-        self.other[row : row + 8, lanes] = self.rcv2[j, 0:8]
-        self.other[64 + row : 72 + row, lanes] = self.rcv2[j, 8:16]
+        self.st[self.k, 0:64, :] = jnp.where(mine_is_base, s, next_s)
+        self.st[self.k, 64:128, :] = jnp.where(mine_is_base, t, next_t)
 
     def drain(self):
         self.to_mate().wait_send()
-        sent(self.snd.at[pl.ds(0, CHIPS - 1), pl.ds(0, self.rows)], self.s_send.at[1], self.mate)
-        sent(self.snd2.at[pl.ds(0, CHIPS - 1)], self.s_send.at[2], self.mate)
+        sent(self.snd.at[pl.ds(0, NZ - 1), :, self.rows], self.s_send.at[1], self.mate)
+        sent(self.tots.at[pl.ds(0, NY - 1), :, self.rows], self.s_send.at[2], self.mate)
+        sent(self.snd2.at[pl.ds(0, NZ - 1)], self.s_send.at[3], self.mate)
         self.back().wait_send()
 
 
@@ -652,8 +672,8 @@
     wts = weights_of(ft)
     pp = pair_parts(ft)
     we, wde, es, eds, eu, edu = streams(wts, v_ref[...], u_ref[...])
-    fw = Half(*forward_scratch, 18, *forward_sems)
-    bw = Half(*backward_scratch, 16, *backward_sems)
+    fw = Half(*forward_scratch, None, *forward_sems)
+    bw = Half(*backward_scratch, fw, *backward_sems)
     row = iota((8, HP), 0)
     dec = jnp.where(row == 0, es[L - 1 :, :], jnp.where(row == 1, eds[L - 1 :, :], 0.0))
     states = forward_states(pp, we, wde)
@@ -671,16 +691,15 @@
     one0, one1 = fw.cores()
     a0, ad0 = one0[128:129], one0[129:130]
     a1, ad1 = one1[128:129], one1[129:130]
-    fw.slices(
-        a1 * one0[0:64] + one1[0:64],
-        a1 * one0[64:128] + ad1 * one0[0:64] + one1[64:128],
-        [a0 * a1, ad0 * a1 + a0 * ad1],
-    )
-    fw.start_one()
+    a, ad = a0 * a1, ad0 * a1 + a0 * ad1
+    fw.start_one(
+        a1 * one0[0:64] + one1[0:64], a1 * one0[64:128] + ad1 * one0[0:64] + one1[64:128], a, ad
+    )
     bw.to_mate().wait_recv()
     one0, one1 = bw.cores()
-    bw.slices(a0 * one1[0:64] + one0[0:64], a0 * one1[64:128] + ad0 * one1[0:64] + one0[64:128], [])
-    bw.start_one()
+    bw.start_one(
+        a0 * one1[0:64] + one0[0:64], a0 * one1[64:128] + ad0 * one1[0:64] + one0[64:128], a, ad
+    )
 
     def tile(ref):
         return lambda i: ref[:, pl.ds(pl.multiple_of(i * 128, 128), 128)]
@@ -693,13 +712,14 @@
             ft, g, gd, tile(v_ref), tile(u_ref), rows_ref, row1_ref, row2_ref, colq_ref, colqd_ref, first, last, carry
         )
 
-    carry = block_terms(0, 6, (zero, zero))
+    carry = block_terms(0, 4, (zero, zero))
     fw.wait_one()
-    fw.prefix(range(CHIPS), fw.rcv)
+    fw.row_total()
+    carry = block_terms(4, 6, carry)
+    bw.wait_one()
+    bw.row_total()
     fw.start_two()
     carry = block_terms(6, 8, carry)
-    bw.wait_one()
-    bw.prefix(range(CHIPS - 1, -1, -1), fw.rcv)
     bw.start_two()
     pairs = intra_pairs(pp, *carry)
     fw.wait_two()
@@ -776,8 +796,11 @@
         + [vmem((8, 128)), vmem((8, 128))]
     )
 
-    def scan_scratch(piece):
-        return [vmem((CHIPS, piece, 128))] * 2 + [vmem((CHIPS, 16, 128))] * 2 + [vmem((128, HALF)), vmem((2, 128, HALF))]
+    def scan_scratch():
+        return (
+            [vmem((NZ, LANES, 24, 128))] * 2 + [vmem((LANES, 24, 128)), vmem((NY, LANES, 24, 128))]
+            + [vmem((NZ, LANES, 16, 128))] * 2 + [vmem((128, HALF)), vmem((2, 128, HALF))]
+        )
 
     scratch = [
         vmem((L, HP), BF16), vmem((L, HP), BF16),
@@ -785,14 +808,14 @@
         vmem((KCONV, 128)), vmem((1, H)), vmem((1, H)),
         vmem((NX, NY, NZ, 2, rows, WIDE), BF16),
         vmem((2 * L, depth), BF16), vmem((depth, 2 * L), BF16), vmem((HALO + L, WIDE)),
-        [vmem((2, 136, HALF)), vmem((136, HALF))] + scan_scratch(24),
-        [vmem((2, 128, HALF)), vmem((128, HALF))] + scan_scratch(16),
+        [vmem((2, 136, HALF)), vmem((136, HALF))] + scan_scratch(),
+        [vmem((2, 128, HALF)), vmem((128, HALF))] + scan_scratch(),
         vmem((3 * H, L)), vmem((L, L)), vmem((L, L)), vmem((H, L)), vmem((H, L)), vmem((HALO + L + 8, 256)),
         reduce_scratch,
         dma(10),
         [dma(5), dma(), dma(), dma(NX * NY), dma(NX * NY)],
-        [dma(4), dma(2), dma(), dma()],
-        [dma(4), dma(2), dma(), dma()],
+        [dma(5), dma(2), dma(), dma(), dma()],
+        [dma(5), dma(2), dma(), dma(), dma()],
         [dma(15), dma(2 * NX), dma(3), dma(3), dma(3), dma()],
     ]
     sums = pl.pallas_call(

time: 82.1 us -> 84.6 us (1.030); the launches traced: 81.9 us -> 83.3 us
  Pallas kernels: 81.2 us -> 82.6 us
    pallas_call x1, Pallas kernels: 79.9 us -> 81.3 us  [body(): pl.pallas_call(functools.partial(everything, scale), out_shape=jax.ShapeD...]
where the time goes in v6:
time: 84.6 us; the launch traced here: 83.3 us
  Pallas kernels  82.6 us (98%)
    pallas_call x1, Pallas kernels, body(): pl.pallas_call(functools.partial(everything, scale), out_shape=jax.ShapeD...  81.3 us

profile of v6, /device:TPU:1, one launch (start us, length us, event | category | flops | bytes accessed | tf_op | source)
XLA Modules:
  0.0 83.3 jit_solution(3448382953313076344)
XLA Ops:
  0.6 81.3 %shard_map.129.sums_ref = f32[8,384]{1,0:T(8,128)} custom-call(bf16[8,128]{1,0:T(8,128)(2,1)} %sw_hbm.1, bf16[8,128]{1,0:T(8,128)(2,1)} %sd_hbm.1, bf16[8,32]{1,0:T(8,128)(2,1)} %tw_hbm.1, bf16[8,32]{1,0:T(8,128)(2,1)} %td_hbm.1, bf16[128,2048]{1,0:T(8,128)(2,1)} %bitcast.5, bf16[128,1024]{1,0:T(8,128)(2,1)} %bitcast.6, bf16[128,1024]{1,0:T(8,128)(2,1)} %bitcast.7, ...), custom_call_target="tpu_custom_call" | custom-call | tf_op jit(solution)/shard_map/pallas_call | solution.py:821
  81.9 1.4 %shard_map.130 = (f32[8,128]{1,0:T(8,128)}, f32[8,32]{1,0:T(8,128)}, f32[8,128]{1,0:T(8,128)}, f32[8,32]{1,0:T(8,128)}) custom-call(f32[8,384]{1,0:T(8,128)} %shard_map.129.sums_ref), custom_call_target="tpu_custom_call" | custom-call | tf_op jit(solution)/shard_map/pallas_call | solution.py:831

commit v7 on v6

--- a/solution.py
+++ b/solution.py
@@ -48,8 +48,11 @@
 
 
 def dot_split(a, b, ca, cb):
-    ah, al = split(a)
-    bh, bl = split(b)
+    return dot_parts(split(a), split(b), ca, cb)
+
+
+def dot_parts(a, b, ca, cb):
+    (ah, al), (bh, bl) = a, b
     return dg(ah, bh, ca, cb) + (dg(ah, bl, ca, cb) + dg(al, bh, ca, cb))
 
 
@@ -230,16 +233,18 @@
     return dot_left(x, head_spread(), 1, 1)
 
 
-def finish_forward(pp, eu, edu, cotangent, xf):
+def finish_forward(pp, e_split, cotangent, xf):
     u = cotangent.astype(F32)
-    zz = dot_split(jnp.concatenate([pp["c_o"], pp["cd_c"]], 0), xf, 1, 0)
-    return head_sums(zz[:L] * u), head_sums(zz[L:] * u), dot_split(jnp.concatenate([eu, edu], 0), xf, 1, 1)
-
-
-def finish_backward(pp, we, wde, values, xb):
+    x_split = split(xf)
+    zz = dot_parts(split(jnp.concatenate([pp["c_o"], pp["cd_c"]], 0)), x_split, 1, 0)
+    return head_sums(zz[:L] * u), head_sums(zz[L:] * u), dot_parts(e_split, x_split, 1, 1)
+
+
+def finish_backward(pp, w_split, values, xb):
     v = values.astype(F32)
-    yy = dot_split(jnp.concatenate([pp["b_o"], pp["bd_b"]], 0), xb, 1, 0)
-    return head_sums(yy[:L] * v), head_sums(yy[L:] * v), dot_split(jnp.concatenate([we, wde], 0), xb, 1, 1)
+    x_split = split(xb)
+    yy = dot_parts(split(jnp.concatenate([pp["b_o"], pp["bd_b"]], 0)), x_split, 1, 0)
+    return head_sums(yy[:L] * v), head_sums(yy[L:] * v), dot_parts(w_split, x_split, 1, 1)
 
 
 def finish(ft, wts, pairs, row1, row2, colq, colqd, from_forward, from_backward, xf, xb, rate, scale):
@@ -307,7 +312,7 @@
 
 
 FAR4 = (2, 1, 3)
-LANES = HALF // 128
+LANES = HALF // 256
 FAR8 = (4, 3, 5, 2, 6, 1, 7)
 
 
@@ -316,8 +321,9 @@
     s = 2 * chip + k
     seq = CHIPS * 2
     partners = [device(x, y, lax.rem(z + d, NZ), k) for d in FAR8]
-    partners += [device(lax.rem(x + d, NX), y, z, k) for d in FAR4]
-    partners += [device(x, lax.rem(y + d, NY), z, k) for d in FAR4]
+    partners += [
+        device(lax.rem(x + dx, NX), lax.rem(y + dy, NY), z, k) for dx in range(NX) for dy in range(NY) if dx or dy
+    ]
     partners += [(x, lax.rem(s + 1, seq)), (x, lax.rem(s + seq - 1, seq)), device(x, y, z, 1 - k)]
     barrier = pltpu.get_barrier_semaphore()
     for dev in partners:
@@ -339,31 +345,21 @@
     halo.start()
     arrived(wbuf.at[x, y, pl.ds(0, NZ - 1), k], s_z, mate)
 
-    def slab_copy(sx, sy, tx, ty, sem):
+    def slab_copy(sx, sy, tx, ty):
         ref = wbuf.at[sx, sy, :, k]
-        return remote(ref, ref, s_send.at[sem], s_slab.at[sx * NY + sy], device(tx, ty, z, k))
+        return remote(ref, ref, s_send.at[1], s_slab.at[sx * NY + sy], device(tx, ty, z, k))
 
     def swap(sx, sy, kk):
         ref = wbuf.at[sx, sy, :, kk]
         return remote(ref, ref, s_send.at[3], s_swap.at[sx * NY + sy], mate)
 
-    def near(d):
-        return lax.rem(x + d * k, NX), lax.rem(y + d * (1 - k), NY)
-
-    def far(d):
-        return lax.rem(x + d * (1 - k), NX), lax.rem(y + d * k, NY)
-
-    for d in FAR4:
-        slab_copy(x, y, *near(d), 1).start()
-    for d in FAR4:
-        slab_copy(x, y, *far(d), 2).start()
+    def hops(offset):
+        return sum(min(d, 4 - d) for d in offset)
+
+    offsets = sorted([(dx, dy) for dx in range(NX) for dy in range(NY) if dx or dy], key=hops)
+    for dx, dy in offsets[::-1]:
+        slab_copy(x, y, lax.rem(x + dx, NX), lax.rem(y + dy, NY)).start()
     swap(x, y, k).start()
-    for d in (1, 3, 2):
-        sx, sy = near(d)
-        slab_copy(sx, sy, x, y, 1).wait_recv()
-        for t in FAR4:
-            slab_copy(sx, sy, *far(t), 2).start()
-        swap(sx, sy, k).start()
     halo.wait_recv()
 
     @pl.when(s == 0)
@@ -371,13 +367,10 @@
         ext[L : L + HALO, :] = jnp.zeros((HALO, ext.shape[1]), BF16)
 
     ext_t[:, L:] = ext[L:, :].T
-    for e in (0, 1, 3, 2):
-        for d in (1, 3, 2):
-            fx, fy = far(d)
-            sx = lax.rem(fx + e * k, NX)
-            sy = lax.rem(fy + e * (1 - k), NY)
-            slab_copy(sx, sy, x, y, 2).wait_recv()
-            swap(sx, sy, k).start()
+    for dx, dy in offsets:
+        sx, sy = lax.rem(x + dx, NX), lax.rem(y + dy, NY)
+        slab_copy(sx, sy, x, y).wait_recv()
+        swap(sx, sy, k).start()
     depth = ext.shape[1] // NX
     total = jnp.zeros((L + HALO, WIDE), F32)
     for d in range(NX):
@@ -392,8 +385,7 @@
 
     def drain():
         sent(wbuf.at[0, 0, pl.ds(0, NZ - 1), 0], s_send.at[0], mate)
-        sent(wbuf.at[0, pl.ds(0, NY - 1), :, 0], s_send.at[1], mate)
-        sent(wbuf.at[pl.ds(0, NX - 1), :, :, 0], s_send.at[2], mate)
+        sent(wbuf.at[pl.ds(0, 3), :, pl.ds(0, 5)], s_send.at[1], mate)
         sent(wbuf.at[:, :, :, 0], s_send.at[3], mate)
         halo.wait_send()
 
@@ -426,72 +418,78 @@
         return jnp.where(self.first, own, other), jnp.where(self.first, other, own)
 
     def start_one(self, s, t, a, ad):
-        for j in range(NZ):
-            rows = slice(8 * j, 8 * j + 8)
-            for i in range(LANES):
-                lanes = slice(128 * i, 128 * i + 128)
-                self.snd[j, i, 0:8] = s[rows, lanes]
-                self.snd[j, i, 8:16] = t[rows, lanes]
-                if not self.reverse:
-                    self.snd[j, i, 16:17] = a[:, lanes]
-                    self.snd[j, i, 17:18] = ad[:, lanes]
+        for h in range(2):
+            for j in range(NZ):
+                rows = slice(8 * j, 8 * j + 8)
+                for i in range(LANES):
+                    at = 128 * (LANES * h + i)
+                    lanes = slice(at, at + 128)
+                    self.snd[h, j, i, 0:8] = s[rows, lanes]
+                    self.snd[h, j, i, 8:16] = t[rows, lanes]
+                    if not self.reverse:
+                        self.snd[h, j, i, 16:17] = a[:, lanes]
+                        self.snd[h, j, i, 17:18] = ad[:, lanes]
+            for d in FAR8:
+                c = lax.rem(self.z + d, NZ)
+                dev = device(self.x, self.y, c, self.k)
+                remote(
+                    self.snd.at[h, c, :, self.rows], self.rcv.at[h, self.z, :, self.rows],
+                    self.s_send.at[1], self.s_one.at[h], dev,
+                ).start()
+            self.rcv[h, self.z] = self.snd[h, self.z]
+
+    @staticmethod
+    def step(carry, ref, decays, c):
+        s, t = carry
+        a, ad = decays[*c, :, 16:17, :], decays[*c, :, 17:18, :]
+        return a * s + ref[*c, :, 0:8, :], a * t + (ad * s + ref[*c, :, 8:16, :])
+
+    def order(self, count):
+        return range(count - 1, -1, -1) if self.reverse else range(count)
+
+    def row_total(self, h):
+        arrived(self.rcv.at[h, pl.ds(0, NZ - 1), :, self.rows], self.s_one.at[h], self.mate)
+        carry = (jnp.zeros((LANES, 8, 128), F32),) * 2
+        for c in self.order(NZ):
+            carry = self.step(carry, self.rcv, self.decays.rcv, (h, c))
+        self.tot[h, :, 0:8, :], self.tot[h, :, 8:16, :] = carry
+        if not self.reverse:
+            a, ad = self.rcv[h, 0, :, 16:17, :], self.rcv[h, 0, :, 17:18, :]
+            for c in range(1, NZ):
+                b, bd = self.rcv[h, c, :, 16:17, :], self.rcv[h, c, :, 17:18, :]
+                a, ad = a * b, ad * b + a * bd
+            self.tot[h, :, 16:17, :], self.tot[h, :, 17:18, :] = a, ad
+        for d in FAR4:
+            dev = device(self.x, lax.rem(self.y + d, NY), self.z, self.k)
+            remote(
+                self.tot.at[h, :, self.rows], self.tots.at[h, self.y, :, self.rows],
+                self.s_send.at[2], self.s_row.at[h], dev,
+            ).start()
+        self.tots[h, self.y] = self.tot[h]
+
+    def start_two(self, h):
+        arrived(self.tots.at[h, pl.ds(0, NY - 1), :, self.rows], self.s_row.at[h], self.mate)
+        carry = (jnp.zeros((LANES, 8, 128), F32),) * 2
+        for row in self.order(NY):
+            after = self.step(carry, self.tots, self.decays.tots, (h, row))
+            ahead = (row > self.y) if self.reverse else (row < self.y)
+            carry = tuple(jnp.where(ahead, new, old) for new, old in zip(after, carry))
+        for c in self.order(NZ):
+            self.snd2[h, c, :, 0:8, :], self.snd2[h, c, :, 8:16, :] = carry
+            carry = self.step(carry, self.rcv, self.decays.rcv, (h, c))
         for d in FAR8:
             c = lax.rem(self.z + d, NZ)
             dev = device(self.x, self.y, c, self.k)
-            remote(self.snd.at[c, :, self.rows], self.rcv.at[self.z, :, self.rows], self.s_send.at[1], self.s_one, dev).start()
-        self.rcv[self.z] = self.snd[self.z]
-
-    def wait_one(self):
-        arrived(self.rcv.at[pl.ds(0, NZ - 1), :, self.rows], self.s_one, self.mate)
-
-    @staticmethod
-    def step(carry, ref, decays, c):
-        s, t = carry
-        a, ad = decays[c, :, 16:17, :], decays[c, :, 17:18, :]
-        return a * s + ref[c, :, 0:8, :], a * t + (ad * s + ref[c, :, 8:16, :])
-
-    def order(self, count):
-        return range(count - 1, -1, -1) if self.reverse else range(count)
-
-    def row_total(self):
-        carry = (jnp.zeros((LANES, 8, 128), F32),) * 2
-        for c in self.order(NZ):
-            carry = self.step(carry, self.rcv, self.decays.rcv, c)
-        self.tot[:, 0:8, :], self.tot[:, 8:16, :] = carry
-        if not self.reverse:
-            a, ad = self.rcv[0, :, 16:17, :], self.rcv[0, :, 17:18, :]
-            for c in range(1, NZ):
-                b, bd = self.rcv[c, :, 16:17, :], self.rcv[c, :, 17:18, :]
-                a, ad = a * b, ad * b + a * bd
-            self.tot[:, 16:17, :], self.tot[:, 17:18, :] = a, ad
-        for d in FAR4:
-            dev = device(self.x, lax.rem(self.y + d, NY), self.z, self.k)
-            remote(self.tot.at[:, self.rows], self.tots.at[self.y, :, self.rows], self.s_send.at[2], self.s_row, dev).start()
-        self.tots[self.y] = self.tot[...]
-
-    def start_two(self):
-        arrived(self.tots.at[pl.ds(0, NY - 1), :, self.rows], self.s_row, self.mate)
-        carry = (jnp.zeros((LANES, 8, 128), F32),) * 2
-        for row in self.order(NY):
-            after = self.step(carry, self.tots, self.decays.tots, row)
-            ahead = (row > self.y) if self.reverse else (row < self.y)
-            carry = tuple(jnp.where(ahead, new, old) for new, old in zip(after, carry))
-        for c in self.order(NZ):
-            self.snd2[c, :, 0:8, :], self.snd2[c, :, 8:16, :] = carry
-            carry = self.step(carry, self.rcv, self.decays.rcv, c)
-        for d in FAR8:
-            c = lax.rem(self.z + d, NZ)
-            dev = device(self.x, self.y, c, self.k)
-            remote(self.snd2.at[c], self.rcv2.at[self.z], self.s_send.at[3], self.s_two, dev).start()
-        self.rcv2[self.z] = self.snd2[self.z]
-
-    def wait_two(self):
-        arrived(self.rcv2.at[pl.ds(0, NZ - 1)], self.s_two, self.mate)
+            remote(self.snd2.at[h, c], self.rcv2.at[h, self.z], self.s_send.at[3], self.s_two.at[h], dev).start()
+        self.rcv2[h, self.z] = self.snd2[h, self.z]
+
+    def wait_two(self, h):
+        arrived(self.rcv2.at[h, pl.ds(0, NZ - 1)], self.s_two.at[h], self.mate)
 
     def assemble(self, a, ad, base, base_first):
         s, t = (
             jnp.concatenate(
-                [jnp.concatenate([self.rcv2[j, i, rows] for j in range(NZ)], 0) for i in range(LANES)], 1
+                [jnp.concatenate([self.rcv2[i // LANES, j, i % LANES, rows] for j in range(NZ)], 0) for i in range(2 * LANES)], 1
             )
             for rows in (slice(0, 8), slice(8, 16))
         )
@@ -506,9 +504,9 @@
 
     def drain(self):
         self.to_mate().wait_send()
-        sent(self.snd.at[pl.ds(0, NZ - 1), :, self.rows], self.s_send.at[1], self.mate)
-        sent(self.tots.at[pl.ds(0, NY - 1), :, self.rows], self.s_send.at[2], self.mate)
-        sent(self.snd2.at[pl.ds(0, NZ - 1)], self.s_send.at[3], self.mate)
+        sent(self.snd.at[:, pl.ds(0, NZ - 1), :, self.rows], self.s_send.at[1], self.mate)
+        sent(self.tots.at[:, pl.ds(0, NY - 1), :, self.rows], self.s_send.at[2], self.mate)
+        sent(self.snd2.at[:, pl.ds(0, NZ - 1)], self.s_send.at[3], self.mate)
         self.back().wait_send()
 
 
@@ -712,26 +710,31 @@
             ft, g, gd, tile(v_ref), tile(u_ref), rows_ref, row1_ref, row2_ref, colq_ref, colqd_ref, first, last, carry
         )
 
-    carry = block_terms(0, 4, (zero, zero))
-    fw.wait_one()
-    fw.row_total()
-    carry = block_terms(4, 6, carry)
-    bw.wait_one()
-    bw.row_total()
-    fw.start_two()
-    carry = block_terms(6, 8, carry)
-    bw.start_two()
+    carry = block_terms(0, 7, (zero, zero))
+    fw.row_total(0)
+    carry = block_terms(7, 8, carry)
+    fw.row_total(1)
+    fw.start_two(0)
+    bw.row_total(0)
+    fw.start_two(1)
+    bw.row_total(1)
+    bw.start_two(0)
     pairs = intra_pairs(pp, *carry)
-    fw.wait_two()
+    bw.start_two(1)
+    e_split = split(jnp.concatenate([eu, edu], 0))
+    w_split = split(jnp.concatenate([we, wde], 0))
+    fw.wait_two(0)
+    fw.wait_two(1)
     fw.assemble(a0, ad0, fw.cores()[0], True)
     fw.back_in().wait_recv()
     xf = jnp.concatenate([fw.st[0], fw.st[1]], 1)
-    from_forward = finish_forward(pp, eu, edu, u_ref[...], xf)
-    bw.wait_two()
+    from_forward = finish_forward(pp, e_split, u_ref[...], xf)
+    bw.wait_two(0)
+    bw.wait_two(1)
     bw.assemble(a1, ad1, bw.cores()[1], False)
     bw.back_in().wait_recv()
     xb = jnp.concatenate([bw.st[0], bw.st[1]], 1)
-    from_backward = finish_backward(pp, we, wde, v_ref[...], xb)
+    from_backward = finish_backward(pp, w_split, v_ref[...], xb)
     dz, dzd, dq, dqd = finish(
         ft, wts, pairs, row1_ref[...], row2_ref[...], colq_ref[...], colqd_ref[...],
         from_forward, from_backward, xf, xb, rate, scale,
@@ -798,8 +801,8 @@
 
     def scan_scratch():
         return (
-            [vmem((NZ, LANES, 24, 128))] * 2 + [vmem((LANES, 24, 128)), vmem((NY, LANES, 24, 128))]
-            + [vmem((NZ, LANES, 16, 128))] * 2 + [vmem((128, HALF)), vmem((2, 128, HALF))]
+            [vmem((2, NZ, LANES, 24, 128))] * 2 + [vmem((2, LANES, 24, 128)), vmem((2, NY, LANES, 24, 128))]
+            + [vmem((2, NZ, LANES, 16, 128))] * 2 + [vmem((128, HALF)), vmem((2, 128, HALF))]
         )
 
     scratch = [
@@ -814,8 +817,8 @@
         reduce_scratch,
         dma(10),
         [dma(5), dma(), dma(), dma(NX * NY), dma(NX * NY)],
-        [dma(5), dma(2), dma(), dma(), dma()],
-        [dma(5), dma(2), dma(), dma(), dma()],
+        [dma(5), dma(2), dma(2), dma(2), dma(2)],
+        [dma(5), dma(2), dma(2), dma(2), dma(2)],
         [dma(15), dma(2 * NX), dma(3), dma(3), dma(3), dma()],
     ]
     sums = pl.pallas_call(

time: 84.6 us -> 81.2 us (0.960); the launches traced: 83.3 us -> 80.9 us
  Pallas kernels: 82.6 us -> 80.3 us
    pallas_call x1, Pallas kernels: 81.3 us -> 78.9 us  [body(): pl.pallas_call(functools.partial(everything, scale), out_shape=jax.ShapeD...]
where the time goes in v7:
time: 81.2 us; the launch traced here: 80.9 us
  Pallas kernels  80.3 us (99%)
    pallas_call x1, Pallas kernels, body(): pl.pallas_call(functools.partial(everything, scale), out_shape=jax.ShapeD...  78.9 us

profile of v7, /device:TPU:1, one launch (start us, length us, event | category | flops | bytes accessed | tf_op | source)
XLA Modules:
  0.0 80.9 jit_solution(7719987345079357326)
XLA Ops:
  0.6 78.9 %shard_map.129.sums_ref = f32[8,384]{1,0:T(8,128)} custom-call(bf16[8,128]{1,0:T(8,128)(2,1)} %sw_hbm.1, bf16[8,128]{1,0:T(8,128)(2,1)} %sd_hbm.1, bf16[8,32]{1,0:T(8,128)(2,1)} %tw_hbm.1, bf16[8,32]{1,0:T(8,128)(2,1)} %td_hbm.1, bf16[128,2048]{1,0:T(8,128)(2,1)} %bitcast.5, bf16[128,1024]{1,0:T(8,128)(2,1)} %bitcast.6, bf16[128,1024]{1,0:T(8,128)(2,1)} %bitcast.7, ...), custom_call_target="tpu_custom_call" | custom-call | tf_op jit(solution)/shard_map/pallas_call | solution.py:824
  79.5 1.4 %shard_map.130 = (f32[8,128]{1,0:T(8,128)}, f32[8,32]{1,0:T(8,128)}, f32[8,128]{1,0:T(8,128)}, f32[8,32]{1,0:T(8,128)}) custom-call(f32[8,384]{1,0:T(8,128)} %shard_map.129.sums_ref), custom_call_target="tpu_custom_call" | custom-call | tf_op jit(solution)/shard_map/pallas_call | solution.py:834

commit v8 on v7

--- a/solution.py
+++ b/solution.py
@@ -321,9 +321,8 @@
     s = 2 * chip + k
     seq = CHIPS * 2
     partners = [device(x, y, lax.rem(z + d, NZ), k) for d in FAR8]
-    partners += [
-        device(lax.rem(x + dx, NX), lax.rem(y + dy, NY), z, k) for dx in range(NX) for dy in range(NY) if dx or dy
-    ]
+    partners += [device(lax.rem(x + d, NX), y, z, k) for d in FAR4]
+    partners += [device(x, lax.rem(y + d, NY), z, k) for d in FAR4]
     partners += [(x, lax.rem(s + 1, seq)), (x, lax.rem(s + seq - 1, seq)), device(x, y, z, 1 - k)]
     barrier = pltpu.get_barrier_semaphore()
     for dev in partners:
@@ -345,21 +344,31 @@
     halo.start()
     arrived(wbuf.at[x, y, pl.ds(0, NZ - 1), k], s_z, mate)
 
-    def slab_copy(sx, sy, tx, ty):
+    def slab_copy(sx, sy, tx, ty, sem):
         ref = wbuf.at[sx, sy, :, k]
-        return remote(ref, ref, s_send.at[1], s_slab.at[sx * NY + sy], device(tx, ty, z, k))
+        return remote(ref, ref, s_send.at[sem], s_slab.at[sx * NY + sy], device(tx, ty, z, k))
 
     def swap(sx, sy, kk):
         ref = wbuf.at[sx, sy, :, kk]
         return remote(ref, ref, s_send.at[3], s_swap.at[sx * NY + sy], mate)
 
-    def hops(offset):
-        return sum(min(d, 4 - d) for d in offset)
-
-    offsets = sorted([(dx, dy) for dx in range(NX) for dy in range(NY) if dx or dy], key=hops)
-    for dx, dy in offsets[::-1]:
-        slab_copy(x, y, lax.rem(x + dx, NX), lax.rem(y + dy, NY)).start()
+    def near(d):
+        return lax.rem(x + d * k, NX), lax.rem(y + d * (1 - k), NY)
+
+    def far(d):
+        return lax.rem(x + d * (1 - k), NX), lax.rem(y + d * k, NY)
+
+    for d in FAR4:
+        slab_copy(x, y, *near(d), 1).start()
+    for d in FAR4:
+        slab_copy(x, y, *far(d), 2).start()
     swap(x, y, k).start()
+    for d in (1, 3, 2):
+        sx, sy = near(d)
+        slab_copy(sx, sy, x, y, 1).wait_recv()
+        for t in FAR4:
+            slab_copy(sx, sy, *far(t), 2).start()
+        swap(sx, sy, k).start()
     halo.wait_recv()
 
     @pl.when(s == 0)
@@ -367,10 +376,13 @@
         ext[L : L + HALO, :] = jnp.zeros((HALO, ext.shape[1]), BF16)
 
     ext_t[:, L:] = ext[L:, :].T
-    for dx, dy in offsets:
-        sx, sy = lax.rem(x + dx, NX), lax.rem(y + dy, NY)
-        slab_copy(sx, sy, x, y).wait_recv()
-        swap(sx, sy, k).start()
+    for e in (0, 1, 3, 2):
+        for d in (1, 3, 2):
+            fx, fy = far(d)
+            sx = lax.rem(fx + e * k, NX)
+            sy = lax.rem(fy + e * (1 - k), NY)
+            slab_copy(sx, sy, x, y, 2).wait_recv()
+            swap(sx, sy, k).start()
     depth = ext.shape[1] // NX
     total = jnp.zeros((L + HALO, WIDE), F32)
     for d in range(NX):
@@ -385,7 +397,8 @@
 
     def drain():
         sent(wbuf.at[0, 0, pl.ds(0, NZ - 1), 0], s_send.at[0], mate)
-        sent(wbuf.at[pl.ds(0, 3), :, pl.ds(0, 5)], s_send.at[1], mate)
+        sent(wbuf.at[0, pl.ds(0, NY - 1), :, 0], s_send.at[1], mate)
+        sent(wbuf.at[pl.ds(0, NX - 1), :, :, 0], s_send.at[2], mate)
         sent(wbuf.at[:, :, :, 0], s_send.at[3], mate)
         halo.wait_send()
 
@@ -511,7 +524,7 @@
 
 
 def reduce(dp, ext_t, full, g2, m01, m2, a0, a1, a2, r0, r1, r2, b0, b1, b2, q0, q1, q2, c0, c1, c2, p0, p1, p2,
-           e2, f2, s_send, s_mate, s_a, s_b, s_c, s_e, out_ref):
+           e2, s_send, s_mate, s_a, s_b, s_c, s_e, out_ref):
     x, y, z, k, chip = place()
     mate = device(x, y, z, 1 - k)
     holder = lax.rem(z, 2) == k
@@ -525,7 +538,7 @@
     def z_to(d):
         return device(x, y, lax.rem(z + d, NZ), k)
 
-    high, low = split(dp)
+    both = jnp.concatenate(split(dp), 1)
     low_half = iota((8, 128), 1) < 64
     block_rows = NY * NZ * 16
 
@@ -546,7 +559,8 @@
     for i in range(NX):
         xb = lax.rem(x + order[i], NX)
         rows = ext_t[pl.ds(pl.multiple_of(xb * block_rows, block_rows), block_rows), :]
-        part = dg(rows, high, 1, 0) + dg(rows, low, 1, 0)
+        part = dg(rows, both, 1, 0)
+        part = part[:, :WIDE] + part[:, WIDE:]
         full[0, xb] = part[:, 0:128].reshape(NY, NZ, 2, 8, 128)
         full[1, xb] = part[:, 128:256].reshape(NY, NZ, 2, 8, 128)
         steps = part[:, 256:384].reshape(NY, NZ // 2, 2, 2, 8, 128)
@@ -572,8 +586,8 @@
         remote(b0.at[lax.rem(y + d, NY)], q0.at[d - 1], s_send.at[8], s_b.at[0], y_to(d)).start()
     arrived(r1, s_a.at[1], mate)
     b1[...] = (a1[:, y] + r1[0]) + (r1[1] + r1[2])
-    for d in FAR8:
-        remote(b1.at[:, lax.rem(z + d, NZ)], q1.at[d - 1], s_send.at[9], s_b.at[1], z_to(d)).start()
+    for d in FAR4:
+        remote(b1.at[lax.rem(x + d, NX)], q1.at[d - 1], s_send.at[9], s_b.at[1], x_to(d)).start()
 
     @pl.when(holder)
     def _():
@@ -588,24 +602,22 @@
     for d in FAR8:
         remote(c0.at[lax.rem(z + d, NZ)], p0.at[d - 1], s_send.at[11], s_c.at[0], z_to(d)).start()
 
+    arrived(q1, s_b.at[1], mate)
+    c1[...] = (b1[x] + q1[0]) + (q1[1] + q1[2])
+    for d in FAR8:
+        remote(c1.at[lax.rem(z + d, NZ)], p1.at[d - 1], s_send.at[13], s_c.at[1], z_to(d)).start()
+    last = remote(c2.at[y], e2, s_send.at[14], s_e, mate)
+
     @pl.when(holder)
     def _():
         arrived(q2, s_b.at[2], mate)
         c2[...] = (b2[x] + q2[0]) + (q2[1] + q2[2])
         for d in FAR4:
-            remote(c2.at[lax.rem(y + d, NY)], p2.at[d - 1], s_send.at[12], s_c.at[2], y_to(d)).start()
-
-    arrived(q1, s_b.at[1], mate)
-    c1[...] = b1[:, z] + ((q1[0] + q1[1]) + (q1[2] + q1[3])) + ((q1[4] + q1[5]) + q1[6])
-    for d in FAR4:
-        remote(c1.at[lax.rem(x + d, NX)], p1.at[d - 1], s_send.at[13], s_c.at[1], x_to(d)).start()
-    last = remote(e2, f2, s_send.at[14], s_e, mate)
-
-    @pl.when(holder)
-    def _():
-        arrived(p2, s_c.at[2], mate)
-        e2[...] = (c2[y] + p2[0]) + (p2[1] + p2[2])
+            for core in range(2):
+                row = lax.rem(y + d, NY)
+                remote(c2.at[row], p2.at[d - 1], s_send.at[12], s_c.at[2], device(x, row, z, core)).start()
         last.start()
+        e2[...] = c2[y]
 
     sent(m01, s_send.at[0], mate)
     sent(m2, s_send.at[1], mate)
@@ -618,21 +630,22 @@
     arrived(p0, s_c.at[0], mate)
     out_ref[:, 0:128] = c0[z] + ((p0[0] + p0[1]) + (p0[2] + p0[3])) + ((p0[4] + p0[5]) + p0[6])
     arrived(p1, s_c.at[1], mate)
-    out_ref[:, 128:256] = (c1[x] + p1[0]) + (p1[1] + p1[2])
+    out_ref[:, 128:256] = c1[z] + ((p1[0] + p1[1]) + (p1[2] + p1[3])) + ((p1[4] + p1[5]) + p1[6])
+    arrived(p2, s_c.at[2], mate)
 
     @pl.when(jnp.logical_not(holder))
     def _():
-        last.wait_recv()
-        e2[...] = f2[...]
-
-    out_ref[:, 256:384] = jnp.where(k == 0, e2[...], roll64(e2[...]))
+        remote(c2.at[y], e2, s_send.at[14], s_e, mate).wait_recv()
+
+    steps = (e2[...] + p2[0]) + (p2[1] + p2[2])
+    out_ref[:, 256:384] = jnp.where(k == 0, steps, roll64(steps))
     sent(p0, s_send.at[11], mate)
     sent(p1, s_send.at[13], mate)
 
     @pl.when(holder)
     def _():
         sent(q2, s_send.at[10], mate)
-        sent(p2, s_send.at[12], mate)
+        sent(p1.at[pl.ds(0, 6)], s_send.at[12], mate)
         last.wait_send()
 
 
@@ -793,10 +806,10 @@
         + [vmem((NX, NY, NZ, 8, 128))] * 2 + [vmem((NX, NY, NZ // 2, 8, 128))]
         + [vmem((3, NY, NZ, 8, 128)), vmem((3, NX, NZ, 8, 128)), vmem((NZ, NX, NY, 8, 128))]
         + [vmem((NY, NZ, 8, 128)), vmem((NX, NZ, 8, 128)), vmem((NX, NY, 8, 128))]
-        + [vmem((3, NZ, 8, 128)), vmem((7, NX, 8, 128)), vmem((3, NY, 8, 128))]
-        + [vmem((NZ, 8, 128)), vmem((NX, 8, 128)), vmem((NY, 8, 128))]
-        + [vmem((7, 8, 128)), vmem((3, 8, 128)), vmem((3, 8, 128))]
-        + [vmem((8, 128)), vmem((8, 128))]
+        + [vmem((3, NZ, 8, 128)), vmem((3, NZ, 8, 128)), vmem((3, NY, 8, 128))]
+        + [vmem((NZ, 8, 128)), vmem((NZ, 8, 128)), vmem((NY, 8, 128))]
+        + [vmem((7, 8, 128)), vmem((7, 8, 128)), vmem((3, 8, 128))]
+        + [vmem((8, 128))]
     )
 
     def scan_scratch():

time: 81.2 us -> 80.5 us (level)
  no operation moved by 1% of the time
where the time goes in v8:
time: 80.5 us; the launch traced here: 80.3 us
  Pallas kernels  79.7 us (99%)
    pallas_call x1, Pallas kernels, body(): pl.pallas_call(functools.partial(everything, scale), out_shape=jax.ShapeD...  78.3 us

profile of v8, /device:TPU:1, one launch (start us, length us, event | category | flops | bytes accessed | tf_op | source)
XLA Modules:
  0.0 80.3 jit_solution(3355836027767407768)
XLA Ops:
  0.6 78.3 %shard_map.129.sums_ref = f32[8,384]{1,0:T(8,128)} custom-call(bf16[8,128]{1,0:T(8,128)(2,1)} %sw_hbm.1, bf16[8,128]{1,0:T(8,128)(2,1)} %sd_hbm.1, bf16[8,32]{1,0:T(8,128)(2,1)} %tw_hbm.1, bf16[8,32]{1,0:T(8,128)(2,1)} %td_hbm.1, bf16[128,2048]{1,0:T(8,128)(2,1)} %bitcast.5, bf16[128,1024]{1,0:T(8,128)(2,1)} %bitcast.6, bf16[128,1024]{1,0:T(8,128)(2,1)} %bitcast.7, ...), custom_call_target="tpu_custom_call" | custom-call | tf_op jit(solution)/shard_map/pallas_call | solution.py:837
  79.0 1.4 %shard_map.130 = (f32[8,128]{1,0:T(8,128)}, f32[8,32]{1,0:T(8,128)}, f32[8,128]{1,0:T(8,128)}, f32[8,32]{1,0:T(8,128)}) custom-call(f32[8,384]{1,0:T(8,128)} %shard_map.129.sums_ref), custom_call_target="tpu_custom_call" | custom-call | tf_op jit(solution)/shard_map/pallas_call | solution.py:847

commit v9 on v8

--- a/solution.py
+++ b/solution.py
@@ -524,7 +524,7 @@
 
 
 def reduce(dp, ext_t, full, g2, m01, m2, a0, a1, a2, r0, r1, r2, b0, b1, b2, q0, q1, q2, c0, c1, c2, p0, p1, p2,
-           e2, s_send, s_mate, s_a, s_b, s_c, s_e, out_ref):
+           e2, s_send, s_mate, s_a, s_b, s_c, s_e, out_sel, out_selh, out_step, out_steph):
     x, y, z, k, chip = place()
     mate = device(x, y, z, 1 - k)
     holder = lax.rem(z, 2) == k
@@ -569,8 +569,9 @@
         for tile in range(2):
             remote(full.at[tile, xb, :, :, 1 - k], m01.at[tile, xb], s_send.at[0], s_mate.at[i], mate).start()
         remote(g2.at[1 - k, xb], m2.at[xb], s_send.at[1], s_mate.at[NX + i], mate).start()
-        if i > 0:
-            settle(i - 1)
+        if i > 1:
+            settle(i - 2)
+    settle(NX - 2)
     settle(NX - 1)
 
     zsend = []
@@ -628,9 +629,9 @@
     sent(q0, s_send.at[8], mate)
     sent(q1, s_send.at[9], mate)
     arrived(p0, s_c.at[0], mate)
-    out_ref[:, 0:128] = c0[z] + ((p0[0] + p0[1]) + (p0[2] + p0[3])) + ((p0[4] + p0[5]) + p0[6])
+    out_sel[...] = c0[z] + ((p0[0] + p0[1]) + (p0[2] + p0[3])) + ((p0[4] + p0[5]) + p0[6])
     arrived(p1, s_c.at[1], mate)
-    out_ref[:, 128:256] = c1[z] + ((p1[0] + p1[1]) + (p1[2] + p1[3])) + ((p1[4] + p1[5]) + p1[6])
+    out_selh[...] = c1[z] + ((p1[0] + p1[1]) + (p1[2] + p1[3])) + ((p1[4] + p1[5]) + p1[6])
     arrived(p2, s_c.at[2], mate)
 
     @pl.when(jnp.logical_not(holder))
@@ -638,7 +639,9 @@
         remote(c2.at[y], e2, s_send.at[14], s_e, mate).wait_recv()
 
     steps = (e2[...] + p2[0]) + (p2[1] + p2[2])
-    out_ref[:, 256:384] = jnp.where(k == 0, steps, roll64(steps))
+    steps = jnp.where(k == 0, steps, roll64(steps))
+    out_step[...] = steps[:, 0:H]
+    out_steph[...] = steps[:, H : 2 * H]
     sent(p0, s_send.at[11], mate)
     sent(p1, s_send.at[13], mate)
 
@@ -650,7 +653,7 @@
 
 
 def everything(scale, sw_hbm, sd_hbm, tw_hbm, td_hbm, tok_ref, v_hbm, u_hbm, conv_hbm, bias_hbm, rate_hbm,
-               out_ref, v_ref, u_ref, sw_ref, sd_ref, tw_ref, td_ref, conv_ref, bias_ref, rate_ref, wbuf, ext, ext_t, proj,
+               out_sel, out_selh, out_step, out_steph, v_ref, u_ref, sw_ref, sd_ref, tw_ref, td_ref, conv_ref, bias_ref, rate_ref, wbuf, ext, ext_t, proj,
                forward_scratch, backward_scratch, rows_ref, row1_ref, row2_ref, colq_ref, colqd_ref, zp_ref, reduce_scratch,
                s_in, gather_sems, forward_sems, backward_sems, reduce_sems):
     entered = enter()
@@ -774,14 +777,16 @@
     drain_gather()
     fw.drain()
     bw.drain()
-    reduce(dp, ext_t, *reduce_scratch, *reduce_sems, out_ref)
-
-
-def split_outputs(sums_ref, o_sel, o_step, o_selh, o_steph):
-    o_sel[...] = sums_ref[:, 0:128]
-    o_selh[...] = sums_ref[:, 128:256]
-    o_step[...] = sums_ref[:, 256 : 256 + H]
-    o_steph[...] = sums_ref[:, 256 + H : 256 + 2 * H]
+    reduce(dp, ext_t, *reduce_scratch, *reduce_sems, out_sel, out_selh, out_step, out_steph)
+
+
+def hand_on(*refs):
+    sources, results, sem = refs[0:4], refs[4:8], refs[8]
+    copies = [pltpu.make_async_copy(src, dst, sem.at[i]) for i, (src, dst) in enumerate(zip(sources, results))]
+    for copy in copies:
+        copy.start()
+    for copy in copies:
+        copy.wait()
 
 
 def vmem(shape, dtype=F32):
@@ -834,25 +839,21 @@
         [dma(5), dma(2), dma(2), dma(2), dma(2)],
         [dma(15), dma(2 * NX), dma(3), dma(3), dma(3), dma()],
     ]
+    shapes = [jax.ShapeDtypeStruct((rows, columns), F32) for columns in (128, 128, H, H)]
     sums = pl.pallas_call(
         functools.partial(everything, scale),
-        out_shape=jax.ShapeDtypeStruct((rows, WIDE), F32),
+        out_shape=shapes,
         in_specs=[hbm] * 10,
-        out_specs=spec,
+        out_specs=[spec] * 4,
         scratch_shapes=scratch,
         compiler_params=pltpu.CompilerParams(
             vmem_limit_bytes=VMEM_LIMIT, collective_id=0, has_side_effects=True
         ),
     )(sel_weight, sel_dir, step_weight, step_dir, own_tokens, v, u, conv_weight, step_bias[None, :], decay_rate[None, :])
-    return pl.pallas_call(
-        split_outputs,
-        out_shape=[
-            jax.ShapeDtypeStruct((rows, 128), F32), jax.ShapeDtypeStruct((rows, H), F32),
-            jax.ShapeDtypeStruct((rows, 128), F32), jax.ShapeDtypeStruct((rows, H), F32),
-        ],
-        in_specs=[spec],
-        out_specs=[spec] * 4,
-    )(sums)
+    sel, selh, step, steph = pl.pallas_call(
+        hand_on, out_shape=shapes, in_specs=[hbm] * 4, out_specs=[hbm] * 4, scratch_shapes=[dma(4)],
+    )(*sums)
+    return sel, step, selh, steph
 
 
 def solution(mesh):

time: 80.5 us -> 81.2 us (level)
  no operation moved by 1% of the time
where the time goes in v9:
time: 81.2 us; the launch traced here: 81.1 us
  Pallas kernels  80.5 us (99%)
    pallas_call x1, Pallas kernels, body(): pl.pallas_call(functools.partial(everything, scale), out_shape=shapes, in...  78.8 us
    pallas_call x1, Pallas kernels, body(): pl.pallas_call(hand_on, out_shape=shapes, in_specs=[hbm] * 4, out_specs=[...  1.64 us

profile of v9, /device:TPU:1, one launch (start us, length us, event | category | flops | bytes accessed | tf_op | source)
XLA Modules:
  0.0 81.1 jit_solution(14353406893901852608)
XLA Ops:
  0.6 78.8 %shard_map.129 = (f32[8,128]{1,0:T(8,128)}, f32[8,128]{1,0:T(8,128)}, f32[8,32]{1,0:T(8,128)}, f32[8,32]{1,0:T(8,128)}) custom-call(bf16[8,128]{1,0:T(8,128)(2,1)} %sw_hbm.1, bf16[8,128]{1,0:T(8,128)(2,1)} %sd_hbm.1, bf16[8,32]{1,0:T(8,128)(2,1)} %tw_hbm.1, bf16[8,32]{1,0:T(8,128)(2,1)} %td_hbm.1, bf16[128,2048]{1,0:T(8,128)(2,1)} %bitcast.5, ...), custom_call_target="tpu_custom_call" | custom-call | tf_op jit(solution)/shard_map/pallas_call | solution.py:843
  79.5 1.6 %shard_map.130 = (f32[8,128]{1,0:T(8,128)}, f32[8,128]{1,0:T(8,128)}, f32[8,32]{1,0:T(8,128)}, f32[8,32]{1,0:T(8,128)}) custom-call(f32[8,128]{1,0:T(8,128)} %get-tuple-element.12.refs_0_, f32[8,128]{1,0:T(8,128)} %get-tuple-element.13.refs_1_, f32[8,32]{1,0:T(8,128)} %get-tuple-element.14.refs_2_, f32[8,32]{1,0:T(8,128)} %get-tuple-element.15.refs_3_), custom_call_target="tpu_custom_call" | custom-call | tf_op jit(solution)/shard_map/pallas_call | solution.py:853

commit v10 on v8

--- a/solution.py
+++ b/solution.py
@@ -247,9 +247,21 @@
     return head_sums(yy[:L] * v), head_sums(yy[L:] * v), dot_parts(w_split, x_split, 1, 1)
 
 
+def sel_terms(ft, dact, dactd, scale):
+    dz = scale * (ft["first"] * dact)
+    return dz, scale * (ft["second"] * ft["zd"] * dact + ft["first"] * dactd)
+
+
+def finish_c(ft, pairs, pc, scale):
+    m = low_lanes()
+    pair = pairs[0] + pc[:L] + jnp.where(m, 0.0, roll64(pairs[1] + pc[L:]))
+    dz, dzd = sel_terms(ft, roll64(pair), pair, scale)
+    return jnp.where(m, roll64(dz), dzd)
+
+
 def finish(ft, wts, pairs, row1, row2, colq, colqd, from_forward, from_backward, xf, xb, rate, scale):
     e, ed, f, fd, w, wd = wts
-    g, gdot, pc = from_forward
+    g, gdot, _ = from_forward
     kk, kdot, pb = from_backward
     kap = jnp.sum(xb[:64] * xf[:64], axis=0, keepdims=True)
     kapd = jnp.sum(xb[64:] * xf[:64] + xb[:64] * xf[64:], axis=0, keepdims=True)
@@ -257,13 +269,9 @@
     kap, kapd = both[0:1], both[8:9]
 
     m = low_lanes()
-    t1, t2, t3, t4 = pairs
-    pair_c = t1 + pc[:L] + jnp.where(m, 0.0, roll64(t2 + pc[L:]))
-    pair_b = t3 + pb[:L] + jnp.where(m, 0.0, roll64(t4 + pb[L:]))
-    dact = jnp.where(m, pair_b, roll64(pair_c))
-    dactd = jnp.where(m, roll64(pair_b), pair_c)
-    dz = scale * (ft["first"] * dact)
-    dzd = scale * (ft["second"] * ft["zd"] * dact + ft["first"] * dactd)
+    pair = pairs[2] + pb[:L] + jnp.where(m, 0.0, roll64(pairs[3] + pb[L:]))
+    dz, dzd = sel_terms(ft, pair, roll64(pair), scale)
+    tile_b = jnp.where(m, dz, roll64(dzd))
 
     delta, deltad, cum, cumd = ft["delta"], ft["deltad"], ft["cum"], ft["cumd"]
     colq, colqd = colq.T, colqd.T
@@ -282,7 +290,7 @@
     sq = ft["sq"]
     dq = scale * (sq * ddelta)
     dqd = scale * (sq * (1.0 - sq) * ft["qd"] * ddelta + sq * ddeltad)
-    return dz, dzd, dq, dqd
+    return tile_b, dq, dqd
 
 
 def place():
@@ -523,130 +531,182 @@
         self.back().wait_send()
 
 
-def reduce(dp, ext_t, full, g2, m01, m2, a0, a1, a2, r0, r1, r2, b0, b1, b2, q0, q1, q2, c0, c1, c2, p0, p1, p2,
-           e2, s_send, s_mate, s_a, s_b, s_c, s_e, out_ref):
-    x, y, z, k, chip = place()
-    mate = device(x, y, z, 1 - k)
-    holder = lax.rem(z, 2) == k
-
-    def x_to(d):
-        return device(lax.rem(x + d, NX), y, z, k)
-
-    def y_to(d):
-        return device(x, lax.rem(y + d, NY), z, k)
-
-    def z_to(d):
-        return device(x, y, lax.rem(z + d, NZ), k)
-
-    both = jnp.concatenate(split(dp), 1)
-    low_half = iota((8, 128), 1) < 64
-    block_rows = NY * NZ * 16
-
-    order = FAR4 + (0,)
-
-    def settle(i):
-        xb = lax.rem(x + order[i], NX)
-        arrived(m01.at[:, xb], s_mate.at[i], mate)
-        a0[xb] = full[0, xb, :, :, k] + m01[0, xb]
-        if i < NX - 1:
-            remote(a0.at[xb], r0.at[i], s_send.at[2], s_a.at[0], x_to(order[i])).start()
-        a1[xb] = full[1, xb, :, :, k] + m01[1, xb]
+class Sums:
+    def __init__(self, ext_t, scratch, sems):
+        self.ext_t, self.sc, self.sb, self.ss = ext_t, scratch[0], scratch[1], scratch[2]
+        self.s_send, self.s_mate, self.s_in = sems
+        self.x, self.y, self.z, self.k, self.chip = place()
+        self.mate = device(self.x, self.y, self.z, 1 - self.k)
+        self.holder = lax.rem(self.z, 2) == self.k
+        self.order = FAR4 + (0,)
+
+    def x_to(self, d):
+        return device(lax.rem(self.x + d, NX), self.y, self.z, self.k)
+
+    def y_to(self, d):
+        return device(self.x, lax.rem(self.y + d, NY), self.z, self.k)
+
+    def z_to(self, d):
+        return device(self.x, self.y, lax.rem(self.z + d, NZ), self.k)
+
+    def block(self, i):
+        xb = lax.rem(self.x + self.order[i], NX)
+        count = NY * NZ * 16
+        return xb, self.ext_t[pl.ds(pl.multiple_of(xb * count, count), count), :]
+
+    def product_c(self, dp):
+        full, m = self.sc[0], self.sc[1]
+        both = jnp.concatenate(split(dp), 1)
+        for i in range(NX):
+            xb, rows = self.block(i)
+            part = dg(rows, both, 1, 0)
+            full[xb] = (part[:, 0:128] + part[:, 128:256]).reshape(NY, NZ, 2, 8, 128)
+            remote(full.at[xb, :, :, 1 - self.k], m.at[xb], self.s_send.at[0], self.s_mate.at[i], self.mate).start()
+
+    def settle_c(self):
+        full, m, a, r = self.sc[0:4]
+        for i in range(NX):
+            xb = lax.rem(self.x + self.order[i], NX)
+            arrived(m.at[xb], self.s_mate.at[i], self.mate)
+            a[xb] = full[xb, :, :, self.k] + m[xb]
+            if i < NX - 1:
+                remote(a.at[xb], r.at[i], self.s_send.at[1], self.s_in.at[0], self.x_to(self.order[i])).start()
+
+    def second_c(self):
+        a, r, b, q = self.sc[2:6]
+        arrived(r, self.s_in.at[0], self.mate)
+        b[...] = (a[self.x] + r[0]) + (r[1] + r[2])
         for d in FAR4:
-            remote(a1.at[xb, lax.rem(y + d, NY)], r1.at[d - 1, xb], s_send.at[3], s_a.at[1], y_to(d)).start()
-        arrived(m2.at[xb], s_mate.at[NX + i], mate)
-        a2[xb] = g2[k, xb] + m2[xb]
-
-    for i in range(NX):
-        xb = lax.rem(x + order[i], NX)
-        rows = ext_t[pl.ds(pl.multiple_of(xb * block_rows, block_rows), block_rows), :]
-        part = dg(rows, both, 1, 0)
-        part = part[:, :WIDE] + part[:, WIDE:]
-        full[0, xb] = part[:, 0:128].reshape(NY, NZ, 2, 8, 128)
-        full[1, xb] = part[:, 128:256].reshape(NY, NZ, 2, 8, 128)
-        steps = part[:, 256:384].reshape(NY, NZ // 2, 2, 2, 8, 128)
-        for zp in range(2):
-            g2[zp, xb] = jnp.where(low_half, steps[:, :, zp, 0], steps[:, :, zp, 1])
-        for tile in range(2):
-            remote(full.at[tile, xb, :, :, 1 - k], m01.at[tile, xb], s_send.at[0], s_mate.at[i], mate).start()
-        remote(g2.at[1 - k, xb], m2.at[xb], s_send.at[1], s_mate.at[NX + i], mate).start()
-        if i > 0:
-            settle(i - 1)
-    settle(NX - 1)
-
-    zsend = []
-    for i in range(NZ // 2):
-        target = 2 * i + k
-        gap = lax.rem(z - target + NZ, NZ)
-        zsend.append((target != z, remote(a2.at[:, :, i], r2.at[gap], s_send.at[4 + i], s_a.at[2], device(x, y, target, k))))
-        pl.when(zsend[-1][0])(zsend[-1][1].start)
-
-    arrived(r0, s_a.at[0], mate)
-    b0[...] = (a0[x] + r0[0]) + (r0[1] + r0[2])
-    for d in FAR4:
-        remote(b0.at[lax.rem(y + d, NY)], q0.at[d - 1], s_send.at[8], s_b.at[0], y_to(d)).start()
-    arrived(r1, s_a.at[1], mate)
-    b1[...] = (a1[:, y] + r1[0]) + (r1[1] + r1[2])
-    for d in FAR4:
-        remote(b1.at[lax.rem(x + d, NX)], q1.at[d - 1], s_send.at[9], s_b.at[1], x_to(d)).start()
-
-    @pl.when(holder)
-    def _():
-        arrived(r2.at[pl.ds(1, NZ - 1)], s_a.at[2], mate)
-        total = a2[:, :, z // 2] + ((r2[1] + r2[2]) + (r2[3] + r2[4]))
-        b2[...] = total + ((r2[5] + r2[6]) + r2[7])
+            remote(b.at[lax.rem(self.y + d, NY)], q.at[d - 1], self.s_send.at[2], self.s_in.at[1], self.y_to(d)).start()
+
+    def third(self, c, p, send, land):
+        for d in FAR8:
+            remote(c.at[lax.rem(self.z + d, NZ)], p.at[d - 1], self.s_send.at[send], self.s_in.at[land], self.z_to(d)).start()
+
+    def third_c(self):
+        b, q, c, p = self.sc[4:8]
+        arrived(q, self.s_in.at[1], self.mate)
+        c[...] = (b[self.y] + q[0]) + (q[1] + q[2])
+        self.third(c, p, 3, 2)
+
+    def product(self, dpb, dps):
+        full, m, a, ry, rx, by, bx, qy, qx, c, p = self.sb
+        g2, m2, a2, r2, b2, q2, c2, p2, e2 = self.ss
+        x, y, z, k = self.x, self.y, self.z, self.k
+        both = jnp.concatenate(split(dpb) + split(dps), 1)
+        low_half = iota((8, 128), 1) < 64
+
+        def settle(i):
+            xb = lax.rem(x + self.order[i], NX)
+            arrived(m.at[xb], self.s_mate.at[NX + i], self.mate)
+            a[xb] = full[xb, :, :, k] + m[xb]
+            if i < NX - 1:
+                remote(
+                    a.at[xb, :, pl.ds(4, 4)], rx.at[i], self.s_send.at[6], self.s_in.at[4], self.x_to(self.order[i])
+                ).start()
+            for d in FAR4:
+                remote(
+                    a.at[xb, lax.rem(y + d, NY), pl.ds(0, 4)], ry.at[d - 1, xb],
+                    self.s_send.at[7], self.s_in.at[5], self.y_to(d),
+                ).start()
+            arrived(m2.at[xb], self.s_mate.at[2 * NX + i], self.mate)
+            a2[xb] = g2[k, xb] + m2[xb]
+
+        for i in range(NX):
+            xb, rows = self.block(i)
+            part = dg(rows, both, 1, 0)
+            full[xb] = (part[:, 0:128] + part[:, 128:256]).reshape(NY, NZ, 2, 8, 128)
+            remote(full.at[xb, :, :, 1 - k], m.at[xb], self.s_send.at[4], self.s_mate.at[NX + i], self.mate).start()
+            steps = (part[:, 256:384] + part[:, 384:512]).reshape(NY, NZ // 2, 2, 2, 8, 128)
+            for zp in range(2):
+                g2[zp, xb] = jnp.where(low_half, steps[:, :, zp, 0], steps[:, :, zp, 1])
+            remote(g2.at[1 - k, xb], m2.at[xb], self.s_send.at[5], self.s_mate.at[2 * NX + i], self.mate).start()
+            if i > 1:
+                settle(i - 2)
+        settle(NX - 2)
+        settle(NX - 1)
+
+    def rest(self, out_ref):
+        full, m, a, ry, rx, by, bx, qy, qx, c, p = self.sb
+        g2, m2, a2, r2, b2, q2, c2, p2, e2 = self.ss
+        x, y, z, k, mate, holder = self.x, self.y, self.z, self.k, self.mate, self.holder
+        s_send, s_in = self.s_send, self.s_in
+        zsend = []
+        for i in range(NZ // 2):
+            target = 2 * i + k
+            gap = lax.rem(z - target + NZ, NZ)
+            copy = remote(a2.at[:, :, i], r2.at[gap], s_send.at[8 + i], s_in.at[6], device(x, y, target, k))
+            zsend.append((target != z, copy))
+            pl.when(target != z)(copy.start)
+        self.third_c()
+
+        arrived(rx, s_in.at[4], mate)
+        bx[...] = (a[x, :, 4:8] + rx[0]) + (rx[1] + rx[2])
         for d in FAR4:
-            remote(b2.at[lax.rem(x + d, NX)], q2.at[d - 1], s_send.at[10], s_b.at[2], x_to(d)).start()
-
-    arrived(q0, s_b.at[0], mate)
-    c0[...] = (b0[y] + q0[0]) + (q0[1] + q0[2])
-    for d in FAR8:
-        remote(c0.at[lax.rem(z + d, NZ)], p0.at[d - 1], s_send.at[11], s_c.at[0], z_to(d)).start()
-
-    arrived(q1, s_b.at[1], mate)
-    c1[...] = (b1[x] + q1[0]) + (q1[1] + q1[2])
-    for d in FAR8:
-        remote(c1.at[lax.rem(z + d, NZ)], p1.at[d - 1], s_send.at[13], s_c.at[1], z_to(d)).start()
-    last = remote(c2.at[y], e2, s_send.at[14], s_e, mate)
-
-    @pl.when(holder)
-    def _():
-        arrived(q2, s_b.at[2], mate)
-        c2[...] = (b2[x] + q2[0]) + (q2[1] + q2[2])
+            remote(bx.at[lax.rem(y + d, NY)], qx.at[d - 1], s_send.at[12], s_in.at[7], self.y_to(d)).start()
+        arrived(ry, s_in.at[5], mate)
+        by[...] = (a[:, y, 0:4] + ry[0]) + (ry[1] + ry[2])
         for d in FAR4:
-            for core in range(2):
-                row = lax.rem(y + d, NY)
-                remote(c2.at[row], p2.at[d - 1], s_send.at[12], s_c.at[2], device(x, row, z, core)).start()
-        last.start()
-        e2[...] = c2[y]
-
-    sent(m01, s_send.at[0], mate)
-    sent(m2, s_send.at[1], mate)
-    sent(r0, s_send.at[2], mate)
-    sent(r1, s_send.at[3], mate)
-    for used, copy in zsend:
-        pl.when(used)(copy.wait_send)
-    sent(q0, s_send.at[8], mate)
-    sent(q1, s_send.at[9], mate)
-    arrived(p0, s_c.at[0], mate)
-    out_ref[:, 0:128] = c0[z] + ((p0[0] + p0[1]) + (p0[2] + p0[3])) + ((p0[4] + p0[5]) + p0[6])
-    arrived(p1, s_c.at[1], mate)
-    out_ref[:, 128:256] = c1[z] + ((p1[0] + p1[1]) + (p1[2] + p1[3])) + ((p1[4] + p1[5]) + p1[6])
-    arrived(p2, s_c.at[2], mate)
-
-    @pl.when(jnp.logical_not(holder))
-    def _():
-        remote(c2.at[y], e2, s_send.at[14], s_e, mate).wait_recv()
-
-    steps = (e2[...] + p2[0]) + (p2[1] + p2[2])
-    out_ref[:, 256:384] = jnp.where(k == 0, steps, roll64(steps))
-    sent(p0, s_send.at[11], mate)
-    sent(p1, s_send.at[13], mate)
-
-    @pl.when(holder)
-    def _():
-        sent(q2, s_send.at[10], mate)
-        sent(p1.at[pl.ds(0, 6)], s_send.at[12], mate)
-        last.wait_send()
+            remote(by.at[lax.rem(x + d, NX)], qy.at[d - 1], s_send.at[13], s_in.at[8], self.x_to(d)).start()
+
+        @pl.when(holder)
+        def _():
+            arrived(r2.at[pl.ds(1, NZ - 1)], s_in.at[6], mate)
+            total = a2[:, :, z // 2] + ((r2[1] + r2[2]) + (r2[3] + r2[4]))
+            b2[...] = total + ((r2[5] + r2[6]) + r2[7])
+            for d in FAR4:
+                remote(b2.at[lax.rem(x + d, NX)], q2.at[d - 1], s_send.at[14], s_in.at[9], self.x_to(d)).start()
+
+        arrived(qx, s_in.at[7], mate)
+        c[4:8] = (bx[y] + qx[0]) + (qx[1] + qx[2])
+        arrived(qy, s_in.at[8], mate)
+        c[0:4] = (by[x] + qy[0]) + (qy[1] + qy[2])
+        self.third(c, p, 15, 10)
+        last = remote(c2.at[y], e2, s_send.at[16], s_in.at[12], mate)
+
+        @pl.when(holder)
+        def _():
+            arrived(q2, s_in.at[9], mate)
+            c2[...] = (b2[x] + q2[0]) + (q2[1] + q2[2])
+            for d in FAR4:
+                for core in range(2):
+                    row = lax.rem(y + d, NY)
+                    remote(c2.at[row], p2.at[d - 1], s_send.at[17], s_in.at[11], device(x, row, z, core)).start()
+            last.start()
+            e2[...] = c2[y]
+
+        cm, cr, cq, cc, cp = self.sc[1], self.sc[3], self.sc[5], self.sc[6], self.sc[7]
+        for sem, ref in ((0, cm), (1, cr), (2, cq), (4, m), (5, m2), (6, rx), (7, ry), (12, qx), (13, qy)):
+            sent(ref, s_send.at[sem], mate)
+        for used, copy in zsend:
+            pl.when(used)(copy.wait_send)
+
+        def total(c, p):
+            return c[z] + ((p[0] + p[1]) + (p[2] + p[3])) + ((p[4] + p[5]) + p[6])
+
+        arrived(cp, s_in.at[2], mate)
+        tile_c = total(cc, cp)
+        arrived(p, s_in.at[10], mate)
+        tile_b = total(c, p)
+        m8 = iota((8, 128), 1) < 64
+        out_ref[:, 0:128] = jnp.where(m8, tile_b, roll64(tile_c))
+        out_ref[:, 128:256] = jnp.where(m8, roll64(tile_b), tile_c)
+        arrived(p2, s_in.at[11], mate)
+
+        @pl.when(jnp.logical_not(holder))
+        def _():
+            remote(c2.at[y], e2, s_send.at[16], s_in.at[12], mate).wait_recv()
+
+        steps = (e2[...] + p2[0]) + (p2[1] + p2[2])
+        out_ref[:, 256:384] = jnp.where(k == 0, steps, roll64(steps))
+        sent(cp, s_send.at[3], mate)
+        sent(p, s_send.at[15], mate)
+
+        @pl.when(holder)
+        def _():
+            sent(q2, s_send.at[14], mate)
+            sent(p.at[pl.ds(0, 6)], s_send.at[17], mate)
+            last.wait_send()
 
 
 def everything(scale, sw_hbm, sd_hbm, tw_hbm, td_hbm, tok_ref, v_hbm, u_hbm, conv_hbm, bias_hbm, rate_hbm,
@@ -742,39 +802,46 @@
     fw.back_in().wait_recv()
     xf = jnp.concatenate([fw.st[0], fw.st[1]], 1)
     from_forward = finish_forward(pp, e_split, u_ref[...], xf)
+
+    conv = conv_ref[...]
+    conv_roll = roll64(jnp.concatenate([conv, conv], 0))[0:KCONV]
+    low = iota((KCONV, 128), 1) < 64
+
+    def to_tokens(tile, taps, lanes):
+        zp_ref[0:HALO, lanes] = jnp.zeros((HALO, 128), F32)
+        zp_ref[HALO + L :, lanes] = jnp.zeros((zp_ref.shape[0] - HALO - L, 128), F32)
+        zp_ref[HALO : HALO + L, lanes] = tile
+
+        def spread(first_row, count):
+            total = taps[0:1, :] * zp_ref[first_row + 3 : first_row + 3 + count, lanes]
+            for tap in range(1, KCONV):
+                total = total + taps[tap : tap + 1, :] * zp_ref[first_row + 3 - tap : first_row + 3 - tap + count, lanes]
+            return total
+
+        return jnp.concatenate([spread(HALO, L), spread(0, HALO), jnp.zeros((128 - HALO, 128), F32)], 0)
+
+    sums = Sums(ext_t, reduce_scratch, reduce_sems)
+    tile_c = finish_c(ft, pairs, from_forward[2], scale)
+    sums.product_c(to_tokens(tile_c, jnp.where(low, conv_roll, conv), slice(0, 128)))
     bw.wait_two(0)
     bw.wait_two(1)
     bw.assemble(a1, ad1, bw.cores()[1], False)
+    sums.settle_c()
     bw.back_in().wait_recv()
     xb = jnp.concatenate([bw.st[0], bw.st[1]], 1)
     from_backward = finish_backward(pp, w_split, v_ref[...], xb)
-    dz, dzd, dq, dqd = finish(
+    tile_b, dq, dqd = finish(
         ft, wts, pairs, row1_ref[...], row2_ref[...], colq_ref[...], colqd_ref[...],
         from_forward, from_backward, xf, xb, rate, scale,
     )
-    zp_ref[...] = jnp.zeros(zp_ref.shape, F32)
-    zp_ref[HALO : HALO + L, 0:128] = dz
-    zp_ref[HALO : HALO + L, 128:256] = dzd
-    conv = conv_ref[...]
-
-    def spread(first_row, count, lanes):
-        total = conv[0:1, :] * zp_ref[first_row + 3 : first_row + 3 + count, lanes]
-        for tap in range(1, KCONV):
-            total = total + conv[tap : tap + 1, :] * zp_ref[first_row + 3 - tap : first_row + 3 - tap + count, lanes]
-        return total
-
-    pad = jnp.zeros((128 - HALO, 128), F32)
-    columns = []
-    for half in range(2):
-        lanes = slice(128 * half, 128 * half + 128)
-        columns.append(jnp.concatenate([spread(HALO, L, lanes), spread(0, HALO, lanes), pad], 0))
-    both = jnp.concatenate([dq, dqd, dq, dqd], 1)
-    columns.append(jnp.concatenate([both, jnp.zeros((128, 128), F32)], 0))
-    dp = jnp.concatenate(columns, 1)
+    dpb = to_tokens(tile_b, jnp.where(low, conv, conv_roll), slice(128, 256))
+    dps = jnp.concatenate([jnp.concatenate([dq, dqd, dq, dqd], 1), jnp.zeros((128, 128), F32)], 0)
+    sums.second_c()
+    sums.product(dpb, dps)
+    sums.rest(out_ref)
     drain_gather()
     fw.drain()
     bw.drain()
-    reduce(dp, ext_t, *reduce_scratch, *reduce_sems, out_ref)
 
 
 def split_outputs(sums_ref, o_sel, o_step, o_selh, o_steph):
@@ -799,18 +866,19 @@
     scale = 1.0 / math.sqrt(NX * CHIPS * 2 * L)
     spec = pl.BlockSpec(memory_space=pltpu.VMEM)
     hbm = pl.BlockSpec(memory_space=pl.ANY)
-    tiles = NX * NY * NZ
-    reduce_scratch = (
-        [vmem((2, NX, NY, NZ, 2, 8, 128)), vmem((2, NX, NY, NZ // 2, 8, 128)),
-         vmem((2, NX, NY, NZ, 8, 128)), vmem((NX, NY, NZ // 2, 8, 128))]
-        + [vmem((NX, NY, NZ, 8, 128))] * 2 + [vmem((NX, NY, NZ // 2, 8, 128))]
-        + [vmem((3, NY, NZ, 8, 128)), vmem((3, NX, NZ, 8, 128)), vmem((NZ, NX, NY, 8, 128))]
-        + [vmem((NY, NZ, 8, 128)), vmem((NX, NZ, 8, 128)), vmem((NX, NY, 8, 128))]
-        + [vmem((3, NZ, 8, 128)), vmem((3, NZ, 8, 128)), vmem((3, NY, 8, 128))]
-        + [vmem((NZ, 8, 128)), vmem((NZ, 8, 128)), vmem((NY, 8, 128))]
-        + [vmem((7, 8, 128)), vmem((7, 8, 128)), vmem((3, 8, 128))]
-        + [vmem((8, 128))]
-    )
+    tile = (8, 128)
+    grid = (NX, NY, NZ)
+    reduce_scratch = [
+        [vmem(shape + tile) for shape in (
+            grid + (2,), grid, grid, (3, NY, NZ), (NY, NZ), (3, NZ), (NZ,), (7,),
+        )],
+        [vmem(shape + tile) for shape in (
+            grid + (2,), grid, grid, (3, NX, 4), (3, NY, 4), (NX, 4), (NY, 4), (3, 4), (3, 4), (NZ,), (7,),
+        )],
+        [vmem(shape + tile) for shape in (
+            (2, NX, NY, NZ // 2), (NX, NY, NZ // 2), (NX, NY, NZ // 2), (NZ, NX, NY), (NX, NY), (3, NY), (NY,), (3,), (),
+        )],
+    ]
 
     def scan_scratch():
         return (
@@ -832,7 +900,7 @@
         [dma(5), dma(), dma(), dma(NX * NY), dma(NX * NY)],
         [dma(5), dma(2), dma(2), dma(2), dma(2)],
         [dma(5), dma(2), dma(2), dma(2), dma(2)],
-        [dma(15), dma(2 * NX), dma(3), dma(3), dma(3), dma()],
+        [dma(18), dma(3 * NX), dma(13)],
     ]
     sums = pl.pallas_call(
         functools.partial(everything, scale),

time: 80.5 us -> 85.7 us (1.065)
  Pallas kernels: 79.7 us -> 84.9 us
    pallas_call x1, Pallas kernels: 78.3 us -> 83.5 us  [body(): pl.pallas_call(functools.partial(everything, scale), out_shape=jax.ShapeD...]
where the time goes in v10:
time: 85.7 us; the launch traced here: 85.5 us
  Pallas kernels  84.9 us (99%)
    pallas_call x1, Pallas kernels, body(): pl.pallas_call(functools.partial(everything, scale), out_shape=jax.ShapeD...  83.5 us

profile of v10, /device:TPU:1, one launch (start us, length us, event | category | flops | bytes accessed | tf_op | source)
XLA Modules:
  0.0 85.5 jit_solution(1453500886613181000)
XLA Ops:
  0.6 83.5 %shard_map.129.sums_ref = f32[8,384]{1,0:T(8,128)} custom-call(bf16[8,128]{1,0:T(8,128)(2,1)} %sw_hbm.1, bf16[8,128]{1,0:T(8,128)(2,1)} %sd_hbm.1, bf16[8,32]{1,0:T(8,128)(2,1)} %tw_hbm.1, bf16[8,32]{1,0:T(8,128)(2,1)} %td_hbm.1, bf16[128,2048]{1,0:T(8,128)(2,1)} %bitcast.5, bf16[128,1024]{1,0:T(8,128)(2,1)} %bitcast.6, bf16[128,1024]{1,0:T(8,128)(2,1)} %bitcast.7, ...), custom_call_target="tpu_custom_call" | custom-call | tf_op jit(solution)/shard_map/pallas_call | solution.py:905
  84.2 1.4 %shard_map.130 = (f32[8,128]{1,0:T(8,128)}, f32[8,32]{1,0:T(8,128)}, f32[8,128]{1,0:T(8,128)}, f32[8,32]{1,0:T(8,128)}) custom-call(f32[8,384]{1,0:T(8,128)} %shard_map.129.sums_ref), custom_call_target="tpu_custom_call" | custom-call | tf_op jit(solution)/shard_map/pallas_call | solution.py:915

commit v11 on v8

--- a/solution.py
+++ b/solution.py
@@ -569,8 +569,9 @@
         for tile in range(2):
             remote(full.at[tile, xb, :, :, 1 - k], m01.at[tile, xb], s_send.at[0], s_mate.at[i], mate).start()
         remote(g2.at[1 - k, xb], m2.at[xb], s_send.at[1], s_mate.at[NX + i], mate).start()
-        if i > 0:
-            settle(i - 1)
+        if i > 1:
+            settle(i - 2)
+    settle(NX - 2)
     settle(NX - 1)
 
     zsend = []
@@ -723,13 +724,15 @@
             ft, g, gd, tile(v_ref), tile(u_ref), rows_ref, row1_ref, row2_ref, colq_ref, colqd_ref, first, last, carry
         )
 
-    carry = block_terms(0, 7, (zero, zero))
+    carry = block_terms(0, 4, (zero, zero))
     fw.row_total(0)
-    carry = block_terms(7, 8, carry)
+    carry = block_terms(4, 6, carry)
     fw.row_total(1)
+    carry = block_terms(6, 7, carry)
     fw.start_two(0)
     bw.row_total(0)
     fw.start_two(1)
+    carry = block_terms(7, 8, carry)
     bw.row_total(1)
     bw.start_two(0)
     pairs = intra_pairs(pp, *carry)

time: 80.5 us -> 80.9 us (level)
  no operation moved by 1% of the time
where the time goes in v11:
time: 80.9 us; the launch traced here: 80.8 us
  Pallas kernels  80.1 us (99%)
    pallas_call x1, Pallas kernels, body(): pl.pallas_call(functools.partial(everything, scale), out_shape=jax.ShapeD...  78.7 us

profile of v11, /device:TPU:1, one launch (start us, length us, event | category | flops | bytes accessed | tf_op | source)
XLA Modules:
  0.0 80.8 jit_solution(1670920810369118979)
XLA Ops:
  0.6 78.7 %shard_map.129.sums_ref = f32[8,384]{1,0:T(8,128)} custom-call(bf16[8,128]{1,0:T(8,128)(2,1)} %sw_hbm.1, bf16[8,128]{1,0:T(8,128)(2,1)} %sd_hbm.1, bf16[8,32]{1,0:T(8,128)(2,1)} %tw_hbm.1, bf16[8,32]{1,0:T(8,128)(2,1)} %td_hbm.1, bf16[128,2048]{1,0:T(8,128)(2,1)} %bitcast.5, bf16[128,1024]{1,0:T(8,128)(2,1)} %bitcast.6, bf16[128,1024]{1,0:T(8,128)(2,1)} %bitcast.7, ...), custom_call_target="tpu_custom_call" | custom-call | tf_op jit(solution)/shard_map/pallas_call | solution.py:840
  79.4 1.4 %shard_map.130 = (f32[8,128]{1,0:T(8,128)}, f32[8,32]{1,0:T(8,128)}, f32[8,128]{1,0:T(8,128)}, f32[8,32]{1,0:T(8,128)}) custom-call(f32[8,384]{1,0:T(8,128)} %shard_map.129.sums_ref), custom_call_target="tpu_custom_call" | custom-call | tf_op jit(solution)/shard_map/pallas_call | solution.py:850

commit v12 on v11

--- a/solution.py
+++ b/solution.py
@@ -145,15 +145,17 @@
     return dot_left(rows, head_spread(), 1, 0)
 
 
-def streams(wts, values, cotangent):
+def forward_streams(wts, values):
     e, ed, _, _, w, wd = wts
     v = values.astype(F32)
+    last = jnp.concatenate([jnp.broadcast_to(row[L - 1 :, :], (8, H)) for row in (e, ed)], 0)
+    last = spread_rows(last)
+    return spread_rows(w) * v, spread_rows(wd) * v, last[0:8], last[8:16]
+
+
+def backward_streams(wts, cotangent):
     u = cotangent.astype(F32)
-    we = spread_rows(w) * v
-    wde = spread_rows(wd) * v
-    es = spread_rows(e)
-    eds = spread_rows(ed)
-    return we, wde, es, eds, es * u, eds * u
+    return spread_rows(wts[0]) * u, spread_rows(wts[1]) * u
 
 
 def forward_states(pp, we, wde):
@@ -266,7 +268,6 @@
     dzd = scale * (ft["second"] * ft["zd"] * dact + ft["first"] * dactd)
 
     delta, deltad, cum, cumd = ft["delta"], ft["deltad"], ft["cum"], ft["cumd"]
-    colq, colqd = colq.T, colqd.T
     colqd = colqd - cumd * colq
     row1, row2 = row1[:, :H], row2[:, :H]
     row2 = row2 + cumd * row1
@@ -375,7 +376,7 @@
     def _():
         ext[L : L + HALO, :] = jnp.zeros((HALO, ext.shape[1]), BF16)
 
-    ext_t[:, L:] = ext[L:, :].T
+    ext_t[:, L : L + HALO] = ext[L:, :].T
     for e in (0, 1, 3, 2):
         for d in (1, 3, 2):
             fx, fy = far(d)
@@ -663,7 +664,7 @@
     for c in local:
         c.start()
     x, y, z, k, _ = place()
-    ext[L + HALO :, :] = jnp.zeros((ext.shape[0] - L - HALO, ext.shape[1]), BF16)
+    ext_t[:, L + HALO :] = jnp.zeros((ext_t.shape[0], L - HALO), BF16)
     for c in local[0:4]:
         c.wait()
     wbuf[x, y, z, k, :, 0:128] = sw_ref[...]
@@ -683,17 +684,18 @@
     ft = features(lambda row, lane, lanes: proj[row : row + L, lane : lane + lanes], conv_ref[...], bias_ref[...], rate)
     wts = weights_of(ft)
     pp = pair_parts(ft)
-    we, wde, es, eds, eu, edu = streams(wts, v_ref[...], u_ref[...])
+    we, wde, decay, decayd = forward_streams(wts, v_ref[...])
     fw = Half(*forward_scratch, None, *forward_sems)
     bw = Half(*backward_scratch, fw, *backward_sems)
     row = iota((8, HP), 0)
-    dec = jnp.where(row == 0, es[L - 1 :, :], jnp.where(row == 1, eds[L - 1 :, :], 0.0))
+    dec = jnp.where(row == 0, decay, jnp.where(row == 1, decayd, 0.0))
     states = forward_states(pp, we, wde)
     for half in range(2):
         lanes = slice(HALF * half, HALF * half + HALF)
         fw.loc[half, 0:128, :] = states[:, lanes]
         fw.loc[half, 128:136, :] = dec[:, lanes]
     fw.to_mate().start()
+    eu, edu = backward_streams(wts, u_ref[...])
     states = backward_states(pp, eu, edu)
     for half in range(2):
         bw.loc[half] = states[:, HALF * half : HALF * half + HALF]
@@ -745,6 +747,7 @@
     fw.back_in().wait_recv()
     xf = jnp.concatenate([fw.st[0], fw.st[1]], 1)
     from_forward = finish_forward(pp, e_split, u_ref[...], xf)
+    colq, colqd = colq_ref[...].T, colqd_ref[...].T
     bw.wait_two(0)
     bw.wait_two(1)
     bw.assemble(a1, ad1, bw.cores()[1], False)
@@ -752,7 +755,7 @@
     xb = jnp.concatenate([bw.st[0], bw.st[1]], 1)
     from_backward = finish_backward(pp, w_split, v_ref[...], xb)
     dz, dzd, dq, dqd = finish(
-        ft, wts, pairs, row1_ref[...], row2_ref[...], colq_ref[...], colqd_ref[...],
+        ft, wts, pairs, row1_ref[...], row2_ref[...], colq, colqd,
         from_forward, from_backward, xf, xb, rate, scale,
     )
     zp_ref[...] = jnp.zeros(zp_ref.shape, F32)
@@ -826,7 +829,7 @@
         vmem((rows, 128), BF16), vmem((rows, 128), BF16), vmem((rows, H), BF16), vmem((rows, H), BF16),
         vmem((KCONV, 128)), vmem((1, H)), vmem((1, H)),
         vmem((NX, NY, NZ, 2, rows, WIDE), BF16),
-        vmem((2 * L, depth), BF16), vmem((depth, 2 * L), BF16), vmem((HALO + L, WIDE)),
+        vmem((L + HALO, depth), BF16), vmem((depth, 2 * L), BF16), vmem((HALO + L, WIDE)),
         [vmem((2, 136, HALF)), vmem((136, HALF))] + scan_scratch(),
         [vmem((2, 128, HALF)), vmem((128, HALF))] + scan_scratch(),
         vmem((3 * H, L)), vmem((L, L)), vmem((L, L)), vmem((H, L)), vmem((H, L)), vmem((HALO + L + 8, 256)),

time: 80.9 us -> 81 us (level)
  no operation moved by 1% of the time
where the time goes in v12:
time: 81 us; the launch traced here: 80.8 us
  Pallas kernels  80.2 us (99%)
    pallas_call x1, Pallas kernels, body(): pl.pallas_call(functools.partial(everything, scale), out_shape=jax.ShapeD...  78.8 us

profile of v12, /device:TPU:1, one launch (start us, length us, event | category | flops | bytes accessed | tf_op | source)
XLA Modules:
  0.0 80.8 jit_solution(12682355690967271636)
XLA Ops:
  0.6 78.8 %shard_map.129.sums_ref = f32[8,384]{1,0:T(8,128)} custom-call(bf16[8,128]{1,0:T(8,128)(2,1)} %sw_hbm.1, bf16[8,128]{1,0:T(8,128)(2,1)} %sd_hbm.1, bf16[8,32]{1,0:T(8,128)(2,1)} %tw_hbm.1, bf16[8,32]{1,0:T(8,128)(2,1)} %td_hbm.1, bf16[128,2048]{1,0:T(8,128)(2,1)} %bitcast.5, bf16[128,1024]{1,0:T(8,128)(2,1)} %bitcast.6, bf16[128,1024]{1,0:T(8,128)(2,1)} %bitcast.7, ...), custom_call_target="tpu_custom_call" | custom-call | tf_op jit(solution)/shard_map/pallas_call | solution.py:843
  79.5 1.4 %shard_map.130 = (f32[8,128]{1,0:T(8,128)}, f32[8,32]{1,0:T(8,128)}, f32[8,128]{1,0:T(8,128)}, f32[8,32]{1,0:T(8,128)}) custom-call(f32[8,384]{1,0:T(8,128)} %shard_map.129.sums_ref), custom_call_target="tpu_custom_call" | custom-call | tf_op jit(solution)/shard_map/pallas_call | solution.py:853

commit v13 on v12

--- a/solution.py
+++ b/solution.py
@@ -570,10 +570,8 @@
         for tile in range(2):
             remote(full.at[tile, xb, :, :, 1 - k], m01.at[tile, xb], s_send.at[0], s_mate.at[i], mate).start()
         remote(g2.at[1 - k, xb], m2.at[xb], s_send.at[1], s_mate.at[NX + i], mate).start()
-        if i > 1:
-            settle(i - 2)
-    settle(NX - 2)
-    settle(NX - 1)
+    for i in range(NX):
+        settle(i)
 
     zsend = []
     for i in range(NZ // 2):

time: 81 us -> 81.1 us (level)
  no operation moved by 1% of the time
where the time goes in v13:
time: 81.1 us; the launch traced here: 80.9 us
  Pallas kernels  80.2 us (99%)
    pallas_call x1, Pallas kernels, body(): pl.pallas_call(functools.partial(everything, scale), out_shape=jax.ShapeD...  78.9 us

profile of v13, /device:TPU:1, one launch (start us, length us, event | category | flops | bytes accessed | tf_op | source)
XLA Modules:
  0.0 80.9 jit_solution(15814720420565852064)
XLA Ops:
  0.6 78.9 %shard_map.129.sums_ref = f32[8,384]{1,0:T(8,128)} custom-call(bf16[8,128]{1,0:T(8,128)(2,1)} %sw_hbm.1, bf16[8,128]{1,0:T(8,128)(2,1)} %sd_hbm.1, bf16[8,32]{1,0:T(8,128)(2,1)} %tw_hbm.1, bf16[8,32]{1,0:T(8,128)(2,1)} %td_hbm.1, bf16[128,2048]{1,0:T(8,128)(2,1)} %bitcast.5, bf16[128,1024]{1,0:T(8,128)(2,1)} %bitcast.6, bf16[128,1024]{1,0:T(8,128)(2,1)} %bitcast.7, ...), custom_call_target="tpu_custom_call" | custom-call | tf_op jit(solution)/shard_map/pallas_call | solution.py:841
  79.5 1.4 %shard_map.130 = (f32[8,128]{1,0:T(8,128)}, f32[8,32]{1,0:T(8,128)}, f32[8,128]{1,0:T(8,128)}, f32[8,32]{1,0:T(8,128)}) custom-call(f32[8,384]{1,0:T(8,128)} %shard_map.129.sums_ref), custom_call_target="tpu_custom_call" | custom-call | tf_op jit(solution)/shard_map/pallas_call | solution.py:851

commit v14 on v12

--- a/solution.py
+++ b/solution.py
@@ -525,7 +525,7 @@
 
 
 def reduce(dp, ext_t, full, g2, m01, m2, a0, a1, a2, r0, r1, r2, b0, b1, b2, q0, q1, q2, c0, c1, c2, p0, p1, p2,
-           e2, s_send, s_mate, s_a, s_b, s_c, s_e, out_ref):
+           e2, s_send, s_mate, s_a, s_b, s_c, s_e, out_ref, drains):
     x, y, z, k, chip = place()
     mate = device(x, y, z, 1 - k)
     holder = lax.rem(z, 2) == k
@@ -621,6 +621,8 @@
         last.start()
         e2[...] = c2[y]
 
+    for drain in drains:
+        drain()
     sent(m01, s_send.at[0], mate)
     sent(m2, s_send.at[1], mate)
     sent(r0, s_send.at[2], mate)
@@ -777,10 +779,7 @@
     both = jnp.concatenate([dq, dqd, dq, dqd], 1)
     columns.append(jnp.concatenate([both, jnp.zeros((128, 128), F32)], 0))
     dp = jnp.concatenate(columns, 1)
-    drain_gather()
-    fw.drain()
-    bw.drain()
-    reduce(dp, ext_t, *reduce_scratch, *reduce_sems, out_ref)
+    reduce(dp, ext_t, *reduce_scratch, *reduce_sems, out_ref, (drain_gather, fw.drain, bw.drain))
 
 
 def split_outputs(sums_ref, o_sel, o_step, o_selh, o_steph):

time: 81 us -> 81 us (level)
  no operation moved by 1% of the time
where the time goes in v14:
time: 81 us; the launch traced here: 80.8 us
  Pallas kernels  80.2 us (99%)
    pallas_call x1, Pallas kernels, body(): pl.pallas_call(functools.partial(everything, scale), out_shape=jax.ShapeD...  78.8 us

profile of v14, /device:TPU:1, one launch (start us, length us, event | category | flops | bytes accessed | tf_op | source)
XLA Modules:
  0.0 80.8 jit_solution(8638565983225681443)
XLA Ops:
  0.6 78.8 %shard_map.129.sums_ref = f32[8,384]{1,0:T(8,128)} custom-call(bf16[8,128]{1,0:T(8,128)(2,1)} %sw_hbm.1, bf16[8,128]{1,0:T(8,128)(2,1)} %sd_hbm.1, bf16[8,32]{1,0:T(8,128)(2,1)} %tw_hbm.1, bf16[8,32]{1,0:T(8,128)(2,1)} %td_hbm.1, bf16[128,2048]{1,0:T(8,128)(2,1)} %bitcast.5, bf16[128,1024]{1,0:T(8,128)(2,1)} %bitcast.6, bf16[128,1024]{1,0:T(8,128)(2,1)} %bitcast.7, ...), custom_call_target="tpu_custom_call" | custom-call | tf_op jit(solution)/shard_map/pallas_call | solution.py:842
  79.5 1.4 %shard_map.130 = (f32[8,128]{1,0:T(8,128)}, f32[8,32]{1,0:T(8,128)}, f32[8,128]{1,0:T(8,128)}, f32[8,32]{1,0:T(8,128)}) custom-call(f32[8,384]{1,0:T(8,128)} %shard_map.129.sums_ref), custom_call_target="tpu_custom_call" | custom-call | tf_op jit(solution)/shard_map/pallas_call | solution.py:852
